TPU v7x, 32 devices: a whole 2x2x4 slice. The times are simulated.
32 devices in a mesh: group: 4 (over y, x), rank: 8 (over z, core).
Axes of the slice: x: 2, y: 2, z: 4, core: 2. Of those that a mesh axis runs over, the one named last changes fastest.
Arguments:
- a_blocks: bfloat16 [256, 22, 128, 128], P(('group', 'rank')), may hold values from -0.5 to 0.5
- a_cols: int32 [256, 22], P(('group', 'rank')), may hold values from 0 to 71, as said below
- p_rows: bfloat16 [256, 128, 128], P(('group', 'rank')), may hold values from -1.1953125 to 1.1953125
- p_cols: int32 [256, 4], P(('group', 'rank')), may hold values from 0 to 127, as said below
- send_rows: int32 [32, 32, 2], P(('group', 'rank')), may hold values from -1 to 7, as said below
- c_cols: int32 [128, 27], P('group'), may hold values from 0 to 127, as said below
Outputs:
- coarse: float32 [128, 32, 864], P(('group', 'rank'))
Inputs may be any that keep to these rules, and one draw needn't show every extreme that they name: `a_cols`: an entry t of 8 or more names slot t - 8 of what the row's device receives, ordered by sending device then slot; every slot whose send_rows entry is not -1 is named by exactly one entry of the receiving device, and no entry names a slot whose entry is -1. `send_rows`: -1 marks an empty slot; a device sends nothing to itself. `p_cols`: the coarse block columns of fine block rows on group g lie in g * 32 to g * 32 + 31. `c_cols`: the 27 block columns of a coarse block row are distinct.
All inputs are finite; a program needn't handle non-finite values.
Results may differ from a plain program's by a relative error of at most 0.0029.
Values may be sent and summed in bfloat16 or wider, within the bound.
No kernel may reach another device: no remote copies, remote signals or barrier semaphores. Data moves between devices by JAX's collectives and lax.ppermute only.
A program may use at most 128 MiB of HBM per device.

v0:
```python
import math

import jax
import jax.numpy as jnp
from jax import lax
from jax.sharding import PartitionSpec as P


def local(a_blocks, a_cols, p_rows, p_cols, send_rows, c_cols):
    fine_rows = a_blocks.shape[0]
    block_cols = a_blocks.shape[1]
    block_span = p_rows.shape[1]
    row_width = p_rows.shape[2]
    part_count = p_cols.shape[1]
    coarse_span = row_width // part_count
    group_rows = c_cols.shape[0]
    pattern = c_cols.shape[1]
    peer_count = send_rows.shape[1]
    slot_count = send_rows.shape[2]
    wanted = send_rows[0]
    is_live = wanted >= 0
    picked = jnp.maximum(wanted, 0)
    outgoing = jnp.where(is_live[:, :, None, None], p_rows[picked], jnp.zeros((), p_rows.dtype))
    out_cols = jnp.where(is_live[:, :, None], p_cols[picked], -1)
    arrived, arrived_cols = (
        lax.all_to_all(outgoing, ("group", "rank"), split_axis=0, concat_axis=0, tiled=True),
        lax.all_to_all(out_cols, ("group", "rank"), split_axis=0, concat_axis=0, tiled=True),
    )
    row_table = jnp.concatenate(
        [p_rows, arrived.reshape(peer_count * slot_count, block_span, row_width)], 0
    )
    col_table = jnp.concatenate(
        [p_cols, arrived_cols.reshape(peer_count * slot_count, part_count)], 0
    )
    group_base = lax.axis_index("group") * group_rows
    step_rows = math.gcd(fine_rows, 4)
    step_count = fine_rows // step_rows

    def one_step(pieces):
        block_a, cols_here, prow_here, pcol_here = pieces
        weighted = jnp.einsum(
            "ixr,ikxy->ikry", prow_here, block_a, preferred_element_type=jnp.float32
        ).astype(jnp.bfloat16)
        fetched = row_table[cols_here]
        product = jnp.einsum(
            "ikry,ikyc->ikrc", weighted, fetched, preferred_element_type=jnp.float32
        )
        product = product.reshape(
            step_rows, block_cols, part_count, coarse_span, part_count, coarse_span
        )
        far_cols = col_table[cols_here]
        targets = c_cols[pcol_here - group_base]
        select = (targets[:, :, :, None, None] == far_cols[:, None, None, :, :]).astype(jnp.float32)
        merged = jnp.einsum("imskn,ikmanb->imasb", select, product, precision=lax.Precision.HIGHEST)
        return merged.reshape(step_rows * part_count, coarse_span * pattern * coarse_span)

    pieces = (
        a_blocks.reshape(step_count, step_rows, block_cols, block_span, block_span),
        a_cols.reshape(step_count, step_rows, block_cols),
        p_rows.reshape(step_count, step_rows, block_span, row_width),
        p_cols.reshape(step_count, step_rows, part_count),
    )
    merged_all = lax.map(one_step, pieces).reshape(
        fine_rows * part_count, coarse_span * pattern * coarse_span
    )
    targets_flat = (p_cols - group_base).reshape(-1)
    onehot = (jnp.arange(group_rows, dtype=jnp.int32)[:, None] == targets_flat[None, :]).astype(
        jnp.float32
    )
    partial_value = jnp.dot(
        onehot, merged_all, precision=lax.Precision.HIGHEST, preferred_element_type=jnp.float32
    )
    partial_value = partial_value.reshape(group_rows, coarse_span, pattern * coarse_span)
    return lax.psum_scatter(partial_value, "rank", scatter_dimension=0, tiled=True)


def solution(mesh):
    in_specs = (
        P(("group", "rank"), None, None, None),
        P(("group", "rank"), None),
        P(("group", "rank"), None, None),
        P(("group", "rank"), None),
        P(("group", "rank"), None, None),
        P("group", None),
    )
    out_specs = P(("group", "rank"), None, None)
    return jax.shard_map(local, mesh=mesh, in_specs=in_specs, out_specs=out_specs, check_vma=False)
```

profile of v0, /device:TPU:0, one launch (start us, length us, event | category | flops | bytes accessed | tf_op | source)
XLA Modules:
  0.0 314.9 jit_solution(336092096920806551)
XLA Ops:
  6.5 0.7 broadcast_maximum_fusion
  7.2 0.7 compare_bitcast_fusion
  7.9 0.1 copy.54
  8.0 0.1 reshape.137
  8.1 0.8 copy.66
  8.9 0.1 copy.53
  9.0 0.6 gather_fusion.4
  9.6 0.7 broadcast_select_fusion.1
  10.3 7.3 %all-to-all-start.1 = ((s32[32,2,4]{2,1,0:T(2,128)}), s32[32,2,4]{2,1,0:T(2,128)S(1)}, u32[]{:S(2)}, u32[]{:S(2)}) async-start(s32[32,2,4]{2,1,0:T(2,128)} %broadcast_select_fusion.1), calls=%async_computation.1 | async-start | bytes 65536 | tf_op jit(solution)/shard_map/all_to_all | solution.py:27
  17.6 1.9 gather_fusion.3
  19.5 1.5 broadcast_select_fusion
  21.0 3.8 %all-to-all-done.1 = s32[32,2,4]{2,1,0:T(2,128)S(1)} async-done(((s32[32,2,4]{2,1,0:T(2,128)}), s32[32,2,4]{2,1,0:T(2,128)S(1)}, u32[]{:S(2)}, u32[]{:S(2)}) %all-to-all-start.1) | async-done | bytes 1056 | tf_op jit(solution)/shard_map/all_to_all | solution.py:27
  24.8 2.7 all-to-all-start
  27.7 8.3 %copy.52 = bf16[8,22,128,128]{2,3,1,0:T(8,128)(2,1)} copy(bf16[8,22,128,128]{3,2,1,0:T(8,128)(2,1)} %param.8) | data formatting | bytes 11534336 | tf_op args[0]
  36.0 0.1 copy.51
  36.1 0.7 eq.29
  36.9 0.1 copy.59
  37.0 40.7 %all-to-all-done = bf16[32,2,128,128]{3,2,1,0:T(8,128)(2,1)S(1)} async-done(((bf16[32,2,128,128]{3,2,1,0:T(8,128)(2,1)}), bf16[32,2,128,128]{3,2,1,0:T(8,128)(2,1)S(1)}, u32[]{:S(2)}, u32[]{:S(2)}) %all-to-all-start) | async-done | bytes 2097184 | tf_op jit(solution)/shard_map/all_to_all | solution.py:26
  77.7 1.6 pad_maximum_fusion
  79.3 170.6 %while.10 = (s32[]{:T(128)}, f32[2,16,27648]{2,1,0:T(8,128)}, bf16[2,4,22,128,128]{3,4,2,1,0:T(8,128)(2,1)}, bf16[2,4,128,128]{3,2,1,0:T(8,128)(2,1)S(1)}, s32[2...) while((s32[]{:T(128)}, f32[2,16,27648]{2,1,0:T(8,128)}, ...), condition=%wide.region_1.2_spmd, body=%wide.region_0.1_spmd.sunk | while | flops 1206820352 | bytes 47150936 | solution.py:63
  79.3 0.1 reshape.178
  79.4 2.8 gather_fusion
  82.2 6.0 %fusion.44 = f32[4,22,128,128]{3,2,1,0:T(8,128)} fusion(bf16[4,22,128,128]{3,2,1,0:T(8,128)(2,1)S(1)} %bitcast.75, bf16[2,4,22,128,128]{3,4,2,1,0:T(8,128)(2,1)} %get-tuple-element.203, s32[]{:T(128)} %get-tuple-element.190, bf16[2,4,128,128]{3,2,1,0:T(8,128)(2,1)S(1)} %get-tuple-element.204), kind=kOutput, calls=%fused_computation.10.clone.1 | convolution fusion | flops 739639296 | bytes 11666432 | tf_op jit(solution)/shard_map/while/body/eval_jaxpr/ikry,ikyc->ikrc/dot_general | solution.py:45
  88.2 16.8 %reshape.179 = f32[4,22,4,32,4,32]{5,4,3,2,1,0:T(4,128)} reshape(f32[4,22,128,128]{3,2,1,0:T(8,128)} %fusion.44) | data formatting | bytes 11534336 | tf_op jit(solution)/shard_map/while/body/eval_jaxpr/reshape | solution.py:48
  105.0 0.6 gather_fusion.1
  105.7 0.1 reshape.180
  105.8 0.1 reshape.181
  105.9 0.6 gather_fusion.2
  106.5 42.4 %fusion.45 = f32[4,4,32,27,32]{3,4,2,1,0:T(8,128)} fusion(f32[4,22,4,32,4,32]{5,4,3,2,1,0:T(4,128)} %reshape.179, s32[4,22,4]{1,2,0:T(4,128)S(1)} %copy.79, s32[4,4,27]{2,1,0:T(4,128)S(1)} %bitcast.82), kind=kOutput, calls=%fused_computation.7.clone.1 | convolution fusion | flops 467178624 | bytes 7539776 | tf_op jit(solution)/shard_map/while/body/eval_jaxpr/imskn,ikmanb->imasb/dot_general | solution.py:54
  148.8 9.6 %copy.80 = f32[4,4,32,27,32]{4,3,2,1,0:T(8,128)} copy(f32[4,4,32,27,32]{3,4,2,1,0:T(8,128)} %fusion.45) | data formatting | bytes 3538944 | tf_op jit(solution)/shard_map/while/body/eval_jaxpr/imskn,ikmanb->imasb/transpose | solution.py:54
  158.4 4.8 %broadcast_in_dim.51 = f32[1,16,27648]{2,1,0:T(8,128)S(1)} reshape(f32[4,4,32,27,32]{4,3,2,1,0:T(8,128)} %copy.80) | data formatting | bytes 3538944 | tf_op jit(solution)/shard_map/while/body/jit(dynamic_update_index_in_dim)/broadcast_in_dim | solution.py:63
  163.3 1.3 constant_dynamic-update-slice_fusion.2
  164.6 0.1 reshape.178
  164.7 2.8 gather_fusion
  167.5 6.0 %fusion.44 = f32[4,22,128,128]{3,2,1,0:T(8,128)} fusion(bf16[4,22,128,128]{3,2,1,0:T(8,128)(2,1)S(1)} %bitcast.75, bf16[2,4,22,128,128]{3,4,2,1,0:T(8,128)(2,1)} %get-tuple-element.203, s32[]{:T(128)} %get-tuple-element.190, bf16[2,4,128,128]{3,2,1,0:T(8,128)(2,1)S(1)} %get-tuple-element.204), kind=kOutput, calls=%fused_computation.10.clone.1 | convolution fusion | flops 739639296 | bytes 11666432 | tf_op jit(solution)/shard_map/while/body/eval_jaxpr/ikry,ikyc->ikrc/dot_general | solution.py:45
  173.5 16.8 %reshape.179 = f32[4,22,4,32,4,32]{5,4,3,2,1,0:T(4,128)} reshape(f32[4,22,128,128]{3,2,1,0:T(8,128)} %fusion.44) | data formatting | bytes 11534336 | tf_op jit(solution)/shard_map/while/body/eval_jaxpr/reshape | solution.py:48
  190.3 0.6 gather_fusion.1
  191.0 0.1 reshape.180
  191.1 0.1 reshape.181
  191.2 0.6 gather_fusion.2
  191.8 42.4 %fusion.45 = f32[4,4,32,27,32]{3,4,2,1,0:T(8,128)} fusion(f32[4,22,4,32,4,32]{5,4,3,2,1,0:T(4,128)} %reshape.179, s32[4,22,4]{1,2,0:T(4,128)S(1)} %copy.79, s32[4,4,27]{2,1,0:T(4,128)S(1)} %bitcast.82), kind=kOutput, calls=%fused_computation.7.clone.1 | convolution fusion | flops 467178624 | bytes 7539776 | tf_op jit(solution)/shard_map/while/body/eval_jaxpr/imskn,ikmanb->imasb/dot_general | solution.py:54
  234.1 9.6 %copy.80 = f32[4,4,32,27,32]{4,3,2,1,0:T(8,128)} copy(f32[4,4,32,27,32]{3,4,2,1,0:T(8,128)} %fusion.45) | data formatting | bytes 3538944 | tf_op jit(solution)/shard_map/while/body/eval_jaxpr/imskn,ikmanb->imasb/transpose | solution.py:54
  243.7 4.8 %broadcast_in_dim.51 = f32[1,16,27648]{2,1,0:T(8,128)S(1)} reshape(f32[4,4,32,27,32]{4,3,2,1,0:T(8,128)} %copy.80) | data formatting | bytes 3538944 | tf_op jit(solution)/shard_map/while/body/jit(dynamic_update_index_in_dim)/broadcast_in_dim | solution.py:63
  248.5 1.3 constant_dynamic-update-slice_fusion.2
  249.9 5.3 %dot_general.17 = f32[32,864,32]{1,0,2:T(8,128)} reshape(f32[27648,32]{0,1:T(8,128)} %bitcast.81) | data formatting | bytes 7077888 | tf_op jit(solution)/shard_map/dot_general | solution.py:70
  255.2 6.1 %fusion.24 = f32[32,32,864]{2,0,1:T(8,128)S(1)} fusion(f32[32,864,32]{1,0,2:T(8,128)} %dot_general.17, s32[32]{0:T(128)S(1)} %copy-done.4), kind=kOutput, calls=%fused_computation.25 | convolution fusion | flops 339739648 | bytes 7078016 | tf_op jit(solution)/shard_map/dot_general | solution.py:70
  261.3 3.9 %copy.61 = f32[32,32,864]{2,1,0:T(8,128)} copy(f32[32,32,864]{2,0,1:T(8,128)S(1)} %fusion.24) | data formatting | bytes 7077888 | tf_op jit(solution)/shard_map/dot_general | solution.py:70
  265.3 42.8 %reduce-scatter.2.cloned.1.call-done = f32[4,32,864]{2,1,0:T(8,128)} async-done(((f32[32,32,864]{2,1,0:T(8,128)}), f32[4,32,864]{2,1,0:T(8,128)}) %reduce-scatter.2.cloned.1.call-update) | async-done | bytes 442384 | tf_op jit(solution)/shard_map/reduce_scatter | solution.py:74
  (29 shorter events, 0.4 us)
Async XLA Ops:
  10.3 14.5 %all-to-all-start.1 = ((s32[32,2,4]{2,1,0:T(2,128)}), s32[32,2,4]{2,1,0:T(2,128)S(1)}, u32[]{:S(2)}, u32[]{:S(2)}) async-start(s32[32,2,4]{2,1,0:T(2,128)} %broadcast_select_fusion.1), calls=%async_computation.1 | async-start | bytes 65536 | tf_op jit(solution)/shard_map/all_to_all | solution.py:27
  24.8 52.8 %all-to-all-start = ((bf16[32,2,128,128]{3,2,1,0:T(8,128)(2,1)}), bf16[32,2,128,128]{3,2,1,0:T(8,128)(2,1)S(1)}, u32[]{:S(2)}, u32[]{:S(2)}) async-start(bf16[32,2,128,128]{3,2,1,0:T(8,128)(2,1)} %broadcast_select_fusion), calls=%async_computation | async-start | bytes 4194304 | tf_op jit(solution)/shard_map/all_to_all | solution.py:26
  27.6 280.5 %reduce-scatter.2.cloned.1.call-start = ((), (), s32[]{:S(2)}) async-start(), calls=%async_computation.3 | async-start | bytes 4128768 | tf_op jit(solution)/shard_map/reduce_scatter | solution.py:74
  27.6 8.3 %copy-start.3 = (s32[8,4]{0,1:T(4,128)S(1)}, s32[8,4]{0,1:T(4,128)}, u32[]{:S(2)}) copy-start(s32[8,4]{0,1:T(4,128)} %param.11) | copy-start | bytes 388
  27.6 50.0 %copy-start = (bf16[8,128,128]{2,1,0:T(8,128)(2,1)S(1)}, bf16[8,128,128]{2,1,0:T(8,128)(2,1)}, u32[]{:S(2)}) copy-start(bf16[8,128,128]{2,1,0:T(8,128)(2,1)} %param.10) | copy-start | bytes 786436
  36.0 43.4 %copy-start.1 = (s32[32,27]{1,0:T(8,128)S(1)}, s32[32,27]{1,0:T(8,128)}, u32[]{:S(2)}) copy-start(s32[32,27]{1,0:T(8,128)} %param.13) | copy-start | bytes 10372
  36.0 43.4 %copy-start.2 = (s32[8,22]{1,0:T(8,128)S(1)}, s32[8,22]{1,0:T(8,128)}, u32[]{:S(2)}) copy-start(s32[8,22]{1,0:T(8,128)} %param.9) | copy-start | bytes 2116
  249.9 5.3 %copy-start.4 = (s32[32]{0:T(128)S(1)}, s32[32]{0:T(128)}, u32[]{:S(2)}) copy-start(s32[32]{0:T(128)} %eq.29) | copy-start | bytes 388
Sparse Core Ops, SparseCore 0:
  265.4 42.5 reduce-scatter.1
where the time goes:
time: 317 us; the launch traced here: 315 us
  matrix products  103 us (32%)
  local copies, waits for them, and re-layouts  95.7 us (30%)
  waiting for transfers between devices  87.3 us (28%)
  between operations  13.5 us (4%)
  starting transfers between devices  10.1 us (3%)
  other arithmetic  5.41 us (2%)
    dot_general x2, matrix products, one_step(): jnp.einsum('imskn,ikmanb->imasb', select, product, precision=lax.Precisio...  84.7 us
    reduce_scatter x1, waiting for transfers between devices, local(): lax.psum_scatter(partial_value, 'rank', scatter_dimension=0, tiled=True)  42.8 us
    all_to_all x1, waiting for transfers between devices, local(): lax.all_to_all(outgoing, ('group', 'rank'), split_axis=0, concat_axis=0,...  40.7 us
    reshape x2, local copies, waits for them, and re-layouts, one_step(): product.reshape(step_rows, block_cols, part_count, coarse_span, part_coun...  33.6 us
    transpose x2, local copies, waits for them, and re-layouts, one_step(): jnp.einsum('imskn,ikmanb->imasb', select, product, precision=lax.Precisio...  19.2 us
    dot_general x2, matrix products, one_step(): jnp.einsum('ikry,ikyc->ikrc', weighted, fetched, preferred_element_type=j...  12.1 us
    broadcast_in_dim x2, local copies, waits for them, and re-layouts, local(): lax.map(one_step, pieces)  9.64 us
    dot_general x2, local copies, waits for them, and re-layouts, local(): jnp.dot(onehot, merged_all, precision=lax.Precision.HIGHEST, preferred_el...  9.25 us
  transfers between devices with their start and end apart: 3, of which 3 were waited for; matrix products, arithmetic and copies ran while one was open for 4% of the time, Pallas kernels for 0%

commit v1 on v0

v1 whole, which is shorter than its diff:
```python
import functools

import jax
import jax.numpy as jnp
from jax import lax
from jax.experimental import pallas as pl
from jax.experimental.pallas import tpu as pltpu
from jax.sharding import Mesh, PartitionSpec as P

NT = (((1,), (1,)), ((), ()))
NN = (((1,), (0,)), ((), ()))


def prep_kernel(wanted_ref, pcols_ref, p_ref, pt_ref, out_ref, cols_ref):
    rows, span, width = p_ref.shape
    slots, parts = wanted_ref.shape[0], pcols_ref.shape[1]
    row_id = lax.broadcasted_iota(jnp.int32, (width, width), 0)
    col_id = lax.broadcasted_iota(jnp.int32, (width, width), 1)
    unit = jnp.where(row_id == col_id, 1.0, 0.0).astype(p_ref.dtype)
    for row in range(rows):
        flipped = lax.dot_general(unit, p_ref[row], NT, preferred_element_type=jnp.float32)
        pt_ref[row] = flipped.astype(pt_ref.dtype)

    def fill(slot, carry):
        row = jnp.maximum(wanted_ref[slot], 0)
        out_ref[slot] = pt_ref[row]
        for part in range(parts):
            cols_ref[slot * parts + part] = pcols_ref[row, part]
        return carry

    lax.fori_loop(0, slots, fill, 0)


def prepare(p_rows, p_cols, wanted):
    rows, span, width = p_rows.shape
    slots, parts = wanted.shape[0], p_cols.shape[1]
    vmem, smem = pl.BlockSpec(memory_space=pltpu.VMEM), pl.BlockSpec(memory_space=pltpu.SMEM)
    return pl.pallas_call(
        prep_kernel,
        out_shape=(
            jax.ShapeDtypeStruct((rows, width, span), p_rows.dtype),
            jax.ShapeDtypeStruct((slots, width, span), p_rows.dtype),
            jax.ShapeDtypeStruct((slots * parts,), jnp.int32),
        ),
        in_specs=[smem, smem, vmem],
        out_specs=(vmem, vmem, smem),
        compiler_params=pltpu.CompilerParams(vmem_limit_bytes=48 << 20),
        name="prep",
    )(wanted, p_cols, p_rows)


def weigh_kernel(pt_ref, a_ref, w_ref):
    left = pt_ref[0]
    for k in range(a_ref.shape[1]):
        w_ref[0, k] = lax.dot_general(
            left, a_ref[0, k], NN, preferred_element_type=jnp.float32
        ).astype(w_ref.dtype)


def weigh(pt, a_blocks):
    rows, cols, span, _ = a_blocks.shape
    width = pt.shape[1]
    return pl.pallas_call(
        weigh_kernel,
        grid=(rows,),
        out_shape=jax.ShapeDtypeStruct((rows, cols, width, span), jnp.bfloat16),
        in_specs=[
            pl.BlockSpec((1, width, span), lambda i: (i, 0, 0)),
            pl.BlockSpec((1, cols, span, span), lambda i: (i, 0, 0, 0)),
        ],
        out_specs=pl.BlockSpec((1, cols, width, span), lambda i: (i, 0, 0, 0)),
        cost_estimate=pl.CostEstimate(
            flops=2 * rows * cols * span * span * width,
            bytes_accessed=2 * a_blocks.size * 2,
            transcendentals=0,
        ),
        name="weigh",
    )(pt, a_blocks)


def merge_kernel(
    place_ref, acols_ref, pcols_ref, far_ref, ccols_ref, w_ref, local_ref, arrived_ref,
    keep_ref, send_ref, table, dense, panel, rounded, sems,
):
    step, steps = pl.program_id(0), pl.num_programs(0)
    fine_rows, part_count = pcols_ref.shape
    block_cols, width = w_ref.shape[1], w_ref.shape[2]
    span = width // part_count
    pattern = ccols_ref.shape[1]
    chips = keep_ref.shape[0]
    own_rows = width // span
    core, base = place_ref[0], place_ref[1]

    @pl.when(step == 0)
    def _():
        near = pltpu.make_async_copy(local_ref, table.at[pl.ds(0, fine_rows)], sems.at[0])
        far = pltpu.make_async_copy(
            arrived_ref, table.at[pl.ds(fine_rows, arrived_ref.shape[0])], sems.at[1]
        )
        near.start()
        far.start()
        panel[...] = jnp.zeros_like(panel)
        near.wait()
        far.wait()

    dense[...] = jnp.zeros_like(dense)
    for k in range(block_cols):
        source = acols_ref[step, k]
        product = lax.dot_general(
            table[source], w_ref[0, k], NT, preferred_element_type=jnp.float32
        )
        for n in range(part_count):
            at = pl.ds(pl.multiple_of(far_ref[source * part_count + n] * span, span), span)
            dense[at, :] += product[n * span : (n + 1) * span, :]

    lane_group = lax.broadcasted_iota(jnp.int32, (span, width), 1) // span
    for m in range(part_count):
        row = pcols_ref[step, m] - base
        owner, within = row // own_rows, lax.rem(row, own_rows)
        shift = lax.rem(within + part_count - m, part_count) * span
        here = lane_group == within
        for s in range(pattern):
            at = pl.ds(pl.multiple_of(ccols_ref[row, s] * span, span), span)
            moved = pltpu.roll(dense[at, :], shift, 1)
            panel[owner, s * span : (s + 1) * span, :] += jnp.where(here, moved, 0.0)

    @pl.when(step == steps - 1)
    def _():
        copies = []
        for chip in range(chips):
            copies.append(
                pltpu.make_async_copy(
                    panel.at[2 * chip + core], keep_ref.at[chip], sems.at[2 + chip]
                )
            )
            copies[-1].start()
        for chip in range(chips):
            rounded[chip] = panel[2 * chip + 1 - core].astype(rounded.dtype)
        out = pltpu.make_async_copy(rounded, send_ref, sems.at[0])
        out.start()
        for copy in copies:
            copy.wait()
        out.wait()


def merge(place, a_cols, p_cols, far_cols, c_cols, weighted, local, arrived, chips, all_cols):
    rows, cols, width, span = weighted.shape
    parts = p_cols.shape[1]
    small = width // parts
    pattern = c_cols.shape[1]
    slots = arrived.shape[0]
    hbm = pl.BlockSpec(memory_space=pl.ANY)
    return pl.pallas_call(
        merge_kernel,
        out_shape=(
            jax.ShapeDtypeStruct((chips, pattern * small, width), jnp.float32),
            jax.ShapeDtypeStruct((chips, pattern * small, width), jnp.bfloat16),
        ),
        grid_spec=pltpu.PrefetchScalarGridSpec(
            num_scalar_prefetch=5,
            grid=(rows,),
            in_specs=[
                pl.BlockSpec((1, cols, width, span), lambda i, *_: (i, 0, 0, 0)),
                hbm,
                hbm,
            ],
            out_specs=(hbm, hbm),
            scratch_shapes=[
                pltpu.VMEM((rows + slots, width, span), local.dtype),
                pltpu.VMEM((all_cols * small, width), jnp.float32),
                pltpu.VMEM((2 * chips, pattern * small, width), jnp.float32),
                pltpu.VMEM((chips, pattern * small, width), jnp.bfloat16),
                pltpu.SemaphoreType.DMA((2 + chips,)),
            ],
        ),
        compiler_params=pltpu.CompilerParams(vmem_limit_bytes=56 << 20),
        name="merge",
    )(place, a_cols, p_cols, far_cols, c_cols, weighted, local, arrived)


def pair_kernel(place_ref, keep_ref, got_ref, mine_ref, *out_refs):
    chips = keep_ref.shape[0]
    chip = place_ref[2]
    mine_ref[...] = keep_ref[chip] + got_ref[chip].astype(jnp.float32)
    for off, out_ref in enumerate(out_refs):
        at = jnp.bitwise_xor(chip, off + 1)
        out_ref[...] = (keep_ref[at] + got_ref[at].astype(jnp.float32)).astype(out_ref.dtype)


def pair(place, keep, got):
    chips, tall, width = keep.shape
    vmem, smem = pl.BlockSpec(memory_space=pltpu.VMEM), pl.BlockSpec(memory_space=pltpu.SMEM)
    return pl.pallas_call(
        pair_kernel,
        out_shape=(jax.ShapeDtypeStruct((tall, width), jnp.float32),)
        + (jax.ShapeDtypeStruct((tall, width), jnp.bfloat16),) * (chips - 1),
        in_specs=[smem, vmem, vmem],
        out_specs=(vmem,) * chips,
        compiler_params=pltpu.CompilerParams(vmem_limit_bytes=56 << 20),
        name="pair",
    )(place, keep, got)


def last_kernel(mine_ref, *refs):
    terms, out_ref = refs[:-1], refs[-1]
    total = mine_ref[...]
    for term in terms:
        total = total + term[...].astype(jnp.float32)
    out_ref[...] = total.T.reshape(out_ref.shape)


def last(mine, terms, own_rows):
    tall, width = mine.shape
    vmem = pl.BlockSpec(memory_space=pltpu.VMEM)
    return pl.pallas_call(
        last_kernel,
        out_shape=jax.ShapeDtypeStruct((own_rows, width // own_rows, tall), jnp.float32),
        in_specs=[vmem] * (1 + len(terms)),
        out_specs=vmem,
        compiler_params=pltpu.CompilerParams(vmem_limit_bytes=56 << 20),
        name="last",
    )(mine, *terms)


def local(chips, groups, a_blocks, a_cols, p_rows, p_cols, send_rows, c_cols):
    parts, width = p_cols.shape[1], p_rows.shape[2]
    group_rows = c_cols.shape[0]
    everyone = ("group", "chip", "core")
    chip = lax.axis_index("chip")
    place = jnp.stack(
        [lax.axis_index("core"), lax.axis_index("group") * group_rows, chip]
    ).astype(jnp.int32)
    pt, outgoing, out_cols = prepare(p_rows, p_cols, send_rows.reshape(-1))
    arrived = lax.all_to_all(outgoing, everyone, split_axis=0, concat_axis=0, tiled=True)
    arrived_cols = lax.all_to_all(out_cols.reshape(-1, 2 * parts), everyone, split_axis=0, concat_axis=0, tiled=True)
    far_cols = jnp.concatenate([p_cols.reshape(-1), arrived_cols.reshape(-1)])
    weighted = weigh(pt, a_blocks)
    keep, give = merge(
        place, a_cols, p_cols, far_cols, c_cols, weighted, pt, arrived, chips, group_rows * groups
    )
    got = lax.ppermute(give, "core", [(0, 1), (1, 0)])
    own_rows = group_rows // (2 * chips)
    if chips == 4:
        mine, *out = pair(place, keep, got)
        terms = [
            lax.ppermute(piece, "chip", [(q, q ^ (off + 1)) for q in range(chips)])
            for off, piece in enumerate(out)
        ]
        return last(mine, terms, own_rows)
    both = keep + got.astype(jnp.float32)
    mine = lax.dynamic_index_in_dim(both, chip, 0, keepdims=False)
    came = lax.all_to_all(
        both.astype(jnp.bfloat16), "chip", split_axis=0, concat_axis=0, tiled=True
    ).astype(jnp.float32)
    other = jnp.arange(chips)[:, None, None] != chip
    return last(mine + jnp.sum(jnp.where(other, came, 0.0), 0), [], own_rows)


def solution(mesh):
    groups, ranks = mesh.shape["group"], mesh.shape["rank"]
    chips = ranks // 2
    fine = Mesh(mesh.devices.reshape(groups, chips, 2), ("group", "chip", "core"))
    every = ("group", "chip", "core")
    in_specs = (P(every), P(every), P(every), P(every), P(every), P("group"))
    return jax.shard_map(
        functools.partial(local, chips, groups),
        mesh=fine,
        in_specs=in_specs,
        out_specs=P(every),
        check_vma=False,
    )
```

time: 317 us -> 120 us (0.38)
  matrix products: 103 us -> 0 us
  local copies, waits for them, and re-layouts: 95.7 us -> 7.06 us
  Pallas kernels: 0 us -> 32 us
  waiting for transfers between devices: 87.3 us -> 55.8 us
  blocking collectives: 0 us -> 14.2 us
  between operations: 13.5 us -> 0.09 us
  other arithmetic: 5.41 us -> 1.93 us
    dot_general x5 -> x0, matrix products: 103 us -> none  [the longest x2 84.7 us: one_step(): jnp.einsum('imskn,ikmanb->imasb', select, product, precision=lax.Precisio...]
    reduce_scatter x1 -> x0, waiting for transfers between devices: 42.8 us -> none  [local(): lax.psum_scatter(partial_value, 'rank', scatter_dimension=0, tiled=True)]
    reshape x3, local copies, waits for them, and re-layouts: 33.7 us -> 0.27 us  [the longest x2 0.17 us: local(): far_cols = jnp.concatenate([p_cols.reshape(-1), arrived_cols.reshape(-1)])]
    pallas_call x0 -> x5, Pallas kernels: none -> 32 us  [the longest x1 15.2 us: merge(): pl.pallas_call(merge_kernel, out_shape=(jax.ShapeDtypeStruct((chips, patt...]
    transpose x2 -> x0, local copies, waits for them, and re-layouts: 19.2 us -> none  [one_step(): jnp.einsum('imskn,ikmanb->imasb', select, product, precision=lax.Precisio...]
    ppermute x0 -> x4, waiting for transfers between devices: none -> 17.1 us  [the longest x3 14.5 us: local(): lax.ppermute(piece, 'chip', [(q, q ^ off + 1) for q in range(chips)])]
    all_to_all x0 -> x1, blocking collectives: none -> 14.2 us  [local(): lax.all_to_all(out_cols.reshape(-1, 2 * parts), everyone, split_axis=0, c...]
    gather x14 -> x0, local copies, waits for them, and re-layouts: 10.7 us -> none  [the longest x2 5.53 us: one_step(): fetched = row_table[cols_here]]
  transfers between devices with their start and end apart: 3 -> 5, of which waited for: 3 -> 4; matrix products, arithmetic and copies ran while one was open for 4% -> 2% of each run, Pallas kernels for 0% -> 7%
where the time goes in v1:
time: 120 us; the launch traced here: 118 us
  waiting for transfers between devices  55.8 us (46%)
  Pallas kernels  32 us (27%)
  blocking collectives  14.2 us (12%)
  starting transfers between devices  7.18 us (6%)
  local copies, waits for them, and re-layouts  7.06 us (6%)
  other arithmetic  1.93 us (2%)
    all_to_all x1, waiting for transfers between devices, local(): lax.all_to_all(outgoing, everyone, split_axis=0, concat_axis=0, tiled=True)  38.7 us
    pallas_call x1, Pallas kernels, merge(): pl.pallas_call(merge_kernel, out_shape=(jax.ShapeDtypeStruct((chips, patt...  15.2 us
    ppermute x3, waiting for transfers between devices, local(): lax.ppermute(piece, 'chip', [(q, q ^ off + 1) for q in range(chips)])  14.5 us
    all_to_all x1, blocking collectives, local(): lax.all_to_all(out_cols.reshape(-1, 2 * parts), everyone, split_axis=0, c...  14.2 us
    pallas_call x1, Pallas kernels, weigh(): pl.pallas_call(weigh_kernel, grid=(rows,), out_shape=jax.ShapeDtypeStruct...  8.77 us
    unnamed x18, local copies, waits for them, and re-layouts  6.18 us
    ppermute x3, starting transfers between devices, local(): lax.ppermute(piece, 'chip', [(q, q ^ off + 1) for q in range(chips)])  4.39 us
    pallas_call x1, Pallas kernels, prepare(): pl.pallas_call(prep_kernel, out_shape=(jax.ShapeDtypeStruct((rows, width,...  2.96 us
  transfers between devices with their start and end apart: 5, of which 4 were waited for; matrix products, arithmetic and copies ran while one was open for 2% of the time, Pallas kernels for 7%

profile of v1, /device:TPU:0, one launch (start us, length us, event | category | flops | bytes accessed | tf_op | source)
XLA Modules:
  0.0 118.3 jit_solution(15851113684693424543)
XLA Ops:
  0.0 0.8 copy.19.pcols_ref
  0.8 0.0 copy-start.2
  0.8 0.8 copy.16
  1.5 0.1 reshape.15.wanted_ref
  1.6 0.0 copy-start.1
  1.6 0.9 copy-done.1
  2.6 3.0 %prep.1 = (bf16[8,128,128]{2,1,0:T(8,128)(2,1)S(1)}, bf16[64,128,128]{2,1,0:T(8,128)(2,1)}, s32[256]{0:T(256)S(1)}) custom-call(s32[64]{0:T(128)S(1)} %reshape.15.wanted_ref, s32[8,4]{1,0:T(8,128)S(1)} %copy.19.pcols_ref, bf16[8,128,128]{2,1,0:T(8,128)(2,1)S(1)} %copy-done.1), custom_call_target="tpu_custom_call" | custom-call | tf_op jit(solution)/shard_map/prep/pallas_call | solution.py:38
  5.5 0.0 copy-start
  5.6 0.7 copy-done
  6.3 0.1 all_to_all.9
  6.3 14.2 %all_to_all.14 = s32[32,1,8]{2,1,0:T(1,128)S(1)} all-to-all(s32[32,1,8]{2,1,0:T(1,128)S(1)} %bitcast.4), channel_id=1, replica_groups=mesh['group'=4,'chip'=4,'core'=2] {'group','chip','core'}, dimensions={0} | all-to-all | bytes 2048 | tf_op jit(solution)/shard_map/all_to_all | solution.py:235
  20.6 2.7 %all-to-all-start.1 = ((bf16[64,128,128]{2,1,0:T(8,128)(2,1)}), bf16[64,128,128]{2,1,0:T(8,128)(2,1)S(1)}, u32[]{:S(2)}, u32[]{:S(2)}) async-start(bf16[64,128,128]{2,1,0:T(8,128)(2,1)} %get-tuple-element.16), calls=%async_computation.1 | async-start | bytes 4194304 | tf_op jit(solution)/shard_map/all_to_all | solution.py:234
  23.3 0.0 copy-done.2
  23.3 0.1 reshape.14
  23.4 8.8 %weigh.1.w_ref = bf16[8,22,128,128]{3,2,1,0:T(8,128)(2,1)} custom-call(bf16[8,128,128]{2,1,0:T(8,128)(2,1)} %copy-done, bf16[8,22,128,128]{3,2,1,0:T(8,128)(2,1)} %a_ref.1), custom_call_target="tpu_custom_call" | custom-call | flops 738197504 | bytes 11534336 | tf_op jit(solution)/shard_map/weigh/pallas_call | solution.py:63
  32.2 0.6 pad_add_fusion.1.place_ref
  32.8 0.5 broadcast.3
  33.4 0.7 reduce.3
  34.0 0.1 reshape.16
  34.1 0.6 pad_add_fusion.far_ref
  34.7 38.7 %all-to-all-done.1.arrived_ref = bf16[64,128,128]{2,1,0:T(8,128)(2,1)S(1)} async-done(((bf16[64,128,128]{2,1,0:T(8,128)(2,1)}), bf16[64,128,128]{2,1,0:T(8,128)(2,1)S(1)}, u32[]{:S(2)}, u32[]{:S(2)}) %all-to-all-start.1) | async-done | bytes 2097184 | tf_op jit(solution)/shard_map/all_to_all | solution.py:234
  73.4 0.0 copy-start.3
  73.4 1.3 %copy-done.3 = bf16[64,128,128]{2,1,0:T(8,128)(2,1)} copy-done((bf16[64,128,128]{2,1,0:T(8,128)(2,1)}, bf16[64,128,128]{2,1,0:T(8,128)(2,1)S(1)}, u32[]{:S(2)}) %copy-start.3) | copy-done | bytes 2097176
  74.7 15.2 %merge.1 = (f32[4,864,128]{2,1,0:T(8,128)}, bf16[4,864,128]{2,1,0:T(8,128)(2,1)}) custom-call(s32[3]{0:T(128)} %pad_add_fusion.1.place_ref, s32[8,22]{1,0:T(8,128)} %acols_ref.1, s32[8,4]{1,0:T(8,128)} %copy-done.2, s32[288]{0:T(512)} %pad_add_fusion.far_ref, s32[32,27]{1,0:T(8,128)} %ccols_ref.1, bf16[8,22,128,128]{3,2,1,0:T(8,128)(2,1)} %weigh.1.w_ref, ...), custom_call_target="tpu_custom_call" | custom-call | tf_op jit(solution)/shard_map/merge/pallas_call | solution.py:153
  90.0 0.1 collective-permute-start
  90.0 2.6 %collective-permute-done.got_ref = bf16[4,864,128]{2,1,0:T(8,128)(2,1)S(1)} collective-permute-done((bf16[4,864,128]{2,1,0:T(8,128)(2,1)}, bf16[4,864,128]{2,1,0:T(8,128)(2,1)S(1)}, u32[]{:S(2)}, u32[]{:S(2)}) %collective-permute-start) | collective-permute-done | bytes 884768 | tf_op jit(solution)/shard_map/ppermute | solution.py:241
  92.7 0.0 copy-start.4
  92.7 0.9 copy-done.4
  93.6 2.8 %pair.1 = (f32[864,128]{1,0:T(8,128)}, bf16[864,128]{1,0:T(8,128)(2,1)}, bf16[864,128]{1,0:T(8,128)(2,1)}, bf16[864,128]{1,0:T(8,128)(2,1)}) custom-call(s32[3]{0:T(128)} %pad_add_fusion.1.place_ref, f32[4,864,128]{2,1,0:T(8,128)} %get-tuple-element.17.keep_ref, bf16[4,864,128]{2,1,0:T(8,128)(2,1)} %copy-done.4), custom_call_target="tpu_custom_call" | custom-call | tf_op jit(solution)/shard_map/pair/pallas_call | solution.py:193
  96.4 0.0 collective-permute-start.1
  96.4 0.3 collective-permute-start.2
  96.7 4.1 %collective-permute-start.3 = (bf16[864,128]{1,0:T(8,128)(2,1)}, bf16[864,128]{1,0:T(8,128)(2,1)S(1)}, u32[]{:S(2)}, u32[]{:S(2)}) collective-permute-start(bf16[864,128]{1,0:T(8,128)(2,1)} %get-tuple-element.22), channel_id=1, source_target_pairs={{0,6},{2,4},{4,2},{6,0},{1,7},{3,5},{5,3},{7,1},{8,14},{10,12},{12... | collective-permute-start | bytes 663560 | tf_op jit(solution)/shard_map/ppermute | solution.py:246
  100.8 5.2 %collective-permute-done.1.refs_0_ = bf16[864,128]{1,0:T(8,128)(2,1)S(1)} collective-permute-done((bf16[864,128]{1,0:T(8,128)(2,1)}, bf16[864,128]{1,0:T(8,128)(2,1)S(1)}, u32[]{:S(2)}, u32[]{:S(2)}) %collective-permute-start.1) | collective-permute-done | bytes 221216 | tf_op jit(solution)/shard_map/ppermute | solution.py:246
  106.0 0.0 copy-start.5
  106.0 9.3 %collective-permute-done.2.refs_1_ = bf16[864,128]{1,0:T(8,128)(2,1)S(1)} collective-permute-done((bf16[864,128]{1,0:T(8,128)(2,1)}, bf16[864,128]{1,0:T(8,128)(2,1)S(1)}, u32[]{:S(2)}, u32[]{:S(2)}) %collective-permute-start.2) | collective-permute-done | bytes 221216 | tf_op jit(solution)/shard_map/ppermute | solution.py:246
  115.3 0.0 copy-start.6
  115.3 0.0 collective-permute-done.3.refs_2_
  115.3 0.0 copy-start.7
  115.3 0.0 copy-done.5
  115.3 0.7 copy-done.6
  116.0 0.1 copy-done.7
  116.1 2.2 %last.1 = f32[4,32,864]{2,1,0:T(8,128)} custom-call(f32[864,128]{1,0:T(8,128)} %get-tuple-element.19.mine_ref, bf16[864,128]{1,0:T(8,128)(2,1)} %copy-done.5, bf16[864,128]{1,0:T(8,128)(2,1)} %copy-done.6, bf16[864,128]{1,0:T(8,128)(2,1)} %copy-done.7), custom_call_target="tpu_custom_call" | custom-call | tf_op jit(solution)/shard_map/last/pallas_call | solution.py:215
Async XLA Ops:
  0.8 22.6 %copy-start.2 = (s32[8,4]{1,0:T(8,128)}, s32[8,4]{1,0:T(8,128)S(1)}, u32[]{:S(2)}) copy-start(s32[8,4]{1,0:T(8,128)S(1)} %copy.19.pcols_ref) | copy-start | bytes 388
  1.6 1.0 copy-start.1
  5.5 0.7 copy-start
  20.6 52.8 %all-to-all-start.1 = ((bf16[64,128,128]{2,1,0:T(8,128)(2,1)}), bf16[64,128,128]{2,1,0:T(8,128)(2,1)S(1)}, u32[]{:S(2)}, u32[]{:S(2)}) async-start(bf16[64,128,128]{2,1,0:T(8,128)(2,1)} %get-tuple-element.16), calls=%async_computation.1 | async-start | bytes 4194304 | tf_op jit(solution)/shard_map/all_to_all | solution.py:234
  73.4 1.3 %copy-start.3 = (bf16[64,128,128]{2,1,0:T(8,128)(2,1)}, bf16[64,128,128]{2,1,0:T(8,128)(2,1)S(1)}, u32[]{:S(2)}) copy-start(bf16[64,128,128]{2,1,0:T(8,128)(2,1)S(1)} %all-to-all-done.1.arrived_ref) | copy-start | bytes 6291460
  90.0 2.7 %collective-permute-start = (bf16[4,864,128]{2,1,0:T(8,128)(2,1)}, bf16[4,864,128]{2,1,0:T(8,128)(2,1)S(1)}, u32[]{:S(2)}, u32[]{:S(2)}) collective-permute-start(bf16[4,864,128]{2,1,0:T(8,128)(2,1)} %get-tuple-element.18), channel_id=1, source_target_pairs={{0,1},{1,0},{2,3},{3,2},{4,5},{5,4},{6,7},{7,6},{8,9},{9,8},{10,11... | collective-permute-start | bytes 2654216 | tf_op jit(solution)/shard_map/ppermute | solution.py:241
  92.7 0.9 copy-start.4
  96.4 9.6 %collective-permute-start.1 = (bf16[864,128]{1,0:T(8,128)(2,1)}, bf16[864,128]{1,0:T(8,128)(2,1)S(1)}, u32[]{:S(2)}, u32[]{:S(2)}) collective-permute-start(bf16[864,128]{1,0:T(8,128)(2,1)} %get-tuple-element.20), channel_id=1, source_target_pairs={{0,2},{2,0},{4,6},{6,4},{1,3},{3,1},{5,7},{7,5},{8,10},{10,8},{12,... | collective-permute-start | bytes 663560 | tf_op jit(solution)/shard_map/ppermute | solution.py:246
  96.4 18.9 %collective-permute-start.2 = (bf16[864,128]{1,0:T(8,128)(2,1)}, bf16[864,128]{1,0:T(8,128)(2,1)S(1)}, u32[]{:S(2)}, u32[]{:S(2)}) collective-permute-start(bf16[864,128]{1,0:T(8,128)(2,1)} %get-tuple-element.21), channel_id=1, source_target_pairs={{0,4},{2,6},{4,0},{6,2},{1,5},{3,7},{5,1},{7,3},{8,12},{10,14},{12... | collective-permute-start | bytes 663560 | tf_op jit(solution)/shard_map/ppermute | solution.py:246
  96.7 18.6 %collective-permute-start.3 = (bf16[864,128]{1,0:T(8,128)(2,1)}, bf16[864,128]{1,0:T(8,128)(2,1)S(1)}, u32[]{:S(2)}, u32[]{:S(2)}) collective-permute-start(bf16[864,128]{1,0:T(8,128)(2,1)} %get-tuple-element.22), channel_id=1, source_target_pairs={{0,6},{2,4},{4,2},{6,0},{1,7},{3,5},{5,3},{7,1},{8,14},{10,12},{12... | collective-permute-start | bytes 663560 | tf_op jit(solution)/shard_map/ppermute | solution.py:246
  106.0 9.3 %copy-start.5 = (bf16[864,128]{1,0:T(8,128)(2,1)}, bf16[864,128]{1,0:T(8,128)(2,1)S(1)}, u32[]{:S(2)}) copy-start(bf16[864,128]{1,0:T(8,128)(2,1)S(1)} %collective-permute-done.1.refs_0_) | copy-start | bytes 663556
  115.3 0.7 copy-start.6
  115.3 0.8 copy-start.7

commit v2 on v1

v2 whole, which is shorter than its diff:
```python
import functools
import math

import jax
import jax.numpy as jnp
from jax import lax
from jax.experimental import pallas as pl
from jax.experimental.pallas import tpu as pltpu
from jax.sharding import Mesh, PartitionSpec as P

NT = (((1,), (1,)), ((), ()))
NN = (((1,), (0,)), ((), ()))


VMEM_SLACK = 4 << 20
VMEM_MOST = 56 << 20
FAR_MOST = 54 << 20


def whole(*shape):
    return pl.BlockSpec(shape, lambda *_: (0,) * len(shape))


def room(*arrays):
    return VMEM_SLACK + sum(math.prod(shape) * jnp.dtype(kind).itemsize for shape, kind in arrays)


def flip(rows_ref, unit, row):
    return lax.dot_general(
        unit, rows_ref[row], NT, preferred_element_type=jnp.float32
    ).astype(rows_ref.dtype)


def identity(width, kind):
    row_id = lax.broadcasted_iota(jnp.int32, (width, width), 0)
    col_id = lax.broadcasted_iota(jnp.int32, (width, width), 1)
    return jnp.where(row_id == col_id, 1.0, 0.0).astype(kind)


def device_of(place_ref, hop, half):
    group = jnp.bitwise_xor(place_ref[5], hop >> 1)
    low = jnp.bitwise_xor(place_ref[6], hop & 1)
    return group, ((group * 2 + half) * 2 + low) * 2


def pack_two_kernel(peers, slots, parts, place_ref, own_ref, other_ref, p_ref, q_ref, *refs):
    outs, pt_ref, table = refs[:8], refs[8], refs[9]
    rows, span, width = p_ref.shape
    core, base, half = place_ref[0], place_ref[1], place_ref[3]
    unit = identity(width, p_ref.dtype)
    for row in range(rows):
        mine = flip(p_ref, unit, row)
        table[core * rows + row] = mine
        table[(1 - core) * rows + row] = flip(q_ref, unit, row)
        pt_ref[row] = mine
    tail = outs[0].shape[1] - slots * width
    lane = lax.broadcasted_iota(jnp.int32, (tail, span), 1)
    for hop, out_ref in enumerate(outs):
        _, device = device_of(place_ref, hop, half)
        for source in range(2):
            note = jnp.zeros((tail, span), jnp.int32)
            mine = core == source
            for slot in range(slots):
                at = slot * peers + device + core
                row = jnp.maximum(jnp.where(mine, own_ref[at], other_ref[at]), 0)
                out_ref[source, slot * width : (slot + 1) * width, :] = table[source * rows + row]
                for part in range(parts):
                    spot = slots * peers + part * rows + row
                    column = jnp.where(mine, own_ref[spot], other_ref[spot]) - base
                    note = jnp.where(lane == slot * parts + part, column, note)
            out_ref[source, slots * width :, :] = note.astype(jnp.float32).astype(out_ref.dtype)


def pack_two(place, own, other, p_rows, q_rows, peers, slots, parts):
    rows, span, width = p_rows.shape
    vmem, smem = pl.BlockSpec(memory_space=pltpu.VMEM), pl.BlockSpec(memory_space=pltpu.SMEM)
    kind = p_rows.dtype
    piece = (2, slots * width + 16, span)
    outs = [jax.ShapeDtypeStruct(piece, kind)] * 8
    outs.append(jax.ShapeDtypeStruct((rows, width, span), kind))
    return pl.pallas_call(
        functools.partial(pack_two_kernel, peers, slots, parts),
        out_shape=tuple(outs),
        in_specs=[smem, smem, smem, vmem, vmem],
        out_specs=(vmem,) * len(outs),
        scratch_shapes=[pltpu.VMEM((2 * rows, width, span), kind)],
        compiler_params=pltpu.CompilerParams(
            vmem_limit_bytes=room((piece, kind), *[(piece, kind)] * 7, *[(p_rows.shape, kind)] * 6)
        ),
        name="pack_two",
    )(place, own, other, p_rows, q_rows)


def pack_kernel(slots, parts, place_ref, facts_ref, p_ref, out_ref, pt_ref):
    rows, span, width = p_ref.shape
    base, half, low = place_ref[1], place_ref[3], place_ref[4]
    unit = identity(width, p_ref.dtype)
    for row in range(rows):
        pt_ref[row] = flip(p_ref, unit, row)
    tail = out_ref.shape[1] - slots * width
    lane = lax.broadcasted_iota(jnp.int32, (tail, span), 1)
    peers = (facts_ref.shape[0] - parts * rows) // slots

    def fill(index, carry):
        device = (2 * (index // low) + half) * low + lax.rem(index, low)
        note = jnp.zeros((tail, span), jnp.int32)
        for slot in range(slots):
            row = jnp.maximum(facts_ref[slot * peers + device], 0)
            out_ref[index, slot * width : (slot + 1) * width, :] = pt_ref[row]
            for part in range(parts):
                column = facts_ref[slots * peers + part * rows + row] - base
                note = jnp.where(lane == slot * parts + part, column, note)
        out_ref[index, slots * width :, :] = note.astype(jnp.float32).astype(out_ref.dtype)
        return carry

    lax.fori_loop(0, out_ref.shape[0], fill, 0)


def pack(place, facts, p_rows, slots, parts):
    rows, span, width = p_rows.shape
    vmem, smem = pl.BlockSpec(memory_space=pltpu.VMEM), pl.BlockSpec(memory_space=pltpu.SMEM)
    kind = p_rows.dtype
    peers = (facts.shape[0] - parts * rows) // slots
    outgoing = (peers // 2, slots * width + 16, span)
    flipped = (rows, width, span)
    return pl.pallas_call(
        functools.partial(pack_kernel, slots, parts),
        out_shape=(jax.ShapeDtypeStruct(outgoing, kind), jax.ShapeDtypeStruct(flipped, kind)),
        in_specs=[smem, smem, vmem],
        out_specs=(vmem, vmem),
        compiler_params=pltpu.CompilerParams(
            vmem_limit_bytes=room((outgoing, kind), *[(flipped, kind)] * 3)
        ),
        name="pack",
    )(place, facts, p_rows)


def distinct(columns, blocks, dump):
    columns, blocks = list(columns), list(blocks)
    for n in range(1, len(columns)):
        again = jnp.bool_(False)
        for before in range(n):
            same = columns[n] == columns[before]
            blocks[before] = blocks[before] + jnp.where(same, blocks[n], 0.0)
            again = again | same
        columns[n] = jnp.where(again, dump, columns[n])
    return columns, blocks


def near_kernel(
    first_row, resumed, place_ref, acols_ref, pcols_ref, ccols_ref, *refs
):
    if resumed:
        where_in, pt_ref, a_ref, panel_in, far_in, panel_out, far_out, where_ref = refs[:8]
        dense, panel, far, weights, products, sems = refs[8:]
        slot_of_ref = ctable_ref = None
    else:
        ctable_ref, pt_ref, a_ref, panel_out, far_out, where_ref, slot_of_ref = refs[:7]
        dense, panel, far, weights, products, sems = refs[7:]
    step, steps = pl.program_id(0), pl.num_programs(0)
    fine_row = step + first_row
    parts, fine_rows = pcols_ref.shape
    block_cols, width = a_ref.shape[1], pt_ref.shape[1]
    span = width // parts
    pattern = ccols_ref.shape[1]
    slots = far_out.shape[0]
    own_rows = width // span
    base = place_ref[1]
    dump = dense.shape[0] // span - 1
    if resumed:
        load_panel = pltpu.make_async_copy(panel_in, panel, sems.at[0])
        load_far = pltpu.make_async_copy(far_in, far.at[pl.ds(0, slots)], sems.at[1])

    @pl.when(step == 0)
    def _():
        if resumed:
            load_panel.start()
            load_far.start()
        else:
            panel[...] = jnp.zeros_like(panel)
            far[...] = jnp.zeros_like(far)
            column = lax.broadcasted_iota(jnp.int32, slot_of_ref.shape, 1)
            found = jnp.full(slot_of_ref.shape, pattern, jnp.int32)
            for s in range(pattern):
                found = jnp.where(column == ctable_ref[:, s : s + 1], s, found)
            slot_of_ref[...] = found

        def begin(slot, carry):
            where_ref[slot] = where_in[slot] if resumed else fine_rows
            return carry

        lax.fori_loop(0, slots, begin, 0)

    dense[...] = jnp.zeros_like(dense)
    left = pt_ref[fine_row]
    for k in range(0, block_cols, 2):
        ahead = range(k, min(k + 2, block_cols))
        weighted = lax.dot_general(
            left,
            jnp.concatenate([a_ref[0, j] for j in ahead], axis=1),
            NN,
            preferred_element_type=jnp.float32,
        ).astype(far.dtype)
        for j in ahead:
            weights[j] = weighted[:, (j - k) * width : (j - k + 1) * width]
    for k in range(block_cols):
        source = acols_ref[fine_row, k]
        row = jnp.where(source >= fine_rows, 0, source)
        products[k] = lax.dot_general(
            pt_ref[row], weights[k], NT, preferred_element_type=jnp.float32
        )
    if resumed:

        @pl.when(step == 0)
        def _():
            load_panel.wait()
            load_far.wait()

    for k in range(block_cols):
        source = acols_ref[fine_row, k]
        is_far = source >= fine_rows
        slot = jnp.where(is_far, source - fine_rows, slots)
        far[slot] = weights[k]
        where_ref[slot] = fine_row
        row = jnp.where(is_far, 0, source)
        columns, blocks = distinct(
            [pcols_ref[n, row] for n in range(parts)],
            [products[k, n * span : (n + 1) * span, :] for n in range(parts)],
            dump,
        )
        places = [
            pl.ds(pl.multiple_of(jnp.where(is_far, dump, column) * span, span), span)
            for column in columns
        ]
        sums = [dense[at, :] + block for at, block in zip(places, blocks)]
        for at, value in zip(places, sums):
            dense[at, :] = value

    lane_group = lax.broadcasted_iota(jnp.int32, (span, width), 1) // span
    for m in range(parts):
        row = pcols_ref[m, fine_row] - base
        owner, within = row // own_rows, lax.rem(row, own_rows)
        shift = lax.rem(within + parts - m, parts) * span
        here = lane_group == within
        for first in range(0, pattern, 9):
            chunk = range(first, min(first + 9, pattern))
            sums = []
            for s in chunk:
                at = pl.ds(pl.multiple_of(ccols_ref[row, s] * span, span), span)
                moved = pltpu.roll(dense[at, :], shift, 1)
                sums.append(
                    panel[owner, s * span : (s + 1) * span, :] + jnp.where(here, moved, 0.0)
                )
            for s, value in zip(chunk, sums):
                panel[owner, s * span : (s + 1) * span, :] = value

    @pl.when(step == steps - 1)
    def _():
        one = pltpu.make_async_copy(panel, panel_out, sems.at[0])
        two = pltpu.make_async_copy(far.at[pl.ds(0, slots)], far_out, sems.at[1])
        one.start()
        two.start()
        one.wait()
        two.wait()


def near(first_row, rows_here, place, a_cols, pcols_t, c_cols, pt, a_blocks, owners, all_cols, slots, before):
    rows, cols, span, _ = a_blocks.shape
    parts, width = pcols_t.shape[0], pt.shape[1]
    small = width // parts
    group_rows, pattern = c_cols.shape
    tall = (pattern + 1) * small
    hbm, smem = pl.BlockSpec(memory_space=pltpu.HBM), pl.BlockSpec(memory_space=pltpu.SMEM)
    out_shape = [
        jax.ShapeDtypeStruct((owners, tall, width), jnp.float32),
        jax.ShapeDtypeStruct((slots, width, span), jnp.bfloat16),
        jax.ShapeDtypeStruct((slots + 1,), jnp.int32),
    ]
    out_specs = [hbm, hbm, smem]
    in_specs = [
        whole(rows, width, span),
        pl.BlockSpec((1, cols, span, span), lambda i, *_: (i + first_row, 0, 0, 0)),
    ]
    scalars = [place, a_cols, pcols_t, c_cols]
    if before is None:
        in_specs.insert(0, whole(group_rows, pattern))
        operands = [c_cols, pt, a_blocks]
        out_shape.append(jax.ShapeDtypeStruct((group_rows, all_cols + 128), jnp.int32))
        out_specs.append(whole(group_rows, all_cols + 128))
    else:
        scalars.append(before[2])
        operands = [pt, a_blocks, before[0], before[1]]
        in_specs += [hbm, hbm]
    scratch = [
        (((all_cols + 1) * small, width), jnp.float32),
        ((owners, tall, width), jnp.float32),
        ((slots + 1, width, span), jnp.bfloat16),
        ((cols, width, span), jnp.bfloat16),
        ((cols, width, width), jnp.float32),
    ]
    return pl.pallas_call(
        functools.partial(near_kernel, first_row, before is not None),
        out_shape=tuple(out_shape),
        grid_spec=pltpu.PrefetchScalarGridSpec(
            num_scalar_prefetch=len(scalars),
            grid=(rows_here,),
            in_specs=in_specs,
            out_specs=tuple(out_specs),
            scratch_shapes=[pltpu.VMEM(*one) for one in scratch] + [pltpu.SemaphoreType.DMA((2,))],
        ),
        compiler_params=pltpu.CompilerParams(
            vmem_limit_bytes=VMEM_MOST
        ),
        cost_estimate=pl.CostEstimate(flops=1, bytes_accessed=1, transcendentals=0),
        name="near",
    )(*scalars, *operands)


def far_kernel(
    counts, steps, place_ref, where_ref, pcols_ref, slot_of_ref, far_in, panel_in, *refs
):
    arrived = refs[: len(counts)]
    keep_ref, send_ref, panel, far_ref, products, columns, columns_s, sems, *extra = refs[
        len(counts) :
    ]
    hidden = bool(extra)
    gathered = extra[0] if hidden else panel
    step = 0 if steps == 1 else pl.program_id(0)
    parts, fine_rows = pcols_ref.shape
    width = far_ref.shape[1]
    small = width // parts
    chips, tall = keep_ref.shape[0], keep_ref.shape[1]
    pattern = tall // small
    own_rows = width // small
    core, base, half, low = (place_ref[at] for at in (0, 1, 3, 4))
    total = sum(counts)
    slots = products.shape[0] // total
    unlisted = slot_of_ref.shape[1] - 1
    load = pltpu.make_async_copy(panel_in, panel, sems.at[0])
    load_far = pltpu.make_async_copy(far_in, far_ref, sems.at[1])

    def spread(peer, which):
        group = peer // low
        return group, (2 * group + which) * low + lax.rem(peer, low)

    def source_of(index):
        if len(counts) == 2:
            each = counts[0]
            peer = step * each + lax.rem(index, each)
            return spread(peer, jnp.bitwise_xor(half, index // each))
        near_by = 2 * (len(counts) - 1)
        hop = jnp.minimum(index, near_by - 1) // 2
        group_a, device_a = device_of(place_ref, hop, half)
        group_b, device_b = spread(jnp.maximum(index - near_by, 0), 1 - half)
        first = index < near_by
        return (
            jnp.where(first, group_a, group_b),
            jnp.where(first, device_a + lax.rem(index, 2), device_b),
        )

    def at_start(action):
        action() if steps == 1 else pl.when(step == 0)(action)

    def begin():
        load_far.start()
        load.start()

    at_start(begin)
    order = [(a, e) for a, count in enumerate(counts) for e in range(count)]
    for index, (a, e) in enumerate(order):
        note = arrived[a][e, slots * width :, :].astype(jnp.float32)[0:1, :]
        columns[index : index + 1, :] = note.astype(jnp.int32)
    tell = pltpu.make_async_copy(columns, columns_s, sems.at[2])
    tell.start()
    if hidden:
        gathered[...] = jnp.zeros_like(gathered)
    at_start(load_far.wait)
    for index, (a, e) in enumerate(order):
        _, device = source_of(jnp.int32(index))
        for slot in range(slots):
            products[index * slots + slot] = lax.dot_general(
                arrived[a][e, slot * width : (slot + 1) * width, :],
                far_ref[device * slots + slot],
                NT,
                preferred_element_type=jnp.float32,
            )
    tell.wait()
    if not hidden:
        at_start(load.wait)

    lane_group = lax.broadcasted_iota(jnp.int32, (small, width), 1) // small

    def place_one(index, slot):
        group, device = source_of(index)
        start = group * (own_rows * 2 * chips)
        row = where_ref[device * slots + slot]
        idle = row >= fine_rows
        row = jnp.minimum(row, fine_rows - 1)
        wanted, blocks = distinct(
            [columns_s[index, slot * parts + n] + start for n in range(parts)],
            [products[index * slots + slot, n * small : (n + 1) * small, :] for n in range(parts)],
            unlisted,
        )
        for m in range(parts):
            target = pcols_ref[m, row] - base
            owner, within = target // own_rows, lax.rem(target, own_rows)
            shift = lax.rem(within + parts - m, parts) * small
            here = lane_group == within
            places = []
            for column in wanted:
                s = jnp.where(idle, pattern, slot_of_ref[target, column])
                places.append(pl.ds(pl.multiple_of(s * small, small), small))
            sums = [
                gathered[owner, at, :] + jnp.where(here, pltpu.roll(block, shift, 1), 0.0)
                for at, block in zip(places, blocks)
            ]
            for at, value in zip(places, sums):
                gathered[owner, at, :] = value

    def place_source(index, carry):
        for slot in range(slots):
            place_one(index, slot)
        return carry

    lax.fori_loop(0, total, place_source, 0, unroll=4)

    def end():
        if hidden:
            load.wait()

        def take(owner):
            value = panel[owner, 0:tall, :]
            return value + gathered[owner, 0:tall, :] if hidden else value

        for chip in range(chips):
            send_ref[chip] = take(2 * chip + 1 - core).astype(send_ref.dtype)
            keep_ref[chip] = take(2 * chip + core)

    end() if steps == 1 else pl.when(step == steps - 1)(end)


def add_far(place, where, pcols_t, slot_of, arrived, far, panel, chips):
    steps = 8 if len(arrived) == 2 else 1
    payload, span = arrived[0].shape[1:]
    counts = tuple(one.shape[0] // steps for one in arrived)
    slots, width = far.shape[0], far.shape[1]
    owners, padded, _ = panel.shape
    tall = padded - width // pcols_t.shape[0]
    hbm, smem = pl.BlockSpec(memory_space=pltpu.HBM), pl.BlockSpec(memory_space=pltpu.SMEM)
    outs = ((chips, tall, width), jnp.float32), ((chips, tall, width), jnp.bfloat16)
    held = ((owners, padded, width), jnp.float32)
    scratch = [
        held,
        (far.shape, far.dtype),
        ((slots // steps, width, width), jnp.float32),
        ((sum(counts), span), jnp.int32),
    ]
    scratch_shapes = [pltpu.VMEM(*one) for one in scratch] + [
        pltpu.SMEM((sum(counts), span), jnp.int32),
        pltpu.SemaphoreType.DMA((3,)),
    ]
    if steps == 1:
        scratch_shapes.append(pltpu.VMEM(*held))
        vmem = pl.BlockSpec(memory_space=pltpu.VMEM)
        how = dict(
            in_specs=[smem] * 4 + [hbm, hbm] + [vmem] * len(arrived),
            out_specs=(vmem, vmem),
            scratch_shapes=scratch_shapes,
        )
    else:
        how = dict(
            grid_spec=pltpu.PrefetchScalarGridSpec(
                num_scalar_prefetch=4,
                grid=(steps,),
                in_specs=[hbm, hbm]
                + [pl.BlockSpec((n, payload, span), lambda i, *_: (i, 0, 0)) for n in counts],
                out_specs=tuple(whole(*shape) for shape, _ in outs),
                scratch_shapes=scratch_shapes,
            )
        )
    return pl.pallas_call(
        functools.partial(far_kernel, counts, steps),
        out_shape=tuple(jax.ShapeDtypeStruct(*one) for one in outs),
        compiler_params=pltpu.CompilerParams(vmem_limit_bytes=FAR_MOST if steps == 1 else VMEM_MOST),
        name="add_far",
        **how,
    )(place, where, pcols_t, slot_of, far, panel, *arrived)


def pair_kernel(place_ref, keep_ref, got_ref, mine_ref, *out_refs):
    chips = keep_ref.shape[0]
    chip = place_ref[2]
    mine_ref[...] = keep_ref[chip] + got_ref[chip].astype(jnp.float32)
    for off, out_ref in enumerate(out_refs):
        at = jnp.bitwise_xor(chip, off + 1)
        out_ref[...] = (keep_ref[at] + got_ref[at].astype(jnp.float32)).astype(out_ref.dtype)


def pair(place, keep, got):
    chips, tall, width = keep.shape
    vmem, smem = pl.BlockSpec(memory_space=pltpu.VMEM), pl.BlockSpec(memory_space=pltpu.SMEM)
    return pl.pallas_call(
        pair_kernel,
        out_shape=(jax.ShapeDtypeStruct((tall, width), jnp.float32),)
        + (jax.ShapeDtypeStruct((tall, width), jnp.bfloat16),) * (chips - 1),
        in_specs=[smem, vmem, vmem],
        out_specs=(vmem,) * chips,
        compiler_params=pltpu.CompilerParams(vmem_limit_bytes=room((keep.shape, keep.dtype), (got.shape, got.dtype), *[((tall, width), jnp.float32)] * chips)),
        name="pair",
    )(place, keep, got)


def last_kernel(mine_ref, *refs):
    terms, out_ref = refs[:-1], refs[-1]
    total = mine_ref[...]
    for term in terms:
        total = total + term[...].astype(jnp.float32)
    out_ref[...] = total.T.reshape(out_ref.shape)


def last(mine, terms, own_rows):
    tall, width = mine.shape
    vmem = pl.BlockSpec(memory_space=pltpu.VMEM)
    return pl.pallas_call(
        last_kernel,
        out_shape=jax.ShapeDtypeStruct((own_rows, width // own_rows, tall), jnp.float32),
        in_specs=[vmem] * (1 + len(terms)),
        out_specs=vmem,
        compiler_params=pltpu.CompilerParams(vmem_limit_bytes=room(*[(mine.shape, mine.dtype)] * (3 + len(terms)))),
        name="last",
    )(mine, *terms)


def swap(axis, *arrays):
    return [lax.ppermute(one, axis, [(0, 1), (1, 0)]) for one in arrays]


def local(chips, groups, a_blocks, a_cols, p_rows, p_cols, send_rows, c_cols):
    group_rows, parts = c_cols.shape[0], p_cols.shape[1]
    peers, slot_count = send_rows.shape[1:]
    slots = peers * slot_count
    group, half = lax.axis_index("group"), lax.axis_index("zh")
    chip = lax.axis_index(("zh", "zl"))
    low = lax.axis_index("zl")
    place = jnp.stack(
        [lax.axis_index("core"), group * group_rows, chip, half, jnp.int32(chips), group, low]
    ).astype(jnp.int32)
    wanted, pcols_t = send_rows[0].T, p_cols.T
    sizes = (2 * chips, group_rows * groups, slots)
    rows = a_blocks.shape[0]
    facts = jnp.concatenate([wanted.reshape(-1), pcols_t.reshape(-1)])
    over, facts_over = swap("zh", p_rows, facts)
    scatter = functools.partial(
        lax.all_to_all, axis_name=("group", "zl", "core"), split_axis=0, concat_axis=0, tiled=True
    )
    if chips == 4 and groups == 4:
        beside, facts_beside = swap("core", p_rows, facts)
        *out, pt = pack_two(
            place, facts, facts_beside, p_rows, beside, peers, slot_count, parts
        )
        arrived = out[:1] + [
            lax.ppermute(out[hop], ("group", "zl"), [(q, q ^ hop) for q in range(8)])
            for hop in range(1, 8)
        ]
        over, facts_over, *arrived = lax.optimization_barrier((over, facts_over, *arrived))
    else:
        outgoing, pt = pack(place, facts, p_rows, slot_count, parts)
        arrived = [scatter(outgoing)]
    outgoing, _ = pack(place, facts_over, over, slot_count, parts)
    outgoing, pt = lax.optimization_barrier((outgoing, pt))
    arrived.append(scatter(outgoing))
    panel, far, where, slot_of = near(
        0, rows, place, a_cols, pcols_t, c_cols, pt, a_blocks, *sizes, None
    )
    keep, give = add_far(place, where, pcols_t, slot_of, arrived, far, panel, chips)
    got, = swap("core", give)
    own_rows = group_rows // (2 * chips)
    line = ("zh", "zl")
    if chips == 4:
        mine, *out = pair(place, keep, got)
        terms = [
            lax.ppermute(piece, line, [(q, q ^ (off + 1)) for q in range(chips)])
            for off, piece in enumerate(out)
        ]
        return last(mine, terms, own_rows)
    both = keep + got.astype(jnp.float32)
    mine = lax.dynamic_index_in_dim(both, chip, 0, keepdims=False)
    came = lax.all_to_all(
        both.astype(jnp.bfloat16), line, split_axis=0, concat_axis=0, tiled=True
    ).astype(jnp.float32)
    other = jnp.arange(chips)[:, None, None] != chip
    return last(mine + jnp.sum(jnp.where(other, came, 0.0), 0), [], own_rows)


def solution(mesh):
    groups, ranks = mesh.shape["group"], mesh.shape["rank"]
    chips = ranks // 2
    every = ("group", "zh", "zl", "core")
    fine = Mesh(mesh.devices.reshape(groups, 2, chips // 2, 2), every)
    in_specs = (P(every), P(every), P(every), P(every), P(every), P("group"))
    return jax.shard_map(
        functools.partial(local, chips, groups),
        mesh=fine,
        in_specs=in_specs,
        out_specs=P(every),
        check_vma=False,
    )
```

time: 120 us -> 101 us (0.84)
  waiting for transfers between devices: 55.8 us -> 32.6 us
  starting transfers between devices: 7.18 us -> 22 us
  blocking collectives: 14.2 us -> 0 us
  Pallas kernels: 32 us -> 38.3 us
  other arithmetic: 1.93 us -> 0.08 us
    all_to_all x1, waiting for transfers between devices: 38.7 us -> 0.01 us  [local(): arrived.append(scatter(outgoing))]
    ppermute x4 -> x15, waiting for transfers between devices: 17.1 us -> 32.6 us  [the longest x3 16.1 us: local(): lax.ppermute(piece, line, [(q, q ^ off + 1) for q in range(chips)])]
    all_to_all x1 -> x0, blocking collectives: 14.2 us -> none  [local(): lax.all_to_all(out_cols.reshape(-1, 2 * parts), everyone, split_axis=0, c...]
    ppermute x4 -> x15, starting transfers between devices: 4.46 us -> 18.3 us  [the longest x7 8.92 us: local(): lax.ppermute(out[hop], ('group', 'zl'), [(q, q ^ hop) for q in range(8)])]
    pallas_call x3 -> x4, Pallas kernels: 26.9 us -> 36.6 us  [the longest x1 18.8 us: near(): pl.pallas_call(functools.partial(near_kernel, first_row, before is not No...]
    pallas_call x1, Pallas kernels: 2.83 us -> 0.72 us  [pair(): pl.pallas_call(pair_kernel, out_shape=(jax.ShapeDtypeStruct((tall, width)...]
    unnamed x18 -> x28, local copies, waits for them, and re-layouts: 6.18 us -> 4.85 us
    reshape x3 -> x2, local copies, waits for them, and re-layouts: 0.27 us -> 1.52 us  [local(): facts = jnp.concatenate([wanted.reshape(-1), pcols_t.reshape(-1)])]
  transfers between devices with their start and end apart: 5 -> 16, of which waited for: 4 -> 10; matrix products, arithmetic and copies ran while one was open for 2% -> 2% of each run, Pallas kernels for 7% -> 20%
where the time goes in v2:
time: 101 us; the launch traced here: 99.6 us
  Pallas kernels  38.3 us (38%)
  waiting for transfers between devices  32.6 us (32%)
  starting transfers between devices  22 us (22%)
  local copies, waits for them, and re-layouts  6.46 us (6%)
    pallas_call x1, Pallas kernels, near(): pl.pallas_call(functools.partial(near_kernel, first_row, before is not No...  18.8 us
    ppermute x3, waiting for transfers between devices, local(): lax.ppermute(piece, line, [(q, q ^ off + 1) for q in range(chips)])  16.1 us
    pallas_call x1, Pallas kernels, add_far(): pl.pallas_call(functools.partial(far_kernel, counts, steps), out_shape=tu...  14.3 us
    ppermute x7, waiting for transfers between devices, local(): lax.ppermute(out[hop], ('group', 'zl'), [(q, q ^ hop) for q in range(8)])  9.46 us
    ppermute x7, starting transfers between devices, local(): lax.ppermute(out[hop], ('group', 'zl'), [(q, q ^ hop) for q in range(8)])  8.92 us
    ppermute x5, waiting for transfers between devices, swap(): return [lax.ppermute(one, axis, [(0, 1), (1, 0)]) for one in arrays]  6.98 us
    ppermute x5, starting transfers between devices, swap(): return [lax.ppermute(one, axis, [(0, 1), (1, 0)]) for one in arrays]  4.95 us
    unnamed x28, local copies, waits for them, and re-layouts  4.85 us
  transfers between devices with their start and end apart: 16, of which 10 were waited for; matrix products, arithmetic and copies ran while one was open for 2% of the time, Pallas kernels for 20%

profile of v2, /device:TPU:0, one launch (start us, length us, event | category | flops | bytes accessed | tf_op | source)
XLA Modules:
  0.0 99.6 jit_solution(16414829861370533272)
XLA Ops:
  0.0 0.5 collective-permute-start.3
  0.5 3.6 %collective-permute-start = (bf16[8,128,128]{2,1,0:T(8,128)(2,1)}, bf16[8,128,128]{2,1,0:T(8,128)(2,1)S(1)}, u32[]{:S(2)}, u32[]{:S(2)}) collective-permute-start(bf16[8,128,128]{2,1,0:T(8,128)(2,1)} %p_ref.1), channel_id=1, source_target_pairs={{0,4},{4,0},{1,5},{5,1},{2,6},{6,2},{3,7},{7,3},{8,12},{12,8},{9,1... | collective-permute-start | bytes 786440 | tf_op jit(solution)/shard_map/ppermute | solution.py:535
  4.0 0.8 reshape.7
  4.8 0.8 reshape.6
  5.6 0.1 pad_add_fusion.own_ref
  5.6 0.2 collective-permute-start.2
  5.9 0.1 stack.27.place_ref
  6.0 0.8 collective-permute-done.2.other_ref
  6.8 0.0 collective-permute-done.3.q_ref
  6.8 0.9 copy-done.2
  7.7 1.1 %pack_two.1 = (bf16[2,272,128]{2,1,0:T(8,128)(2,1)S(1)}, bf16[2,272,128]{2,1,0:T(8,128)(2,1)S(1)}, bf16[2,272,128]{2,1,0:T(8,128)(2,1)S(1)}, bf16[2,272,128]{2,1...) custom-call(s32[7]{0:T(128)S(1)} %stack.27.place_ref, ...), custom_call_target="tpu_custom_call" | custom-call | tf_op jit(solution)/shard_map/pack_two/pallas_call | solution.py:81
  8.8 0.0 copy-start.1
  8.8 0.7 copy-done.1
  9.5 0.7 copy-done.3
  10.2 1.6 %collective-permute-start.4 = (bf16[2,272,128]{2,1,0:T(8,128)(2,1)S(1)}, bf16[2,272,128]{2,1,0:T(8,128)(2,1)S(1)}, u32[]{:S(2)}, u32[]{:S(2)}) collective-permute-start(bf16[2,272,128]{2,1,0:T(8,128)(2,1)S(1)} %get-tuple-element.38), channel_id=1, source_target_pairs={{0,2},{2,0},{8,10},{10,8},{16,18},{18,16},{24,26},{26,24},{1,3},{3... | collective-permute-start | bytes 417800 | tf_op jit(solution)/shard_map/ppermute | solution.py:562
  11.8 1.5 %collective-permute-start.5 = (bf16[2,272,128]{2,1,0:T(8,128)(2,1)S(1)}, bf16[2,272,128]{2,1,0:T(8,128)(2,1)S(1)}, u32[]{:S(2)}, u32[]{:S(2)}) collective-permute-start(bf16[2,272,128]{2,1,0:T(8,128)(2,1)S(1)} %get-tuple-element.39), channel_id=1, source_target_pairs={{0,8},{2,10},{8,0},{10,2},{16,24},{18,26},{24,16},{26,18},{1,9},{3... | collective-permute-start | bytes 417800 | tf_op jit(solution)/shard_map/ppermute | solution.py:562
  13.3 0.3 collective-permute-start.1
  13.6 0.3 collective-permute-start.6
  13.9 3.8 %collective-permute-done.1.facts_ref = s32[96]{0:T(128)S(1)} collective-permute-done((s32[96]{0:T(128)S(1)}, s32[96]{0:T(128)S(1)}, u32[]{:S(2)}, u32[]{:S(2)}) %collective-permute-start.1) | collective-permute-done | bytes 416 | tf_op jit(solution)/shard_map/ppermute | solution.py:535
  17.7 1.5 %collective-permute-start.7 = (bf16[2,272,128]{2,1,0:T(8,128)(2,1)S(1)}, bf16[2,272,128]{2,1,0:T(8,128)(2,1)S(1)}, u32[]{:S(2)}, u32[]{:S(2)}) collective-permute-start(bf16[2,272,128]{2,1,0:T(8,128)(2,1)S(1)} %get-tuple-element.41), channel_id=1, source_target_pairs={{0,16},{2,18},{8,24},{10,26},{16,0},{18,2},{24,8},{26,10},{1,17},{... | collective-permute-start | bytes 417800 | tf_op jit(solution)/shard_map/ppermute | solution.py:562
  19.2 0.0 collective-permute-done.p_ref
  19.2 0.4 collective-permute-start.8
  19.6 0.3 collective-permute-done.4.refs_1_
  19.9 2.5 %collective-permute-start.9 = (bf16[2,272,128]{2,1,0:T(8,128)(2,1)S(1)}, bf16[2,272,128]{2,1,0:T(8,128)(2,1)S(1)}, u32[]{:S(2)}, u32[]{:S(2)}) collective-permute-start(bf16[2,272,128]{2,1,0:T(8,128)(2,1)S(1)} %get-tuple-element.43), channel_id=1, source_target_pairs={{0,24},{2,26},{8,16},{10,18},{16,8},{18,10},{24,0},{26,2},{1,25},{... | collective-permute-start | bytes 417800 | tf_op jit(solution)/shard_map/ppermute | solution.py:562
  22.4 0.0 collective-permute-done.5.refs_2_
  22.4 1.1 %collective-permute-start.10 = (bf16[2,272,128]{2,1,0:T(8,128)(2,1)S(1)}, bf16[2,272,128]{2,1,0:T(8,128)(2,1)S(1)}, u32[]{:S(2)}, u32[]{:S(2)}) collective-permute-start(bf16[2,272,128]{2,1,0:T(8,128)(2,1)S(1)} %get-tuple-element.44), channel_id=1, source_target_pairs={{0,26},{2,24},{8,18},{10,16},{16,10},{18,8},{24,2},{26,0},{1,27},{... | collective-permute-start | bytes 417800 | tf_op jit(solution)/shard_map/ppermute | solution.py:562
  23.6 0.3 collective-permute-done.6.refs_3_
  23.9 0.0 collective-permute-done.7.refs_4_
  23.9 4.9 %collective-permute-done.8.refs_5_ = bf16[2,272,128]{2,1,0:T(8,128)(2,1)S(1)} collective-permute-done((bf16[2,272,128]{2,1,0:T(8,128)(2,1)S(1)}, bf16[2,272,128]{2,1,0:T(8,128)(2,1)S(1)}, u32[]{:S(2)}, u32[]{:S(2)}) %collective-permute-start.8) | collective-permute-done | bytes 139296 | tf_op jit(solution)/shard_map/ppermute | solution.py:562
  28.8 2.0 %collective-permute-done.9.refs_6_ = bf16[2,272,128]{2,1,0:T(8,128)(2,1)S(1)} collective-permute-done((bf16[2,272,128]{2,1,0:T(8,128)(2,1)S(1)}, bf16[2,272,128]{2,1,0:T(8,128)(2,1)S(1)}, u32[]{:S(2)}, u32[]{:S(2)}) %collective-permute-start.9) | collective-permute-done | bytes 139296 | tf_op jit(solution)/shard_map/ppermute | solution.py:562
  30.8 1.9 %collective-permute-done.10.refs_7_ = bf16[2,272,128]{2,1,0:T(8,128)(2,1)S(1)} collective-permute-done((bf16[2,272,128]{2,1,0:T(8,128)(2,1)S(1)}, bf16[2,272,128]{2,1,0:T(8,128)(2,1)S(1)}, u32[]{:S(2)}, u32[]{:S(2)}) %collective-permute-start.10) | collective-permute-done | bytes 139296 | tf_op jit(solution)/shard_map/ppermute | solution.py:562
  32.7 2.4 %pack.1 = (bf16[16,272,128]{2,1,0:T(8,128)(2,1)}, bf16[8,128,128]{2,1,0:T(8,128)(2,1)}) custom-call(s32[7]{0:T(128)S(1)} %stack.27.place_ref, s32[96]{0:T(128)S(1)} %collective-permute-done.1.facts_ref, bf16[8,128,128]{2,1,0:T(8,128)(2,1)S(1)} %collective-permute-done.p_ref), custom_call_target="tpu_custom_call" | custom-call | tf_op jit(solution)/shard_map/pack/pallas_call | solution.py:126
  35.2 3.7 %all-to-all-start = ((bf16[16,272,128]{2,1,0:T(8,128)(2,1)}), bf16[16,272,128]{2,1,0:T(8,128)(2,1)S(1)}, u32[]{:S(2)}, u32[]{:S(2)}) async-start(bf16[16,272,128]{2,1,0:T(8,128)(2,1)} %get-tuple-element.62), calls=%async_computation | async-start | bytes 2228224 | tf_op jit(solution)/shard_map/all_to_all | solution.py:571
  38.9 18.8 %near.1 = (f32[8,896,128]{2,1,0:T(8,128)}, bf16[64,128,128]{2,1,0:T(8,128)(2,1)}, s32[65]{0:T(128)}, s32[32,256]{1,0:T(8,128)}) custom-call(s32[7]{0:T(128)} %copy-done.4, s32[8,22]{1,0:T(8,128)} %acols_ref.1, s32[4,8]{1,0:T(4,128)} %bitcast.11, s32[32,27]{1,0:T(8,128)} %refs_0_.1, s32[32,27]{1,0:T(8,128)} %refs_0_.1, bf16[8,128,128]{2,1,0:T(8,128)(2,1)} %copy-done.1, ...), custom_call_target="tpu_custom_call" | custom-call | flops 1 | bytes 1 | tf_op jit(solution)/shard_map/near/pallas_call | solution.py:301
  57.8 0.0 all-to-all-done.refs_8_
  57.8 1.0 %copy-done.6 = bf16[16,272,128]{2,1,0:T(8,128)(2,1)} copy-done((bf16[16,272,128]{2,1,0:T(8,128)(2,1)}, bf16[16,272,128]{2,1,0:T(8,128)(2,1)S(1)}, u32[]{:S(2)}) %copy-start.6) | copy-done | bytes 1114136
  58.8 14.3 %add_far.1 = (f32[4,864,128]{2,1,0:T(8,128)}, bf16[4,864,128]{2,1,0:T(8,128)(2,1)}) custom-call(s32[7]{0:T(128)} %copy-done.4, s32[65]{0:T(128)} %get-tuple-element.50.where_ref, s32[4,8]{1,0:T(4,128)} %bitcast.12, s32[32,256]{1,0:T(8,128)} %get-tuple-element.51.slot_of_ref, bf16[64,128,128]{2,1,0:T(8,128)(2,1)} %get-tuple-element.52.far_in, ...), custom_call_target="tpu_custom_call" | custom-call | tf_op jit(solution)/shard_map/add_far/pallas_call | solution.py:481
  73.1 0.3 collective-permute-start.11
  73.5 2.4 %collective-permute-done.11.got_ref = bf16[4,864,128]{2,1,0:T(8,128)(2,1)S(1)} collective-permute-done((bf16[4,864,128]{2,1,0:T(8,128)(2,1)}, bf16[4,864,128]{2,1,0:T(8,128)(2,1)S(1)}, u32[]{:S(2)}, u32[]{:S(2)}) %collective-permute-start.11) | collective-permute-done | bytes 884768 | tf_op jit(solution)/shard_map/ppermute | solution.py:535
  75.8 1.5 %copy-done = f32[4,864,128]{2,1,0:T(8,128)S(1)} copy-done((f32[4,864,128]{2,1,0:T(8,128)S(1)}, f32[4,864,128]{2,1,0:T(8,128)}, u32[]{:S(2)}) %copy-start) | copy-done | bytes 1769496
  77.3 0.7 pair.1
  78.0 1.9 %collective-permute-start.12 = (bf16[864,128]{1,0:T(8,128)(2,1)S(1)}, bf16[864,128]{1,0:T(8,128)(2,1)S(1)}, u32[]{:S(2)}, u32[]{:S(2)}) collective-permute-start(bf16[864,128]{1,0:T(8,128)(2,1)S(1)} %get-tuple-element.66), channel_id=1, source_target_pairs={{0,2},{2,0},{4,6},{6,4},{1,3},{3,1},{5,7},{7,5},{8,10},{10,8},{12,... | collective-permute-start | bytes 663560 | tf_op jit(solution)/shard_map/ppermute | solution.py:582
  79.9 2.6 %collective-permute-start.13 = (bf16[864,128]{1,0:T(8,128)(2,1)S(1)}, bf16[864,128]{1,0:T(8,128)(2,1)S(1)}, u32[]{:S(2)}, u32[]{:S(2)}) collective-permute-start(bf16[864,128]{1,0:T(8,128)(2,1)S(1)} %get-tuple-element.67), channel_id=1, source_target_pairs={{0,4},{2,6},{4,0},{6,2},{1,5},{3,7},{5,1},{7,3},{8,12},{10,14},{12... | collective-permute-start | bytes 663560 | tf_op jit(solution)/shard_map/ppermute | solution.py:582
  82.5 0.0 collective-permute-start.14
  82.5 7.3 %collective-permute-done.12.refs_0_ = bf16[864,128]{1,0:T(8,128)(2,1)S(1)} collective-permute-done((bf16[864,128]{1,0:T(8,128)(2,1)S(1)}, bf16[864,128]{1,0:T(8,128)(2,1)S(1)}, u32[]{:S(2)}, u32[]{:S(2)}) %collective-permute-start.12) | collective-permute-done | bytes 221216 | tf_op jit(solution)/shard_map/ppermute | solution.py:582
  89.8 8.8 %collective-permute-done.13.refs_1_ = bf16[864,128]{1,0:T(8,128)(2,1)S(1)} collective-permute-done((bf16[864,128]{1,0:T(8,128)(2,1)S(1)}, bf16[864,128]{1,0:T(8,128)(2,1)S(1)}, u32[]{:S(2)}, u32[]{:S(2)}) %collective-permute-start.13) | collective-permute-done | bytes 221216 | tf_op jit(solution)/shard_map/ppermute | solution.py:582
  98.6 0.0 collective-permute-done.14.refs_2_
  98.6 1.0 last.1
  (22 shorter events, 0.0 us)
Async XLA Ops:
  0.0 6.8 %collective-permute-start.3 = (bf16[8,128,128]{2,1,0:T(8,128)(2,1)}, bf16[8,128,128]{2,1,0:T(8,128)(2,1)S(1)}, u32[]{:S(2)}, u32[]{:S(2)}) collective-permute-start(bf16[8,128,128]{2,1,0:T(8,128)(2,1)} %p_ref.1), channel_id=1, source_target_pairs={{0,1},{1,0},{2,3},{3,2},{4,5},{5,4},{6,7},{7,6},{8,9},{9,8},{10,11... | collective-permute-start | bytes 786440 | tf_op jit(solution)/shard_map/ppermute | solution.py:535
  0.5 18.8 %collective-permute-start = (bf16[8,128,128]{2,1,0:T(8,128)(2,1)}, bf16[8,128,128]{2,1,0:T(8,128)(2,1)S(1)}, u32[]{:S(2)}, u32[]{:S(2)}) collective-permute-start(bf16[8,128,128]{2,1,0:T(8,128)(2,1)} %p_ref.1), channel_id=1, source_target_pairs={{0,4},{4,0},{1,5},{5,1},{2,6},{6,2},{3,7},{7,3},{8,12},{12,8},{9,1... | collective-permute-start | bytes 786440 | tf_op jit(solution)/shard_map/ppermute | solution.py:535
  5.6 1.1 %collective-permute-start.2 = (s32[96]{0:T(128)S(1)}, s32[96]{0:T(128)S(1)}, u32[]{:S(2)}, u32[]{:S(2)}) collective-permute-start(s32[96]{0:T(128)S(1)} %pad_add_fusion.own_ref), channel_id=1, source_target_pairs={{0,1},{1,0},{2,3},{3,2},{4,5},{5,4},{6,7},{7,6},{8,9},{9,8},{10,11... | collective-permute-start | bytes 1160 | tf_op jit(solution)/shard_map/ppermute | solution.py:535
  6.0 32.9 %copy-start.4 = (s32[7]{0:T(128)}, s32[7]{0:T(128)S(1)}, u32[]{:S(2)}) copy-start(s32[7]{0:T(128)S(1)} %stack.27.place_ref) | copy-start | bytes 88
  6.8 1.0 copy-start.2
  8.8 0.7 copy-start.1
  9.5 0.7 copy-start.3
  10.2 9.7 %collective-permute-start.4 = (bf16[2,272,128]{2,1,0:T(8,128)(2,1)S(1)}, bf16[2,272,128]{2,1,0:T(8,128)(2,1)S(1)}, u32[]{:S(2)}, u32[]{:S(2)}) collective-permute-start(bf16[2,272,128]{2,1,0:T(8,128)(2,1)S(1)} %get-tuple-element.38), channel_id=1, source_target_pairs={{0,2},{2,0},{8,10},{10,8},{16,18},{18,16},{24,26},{26,24},{1,3},{3... | collective-permute-start | bytes 417800 | tf_op jit(solution)/shard_map/ppermute | solution.py:562
  11.8 10.7 %collective-permute-start.5 = (bf16[2,272,128]{2,1,0:T(8,128)(2,1)S(1)}, bf16[2,272,128]{2,1,0:T(8,128)(2,1)S(1)}, u32[]{:S(2)}, u32[]{:S(2)}) collective-permute-start(bf16[2,272,128]{2,1,0:T(8,128)(2,1)S(1)} %get-tuple-element.39), channel_id=1, source_target_pairs={{0,8},{2,10},{8,0},{10,2},{16,24},{18,26},{24,16},{26,18},{1,9},{3... | collective-permute-start | bytes 417800 | tf_op jit(solution)/shard_map/ppermute | solution.py:562
  13.3 4.4 %collective-permute-start.1 = (s32[96]{0:T(128)S(1)}, s32[96]{0:T(128)S(1)}, u32[]{:S(2)}, u32[]{:S(2)}) collective-permute-start(s32[96]{0:T(128)S(1)} %pad_add_fusion.own_ref), channel_id=1, source_target_pairs={{0,4},{4,0},{1,5},{5,1},{2,6},{6,2},{3,7},{7,3},{8,12},{12,8},{9,1... | collective-permute-start | bytes 1160 | tf_op jit(solution)/shard_map/ppermute | solution.py:535
  13.6 10.3 %collective-permute-start.6 = (bf16[2,272,128]{2,1,0:T(8,128)(2,1)S(1)}, bf16[2,272,128]{2,1,0:T(8,128)(2,1)S(1)}, u32[]{:S(2)}, u32[]{:S(2)}) collective-permute-start(bf16[2,272,128]{2,1,0:T(8,128)(2,1)S(1)} %get-tuple-element.40), channel_id=1, source_target_pairs={{0,10},{2,8},{8,2},{10,0},{16,26},{18,24},{24,18},{26,16},{1,11},{... | collective-permute-start | bytes 417800 | tf_op jit(solution)/shard_map/ppermute | solution.py:562
  17.7 6.2 %collective-permute-start.7 = (bf16[2,272,128]{2,1,0:T(8,128)(2,1)S(1)}, bf16[2,272,128]{2,1,0:T(8,128)(2,1)S(1)}, u32[]{:S(2)}, u32[]{:S(2)}) collective-permute-start(bf16[2,272,128]{2,1,0:T(8,128)(2,1)S(1)} %get-tuple-element.41), channel_id=1, source_target_pairs={{0,16},{2,18},{8,24},{10,26},{16,0},{18,2},{24,8},{26,10},{1,17},{... | collective-permute-start | bytes 417800 | tf_op jit(solution)/shard_map/ppermute | solution.py:562
  19.2 9.6 %collective-permute-start.8 = (bf16[2,272,128]{2,1,0:T(8,128)(2,1)S(1)}, bf16[2,272,128]{2,1,0:T(8,128)(2,1)S(1)}, u32[]{:S(2)}, u32[]{:S(2)}) collective-permute-start(bf16[2,272,128]{2,1,0:T(8,128)(2,1)S(1)} %get-tuple-element.42), channel_id=1, source_target_pairs={{0,18},{2,16},{8,26},{10,24},{16,2},{18,0},{24,10},{26,8},{1,19},{... | collective-permute-start | bytes 417800 | tf_op jit(solution)/shard_map/ppermute | solution.py:562
  19.9 37.8 %copy-start.7 = (bf16[2,272,128]{2,1,0:T(8,128)(2,1)}, bf16[2,272,128]{2,1,0:T(8,128)(2,1)S(1)}, u32[]{:S(2)}) copy-start(bf16[2,272,128]{2,1,0:T(8,128)(2,1)S(1)} %collective-permute-done.4.refs_1_) | copy-start | bytes 417796
  19.9 10.9 %collective-permute-start.9 = (bf16[2,272,128]{2,1,0:T(8,128)(2,1)S(1)}, bf16[2,272,128]{2,1,0:T(8,128)(2,1)S(1)}, u32[]{:S(2)}, u32[]{:S(2)}) collective-permute-start(bf16[2,272,128]{2,1,0:T(8,128)(2,1)S(1)} %get-tuple-element.43), channel_id=1, source_target_pairs={{0,24},{2,26},{8,16},{10,18},{16,8},{18,10},{24,0},{26,2},{1,25},{... | collective-permute-start | bytes 417800 | tf_op jit(solution)/shard_map/ppermute | solution.py:562
  22.4 35.3 %copy-start.8 = (bf16[2,272,128]{2,1,0:T(8,128)(2,1)}, bf16[2,272,128]{2,1,0:T(8,128)(2,1)S(1)}, u32[]{:S(2)}) copy-start(bf16[2,272,128]{2,1,0:T(8,128)(2,1)S(1)} %collective-permute-done.5.refs_2_) | copy-start | bytes 417796
  22.4 10.3 %collective-permute-start.10 = (bf16[2,272,128]{2,1,0:T(8,128)(2,1)S(1)}, bf16[2,272,128]{2,1,0:T(8,128)(2,1)S(1)}, u32[]{:S(2)}, u32[]{:S(2)}) collective-permute-start(bf16[2,272,128]{2,1,0:T(8,128)(2,1)S(1)} %get-tuple-element.44), channel_id=1, source_target_pairs={{0,26},{2,24},{8,18},{10,16},{16,10},{18,8},{24,2},{26,0},{1,27},{... | collective-permute-start | bytes 417800 | tf_op jit(solution)/shard_map/ppermute | solution.py:562
  23.9 33.8 %copy-start.9 = (bf16[2,272,128]{2,1,0:T(8,128)(2,1)}, bf16[2,272,128]{2,1,0:T(8,128)(2,1)S(1)}, u32[]{:S(2)}) copy-start(bf16[2,272,128]{2,1,0:T(8,128)(2,1)S(1)} %collective-permute-done.6.refs_3_) | copy-start | bytes 417796
  23.9 33.8 %copy-start.10 = (bf16[2,272,128]{2,1,0:T(8,128)(2,1)}, bf16[2,272,128]{2,1,0:T(8,128)(2,1)S(1)}, u32[]{:S(2)}) copy-start(bf16[2,272,128]{2,1,0:T(8,128)(2,1)S(1)} %collective-permute-done.7.refs_4_) | copy-start | bytes 417796
  28.8 28.9 %copy-start.11 = (bf16[2,272,128]{2,1,0:T(8,128)(2,1)}, bf16[2,272,128]{2,1,0:T(8,128)(2,1)S(1)}, u32[]{:S(2)}) copy-start(bf16[2,272,128]{2,1,0:T(8,128)(2,1)S(1)} %collective-permute-done.8.refs_5_) | copy-start | bytes 417796
  30.8 27.0 %copy-start.12 = (bf16[2,272,128]{2,1,0:T(8,128)(2,1)}, bf16[2,272,128]{2,1,0:T(8,128)(2,1)S(1)}, u32[]{:S(2)}) copy-start(bf16[2,272,128]{2,1,0:T(8,128)(2,1)S(1)} %collective-permute-done.9.refs_6_) | copy-start | bytes 417796
  32.7 25.0 %copy-start.13 = (bf16[2,272,128]{2,1,0:T(8,128)(2,1)}, bf16[2,272,128]{2,1,0:T(8,128)(2,1)S(1)}, u32[]{:S(2)}) copy-start(bf16[2,272,128]{2,1,0:T(8,128)(2,1)S(1)} %collective-permute-done.10.refs_7_) | copy-start | bytes 417796
  35.2 22.6 %all-to-all-start = ((bf16[16,272,128]{2,1,0:T(8,128)(2,1)}), bf16[16,272,128]{2,1,0:T(8,128)(2,1)S(1)}, u32[]{:S(2)}, u32[]{:S(2)}) async-start(bf16[16,272,128]{2,1,0:T(8,128)(2,1)} %get-tuple-element.62), calls=%async_computation | async-start | bytes 2228224 | tf_op jit(solution)/shard_map/all_to_all | solution.py:571
  57.8 1.0 %copy-start.6 = (bf16[16,272,128]{2,1,0:T(8,128)(2,1)}, bf16[16,272,128]{2,1,0:T(8,128)(2,1)S(1)}, u32[]{:S(2)}) copy-start(bf16[16,272,128]{2,1,0:T(8,128)(2,1)S(1)} %all-to-all-done.refs_8_) | copy-start | bytes 3342340
  58.8 17.0 %copy-start.5 = (s32[7]{0:T(128)S(1)}, s32[7]{0:T(128)}, u32[]{:S(2)}) copy-start(s32[7]{0:T(128)} %copy-done.4) | copy-start | bytes 88
  73.1 2.7 %collective-permute-start.11 = (bf16[4,864,128]{2,1,0:T(8,128)(2,1)}, bf16[4,864,128]{2,1,0:T(8,128)(2,1)S(1)}, u32[]{:S(2)}, u32[]{:S(2)}) collective-permute-start(bf16[4,864,128]{2,1,0:T(8,128)(2,1)} %get-tuple-element.64), channel_id=1, source_target_pairs={{0,1},{1,0},{2,3},{3,2},{4,5},{5,4},{6,7},{7,6},{8,9},{9,8},{10,11... | collective-permute-start | bytes 2654216 | tf_op jit(solution)/shard_map/ppermute | solution.py:535
  75.8 1.5 %copy-start = (f32[4,864,128]{2,1,0:T(8,128)S(1)}, f32[4,864,128]{2,1,0:T(8,128)}, u32[]{:S(2)}) copy-start(f32[4,864,128]{2,1,0:T(8,128)} %get-tuple-element.63.keep_ref) | copy-start | bytes 5308420
  78.0 11.8 %collective-permute-start.12 = (bf16[864,128]{1,0:T(8,128)(2,1)S(1)}, bf16[864,128]{1,0:T(8,128)(2,1)S(1)}, u32[]{:S(2)}, u32[]{:S(2)}) collective-permute-start(bf16[864,128]{1,0:T(8,128)(2,1)S(1)} %get-tuple-element.66), channel_id=1, source_target_pairs={{0,2},{2,0},{4,6},{6,4},{1,3},{3,1},{5,7},{7,5},{8,10},{10,8},{12,... | collective-permute-start | bytes 663560 | tf_op jit(solution)/shard_map/ppermute | solution.py:582
  79.9 18.7 %collective-permute-start.13 = (bf16[864,128]{1,0:T(8,128)(2,1)S(1)}, bf16[864,128]{1,0:T(8,128)(2,1)S(1)}, u32[]{:S(2)}, u32[]{:S(2)}) collective-permute-start(bf16[864,128]{1,0:T(8,128)(2,1)S(1)} %get-tuple-element.67), channel_id=1, source_target_pairs={{0,4},{2,6},{4,0},{6,2},{1,5},{3,7},{5,1},{7,3},{8,12},{10,14},{12... | collective-permute-start | bytes 663560 | tf_op jit(solution)/shard_map/ppermute | solution.py:582
  82.5 16.1 %collective-permute-start.14 = (bf16[864,128]{1,0:T(8,128)(2,1)S(1)}, bf16[864,128]{1,0:T(8,128)(2,1)S(1)}, u32[]{:S(2)}, u32[]{:S(2)}) collective-permute-start(bf16[864,128]{1,0:T(8,128)(2,1)S(1)} %get-tuple-element.68), channel_id=1, source_target_pairs={{0,6},{2,4},{4,2},{6,0},{1,7},{3,5},{5,3},{7,1},{8,14},{10,12},{12... | collective-permute-start | bytes 663560 | tf_op jit(solution)/shard_map/ppermute | solution.py:582

commit v3 on v2

v3 whole, which is shorter than its diff:
```python
import functools
import math

import jax
import jax.numpy as jnp
from jax import lax
from jax.experimental import pallas as pl
from jax.experimental.pallas import tpu as pltpu
from jax.sharding import Mesh, PartitionSpec as P

NT = (((1,), (1,)), ((), ()))
NN = (((1,), (0,)), ((), ()))


VMEM_SLACK = 4 << 20
VMEM_MOST = 56 << 20
PACK_MOST = 60 << 20
FAR_MOST = 50 << 20
FIRST_ROWS = 5


def whole(*shape):
    return pl.BlockSpec(shape, lambda *_: (0,) * len(shape))


def room(*arrays):
    return VMEM_SLACK + sum(math.prod(shape) * jnp.dtype(kind).itemsize for shape, kind in arrays)


def flip(rows_ref, unit, row):
    return lax.dot_general(
        unit, rows_ref[row], NT, preferred_element_type=jnp.float32
    ).astype(rows_ref.dtype)


def identity(width, kind):
    row_id = lax.broadcasted_iota(jnp.int32, (width, width), 0)
    col_id = lax.broadcasted_iota(jnp.int32, (width, width), 1)
    return jnp.where(row_id == col_id, 1.0, 0.0).astype(kind)


def pack_kernel(slots, parts, place_ref, facts_ref, p_in, out_ref, *refs):
    *pt_out, p_ref, pt_ref, sems = refs
    load = pltpu.make_async_copy(p_in, p_ref, sems.at[0])
    load.start()
    load.wait()
    rows, span, width = p_ref.shape
    base, half, low = place_ref[1], place_ref[3], place_ref[4]
    unit = identity(width, p_ref.dtype)
    for row in range(rows):
        pt_ref[row] = flip(p_ref, unit, row)
    saves = [pltpu.make_async_copy(pt_ref, one, sems.at[1]) for one in pt_out]
    for save in saves:
        save.start()
    tail = out_ref.shape[1] - slots * width
    lane = lax.broadcasted_iota(jnp.int32, (tail, span), 1)

    def fill(index, carry):
        device = (2 * (index // low) + half) * low + lax.rem(index, low)
        note = jnp.zeros((tail, span), jnp.int32)
        for slot in range(slots):
            row = jnp.maximum(facts_ref[slot, device], 0)
            out_ref[index, slot * width : (slot + 1) * width, :] = pt_ref[row]
            for part in range(parts):
                column = facts_ref[slots + part, row] - base
                note = jnp.where(lane == slot * parts + part, column, note)
        out_ref[index, slots * width :, :] = note.astype(jnp.float32).astype(out_ref.dtype)
        return carry

    lax.fori_loop(0, out_ref.shape[0], fill, 0)
    for save in saves:
        save.wait()


def pack(place, facts, p_rows, slots, parts, keep_flipped):
    rows, span, width = p_rows.shape
    vmem, smem = pl.BlockSpec(memory_space=pltpu.VMEM), pl.BlockSpec(memory_space=pltpu.SMEM)
    kind = p_rows.dtype
    outgoing = (facts.shape[1] // 2, slots * width + 16, span)
    flipped = (rows, width, span)
    hbm = pl.BlockSpec(memory_space=pltpu.HBM)
    kept = 1 if keep_flipped else 0
    return pl.pallas_call(
        functools.partial(pack_kernel, slots, parts),
        out_shape=(jax.ShapeDtypeStruct(outgoing, kind),)
        + (jax.ShapeDtypeStruct(flipped, kind),) * kept,
        in_specs=[smem, smem, hbm],
        out_specs=(vmem,) + (hbm,) * kept,
        scratch_shapes=[
            pltpu.VMEM(p_rows.shape, kind),
            pltpu.VMEM(flipped, kind),
            pltpu.SemaphoreType.DMA((2,)),
        ],
        compiler_params=pltpu.CompilerParams(
            vmem_limit_bytes=PACK_MOST if kept else room((outgoing, kind), *[(flipped, kind)] * 3)
        ),
        name="pack",
    )(place, facts, p_rows)


def distinct(columns, blocks, dump):
    columns, blocks = list(columns), list(blocks)
    for n in range(1, len(columns)):
        again = jnp.bool_(False)
        for before in range(n):
            same = columns[n] == columns[before]
            blocks[before] = blocks[before] + jnp.where(same, blocks[n], 0.0)
            again = again | same
        columns[n] = jnp.where(again, dump, columns[n])
    return columns, blocks


def sources(kind, place_ref, each, step):
    half, low = place_ref[3], place_ref[4]

    def spread(peer, which):
        group = peer // low
        return group, (2 * group + which) * low + lax.rem(peer, low)

    def along(index):
        return spread(index, half)

    def across(index):
        return spread(index, 1 - half)

    def both(index):
        peer = step * each + lax.rem(index, each)
        return spread(peer, jnp.bitwise_xor(half, index // each))

    return {"along": along, "across": across, "both": both}[kind]


def add_slots(
    source_of, pieces, far_ready, panel_ready, place_ref, where_ref, pcols_ref, slot_of_ref,
    far_ref, gathered, products, columns, columns_s, sem,
):
    parts, fine_rows = pcols_ref.shape
    width = far_ref.shape[1]
    small = width // parts
    own_rows = width // small
    base, group_span = place_ref[1], gathered.shape[0] * own_rows
    pattern = gathered.shape[1] // small - 1
    total = len(pieces)
    slots = products.shape[0] // total
    unlisted = slot_of_ref.shape[1] - 1
    for index, (ref, e) in enumerate(pieces):
        note = ref[e, slots * width :, :].astype(jnp.float32)[0:1, :]
        columns[index : index + 1, :] = note.astype(jnp.int32)
    tell = pltpu.make_async_copy(columns, columns_s, sem)
    tell.start()
    far_ready()
    for index, (ref, e) in enumerate(pieces):
        _, device = source_of(jnp.int32(index))
        for slot in range(slots):
            products[index * slots + slot] = lax.dot_general(
                ref[e, slot * width : (slot + 1) * width, :],
                far_ref[device * slots + slot],
                NT,
                preferred_element_type=jnp.float32,
            )
    tell.wait()
    panel_ready()
    lane_group = lax.broadcasted_iota(jnp.int32, (small, width), 1) // small

    def place_one(index, slot):
        group, device = source_of(index)
        start = group * group_span
        row = where_ref[device * slots + slot]
        idle = row >= fine_rows
        row = jnp.minimum(row, fine_rows - 1)
        wanted, blocks = distinct(
            [columns_s[index, slot * parts + n] + start for n in range(parts)],
            [products[index * slots + slot, n * small : (n + 1) * small, :] for n in range(parts)],
            unlisted,
        )
        for m in range(parts):
            target = pcols_ref[m, row] - base
            owner, within = target // own_rows, lax.rem(target, own_rows)
            shift = lax.rem(within + parts - m, parts) * small
            here = lane_group == within
            places = []
            for column in wanted:
                s = jnp.where(idle, pattern, slot_of_ref[target, column])
                places.append(pl.ds(pl.multiple_of(s * small, small), small))
            sums = [
                gathered[owner, at, :] + jnp.where(here, pltpu.roll(block, shift, 1), 0.0)
                for at, block in zip(places, blocks)
            ]
            for at, value in zip(places, sums):
                gathered[owner, at, :] = value

    def place_source(index, carry):
        for slot in range(slots):
            place_one(index, slot)
        return carry

    lax.fori_loop(0, total, place_source, 0, unroll=4)


def near_kernel(
    first_row, hops, place_ref, acols_ref, pcols_ref, ccols_ref, *refs
):
    resumed = hops > 0
    if resumed:
        where_in, slot_of_ref, pt_ref, a_ref, panel_in, far_in = refs[:6]
        came, refs = refs[6 : 6 + hops], refs[6 + hops :]
        panel_out, far_out, where_ref = refs[:3]
        dense, panel, far, weights, products, sems = refs[3:9]
        landed, far_products, notes, notes_s = refs[9:]
    else:
        ctable_ref, pt_ref, a_ref, panel_out, far_out, where_ref, slot_of_ref = refs[:7]
        dense, panel, far, weights, products, sems = refs[7:]
    step, steps = pl.program_id(0), pl.num_programs(0)
    fine_row = step + first_row
    parts, fine_rows = pcols_ref.shape
    block_cols, width = a_ref.shape[1], pt_ref.shape[1]
    span = width // parts
    pattern = ccols_ref.shape[1]
    slots = far_out.shape[0]
    own_rows = width // span
    base = place_ref[1]
    dump = dense.shape[0] // span - 1
    if resumed:
        load_panel = pltpu.make_async_copy(panel_in, panel, sems.at[0])
        load_far = pltpu.make_async_copy(far_in, far.at[pl.ds(0, slots)], sems.at[1])
        land = [
            pltpu.make_async_copy(one, landed.at[at], sems.at[2 + at]) for at, one in enumerate(came)
        ]

    @pl.when(step == 0)
    def _():
        if resumed:
            for one in [load_panel, load_far] + land:
                one.start()
        else:
            panel[...] = jnp.zeros_like(panel)
            far[...] = jnp.zeros_like(far)
            column = lax.broadcasted_iota(jnp.int32, slot_of_ref.shape, 1)
            found = jnp.full(slot_of_ref.shape, pattern, jnp.int32)
            for s in range(pattern):
                found = jnp.where(column == ctable_ref[:, s : s + 1], s, found)
            slot_of_ref[...] = found

        def begin(slot, carry):
            where_ref[slot] = where_in[slot] if resumed else fine_rows
            return carry

        lax.fori_loop(0, slots, begin, 0)

    dense[...] = jnp.zeros_like(dense)
    left = pt_ref[fine_row]
    for k in range(0, block_cols, 2):
        ahead = range(k, min(k + 2, block_cols))
        weighted = lax.dot_general(
            left,
            jnp.concatenate([a_ref[0, j] for j in ahead], axis=1),
            NN,
            preferred_element_type=jnp.float32,
        ).astype(far.dtype)
        for j in ahead:
            weights[j] = weighted[:, (j - k) * width : (j - k + 1) * width]
    for k in range(block_cols):
        source = acols_ref[fine_row, k]
        row = jnp.where(source >= fine_rows, 0, source)
        products[k] = lax.dot_general(
            pt_ref[row], weights[k], NT, preferred_element_type=jnp.float32
        )
    if resumed:

        @pl.when(step == 0)
        def _():
            load_panel.wait()
            load_far.wait()

    for k in range(block_cols):
        source = acols_ref[fine_row, k]
        is_far = source >= fine_rows
        slot = jnp.where(is_far, source - fine_rows, slots)
        far[slot] = weights[k]
        where_ref[slot] = fine_row
        row = jnp.where(is_far, 0, source)
        columns, blocks = distinct(
            [pcols_ref[n, row] for n in range(parts)],
            [products[k, n * span : (n + 1) * span, :] for n in range(parts)],
            dump,
        )
        places = [
            pl.ds(pl.multiple_of(jnp.where(is_far, dump, column) * span, span), span)
            for column in columns
        ]
        sums = [dense[at, :] + block for at, block in zip(places, blocks)]
        for at, value in zip(places, sums):
            dense[at, :] = value

    lane_group = lax.broadcasted_iota(jnp.int32, (span, width), 1) // span
    for m in range(parts):
        row = pcols_ref[m, fine_row] - base
        owner, within = row // own_rows, lax.rem(row, own_rows)
        shift = lax.rem(within + parts - m, parts) * span
        here = lane_group == within
        for first in range(0, pattern, 9):
            chunk = range(first, min(first + 9, pattern))
            sums = []
            for s in chunk:
                at = pl.ds(pl.multiple_of(ccols_ref[row, s] * span, span), span)
                moved = pltpu.roll(dense[at, :], shift, 1)
                sums.append(
                    panel[owner, s * span : (s + 1) * span, :] + jnp.where(here, moved, 0.0)
                )
            for s, value in zip(chunk, sums):
                panel[owner, s * span : (s + 1) * span, :] = value

    @pl.when(step == steps - 1)
    def _():
        if resumed:
            for one in land:
                one.wait()
            add_slots(
                sources("along", place_ref, 1, 0),
                [(landed.at[at], e) for at in range(hops) for e in range(landed.shape[1])],
                lambda: None, lambda: None, place_ref, where_ref, pcols_ref, slot_of_ref,
                far, panel, far_products, notes, notes_s, sems.at[0],
            )
        one = pltpu.make_async_copy(panel, panel_out, sems.at[0])
        two = pltpu.make_async_copy(far.at[pl.ds(0, slots)], far_out, sems.at[1])
        one.start()
        two.start()
        one.wait()
        two.wait()


def near(first_row, rows_here, place, a_cols, pcols_t, c_cols, pt, a_blocks, owners, all_cols, slots, before=None, came=()):
    rows, cols, span, _ = a_blocks.shape
    parts, width = pcols_t.shape[0], pt.shape[1]
    small = width // parts
    group_rows, pattern = c_cols.shape
    tall = (pattern + 1) * small
    hbm, smem = pl.BlockSpec(memory_space=pltpu.HBM), pl.BlockSpec(memory_space=pltpu.SMEM)
    out_shape = [
        jax.ShapeDtypeStruct((owners, tall, width), jnp.float32),
        jax.ShapeDtypeStruct((slots, width, span), jnp.bfloat16),
        jax.ShapeDtypeStruct((slots + 1,), jnp.int32),
    ]
    out_specs = [hbm, hbm, smem]
    in_specs = [
        whole(rows, width, span),
        pl.BlockSpec((1, cols, span, span), lambda i, *_: (i + first_row, 0, 0, 0)),
    ]
    scalars = [place, a_cols, pcols_t, c_cols]
    if before is None:
        in_specs.insert(0, whole(group_rows, pattern))
        operands = [c_cols, pt, a_blocks]
        out_shape.append(jax.ShapeDtypeStruct((group_rows, all_cols + 128), jnp.int32))
        out_specs.append(whole(group_rows, all_cols + 128))
    else:
        scalars += [before[2], before[3]]
        operands = [pt, a_blocks, before[0], before[1], *came]
        in_specs += [hbm, hbm] + [pl.BlockSpec(memory_space=pl.ANY)] * len(came)
    scratch = [
        (((all_cols + 1) * small, width), jnp.float32),
        ((owners, tall, width), jnp.float32),
        ((slots + 1, width, span), jnp.bfloat16),
        ((cols, width, span), jnp.bfloat16),
        ((cols, width, width), jnp.float32),
    ]
    smem_scratch = []
    if before is not None:
        total = len(came) * came[0].shape[0]
        scratch += [
            ((len(came), *came[0].shape), jnp.bfloat16),
            ((slots // 2, width, width), jnp.float32),
            ((total, span), jnp.int32),
        ]
        smem_scratch = [pltpu.SMEM((total, span), jnp.int32)]
    return pl.pallas_call(
        functools.partial(near_kernel, first_row, len(came)),
        out_shape=tuple(out_shape),
        grid_spec=pltpu.PrefetchScalarGridSpec(
            num_scalar_prefetch=len(scalars),
            grid=(rows_here,),
            in_specs=in_specs,
            out_specs=tuple(out_specs),
            scratch_shapes=[pltpu.VMEM(*one) for one in scratch[:5]]
            + [pltpu.SemaphoreType.DMA((2 + len(came),))]
            + [pltpu.VMEM(*one) for one in scratch[5:]]
            + smem_scratch,
        ),
        compiler_params=pltpu.CompilerParams(
            vmem_limit_bytes=VMEM_MOST
        ),
        cost_estimate=pl.CostEstimate(flops=int(1e11), bytes_accessed=int(1e8), transcendentals=0),
        name="near",
    )(*scalars, *operands)


def far_kernel(
    counts, steps, chips, place_ref, where_ref, pcols_ref, slot_of_ref, far_in, panel_in, *refs
):
    arrived, refs = refs[: len(counts)], refs[len(counts) :]
    waves = 2 if steps == 1 else 1
    outs, refs = refs[: 2 * waves], refs[2 * waves :]
    panel, far_ref, products, columns, columns_s, sems, *extra = refs
    hidden = bool(extra)
    gathered = extra[0] if hidden else panel
    step = 0 if steps == 1 else pl.program_id(0)
    tall = outs[0].shape[1]
    core, own_chip = place_ref[0], place_ref[2]
    load = pltpu.make_async_copy(panel_in, panel, sems.at[0])
    load_far = pltpu.make_async_copy(far_in, far_ref, sems.at[1])

    def at_start(action):
        action() if steps == 1 else pl.when(step == 0)(action)

    def begin():
        load_far.start()
        load.start()

    at_start(begin)
    if hidden:
        gathered[...] = jnp.zeros_like(gathered)
    add_slots(
        sources("across" if steps == 1 else "both", place_ref, counts[0], step),
        [(arrived[a], e) for a, count in enumerate(counts) for e in range(count)],
        lambda: at_start(load_far.wait),
        (lambda: None) if hidden else (lambda: at_start(load.wait)),
        place_ref, where_ref, pcols_ref, slot_of_ref, far_ref, gathered,
        products, columns, columns_s, sems.at[2],
    )

    def end():
        if hidden:
            load.wait()

        def take(owner):
            value = panel[owner, 0:tall, :]
            return value + gathered[owner, 0:tall, :] if hidden else value

        for at in range(chips):
            wave, spot = divmod(at, chips // waves)
            send_ref, keep_ref = outs[2 * wave], outs[2 * wave + 1]
            chip = at if waves == 1 else jnp.bitwise_xor(own_chip, chips - 1 - at)
            send_ref[spot] = take(2 * chip + 1 - core).astype(send_ref.dtype)
            keep_ref[spot] = take(2 * chip + core)

    end() if steps == 1 else pl.when(step == steps - 1)(end)


def add_far(place, where, pcols_t, slot_of, arrived, far, panel, chips):
    steps = 8 if len(arrived) == 2 else 1
    waves = 2 if steps == 1 else 1
    payload, span = arrived[0].shape[1:]
    counts = tuple(one.shape[0] // steps for one in arrived)
    width = far.shape[1]
    slot_count = (payload - 16) // width
    owners, padded, _ = panel.shape
    tall = padded - width // pcols_t.shape[0]
    hbm, smem = pl.BlockSpec(memory_space=pltpu.HBM), pl.BlockSpec(memory_space=pltpu.SMEM)
    some = (chips // waves, tall, width)
    outs = ((some, jnp.bfloat16), (some, jnp.float32)) * waves
    held = ((owners, padded, width), jnp.float32)
    scratch = [
        held,
        (far.shape, far.dtype),
        ((sum(counts) * slot_count, width, width), jnp.float32),
        ((sum(counts), span), jnp.int32),
    ]
    scratch_shapes = [pltpu.VMEM(*one) for one in scratch] + [
        pltpu.SMEM((sum(counts), span), jnp.int32),
        pltpu.SemaphoreType.DMA((3,)),
    ]
    if steps == 1:
        scratch_shapes.append(pltpu.VMEM(*held))
        vmem = pl.BlockSpec(memory_space=pltpu.VMEM)
        how = dict(
            in_specs=[smem] * 4 + [hbm, hbm] + [vmem] * len(arrived),
            out_specs=(vmem,) * len(outs),
            scratch_shapes=scratch_shapes,
        )
    else:
        how = dict(
            grid_spec=pltpu.PrefetchScalarGridSpec(
                num_scalar_prefetch=4,
                grid=(steps,),
                in_specs=[hbm, hbm]
                + [pl.BlockSpec((n, payload, span), lambda i, *_: (i, 0, 0)) for n in counts],
                out_specs=tuple(whole(*shape) for shape, _ in outs),
                scratch_shapes=scratch_shapes,
            )
        )
    return pl.pallas_call(
        functools.partial(far_kernel, counts, steps, chips),
        out_shape=tuple(jax.ShapeDtypeStruct(*one) for one in outs),
        compiler_params=pltpu.CompilerParams(vmem_limit_bytes=FAR_MOST if steps == 1 else VMEM_MOST),
        name="add_far",
        **how,
    )(place, where, pcols_t, slot_of, far, panel, *arrived)


def pair_kernel(keep_ref, got_ref, *out_refs):
    for at, out_ref in enumerate(out_refs):
        out_ref[...] = (keep_ref[at] + got_ref[at].astype(jnp.float32)).astype(out_ref.dtype)


def pair(keep, got, kinds):
    _, tall, width = keep.shape
    vmem = pl.BlockSpec(memory_space=pltpu.VMEM)
    return pl.pallas_call(
        pair_kernel,
        out_shape=tuple(jax.ShapeDtypeStruct((tall, width), kind) for kind in kinds),
        in_specs=[vmem, vmem],
        out_specs=(vmem,) * len(kinds),
        compiler_params=pltpu.CompilerParams(
            vmem_limit_bytes=room(
                (keep.shape, keep.dtype), (got.shape, got.dtype), *[((tall, width), jnp.float32)] * 2
            )
        ),
        name="pair",
    )(keep, got)


def last_kernel(mine_ref, *refs):
    terms, out_ref = refs[:-1], refs[-1]
    total = mine_ref[...]
    for term in terms:
        total = total + term[...].astype(jnp.float32)
    out_ref[...] = total.T.reshape(out_ref.shape)


def last(mine, terms, own_rows):
    tall, width = mine.shape
    vmem = pl.BlockSpec(memory_space=pltpu.VMEM)
    return pl.pallas_call(
        last_kernel,
        out_shape=jax.ShapeDtypeStruct((own_rows, width // own_rows, tall), jnp.float32),
        in_specs=[vmem] * (1 + len(terms)),
        out_specs=vmem,
        compiler_params=pltpu.CompilerParams(vmem_limit_bytes=room(*[(mine.shape, mine.dtype)] * (3 + len(terms)))),
        name="last",
    )(mine, *terms)


def swap(axis, *arrays):
    return [lax.ppermute(one, axis, [(0, 1), (1, 0)]) for one in arrays]


def local(chips, groups, a_blocks, a_cols, p_rows, p_cols, send_rows, c_cols):
    group_rows, parts = c_cols.shape[0], p_cols.shape[1]
    peers, slot_count = send_rows.shape[1:]
    slots = peers * slot_count
    group, half = lax.axis_index("group"), lax.axis_index("zh")
    chip = lax.axis_index(("zh", "zl"))
    low = lax.axis_index("zl")
    place = jnp.stack(
        [lax.axis_index("core"), group * group_rows, chip, half, jnp.int32(chips), group, low]
    ).astype(jnp.int32)
    wanted, pcols_t = send_rows[0].T, p_cols.T
    sizes = (2 * chips, group_rows * groups, slots)
    rows = a_blocks.shape[0]
    facts = jnp.concatenate(
        [wanted, jnp.pad(pcols_t, ((0, 0), (0, peers - pcols_t.shape[1])))], axis=0
    )
    over, facts_over = swap("zh", p_rows, facts)
    scatter = functools.partial(
        lax.all_to_all, axis_name=("group", "zl", "core"), split_axis=0, concat_axis=0, tiled=True
    )
    across = functools.partial(pack, place, slots=slot_count, parts=parts)
    shared = (place, a_cols, pcols_t, c_cols)
    outgoing, pt = across(facts, p_rows, keep_flipped=True)
    came = [scatter(outgoing)]
    if chips == 4:
        before = near(0, FIRST_ROWS, *shared, pt, a_blocks, *sizes)
        over, facts_over, before = lax.optimization_barrier((over, facts_over, before))
        outgoing, = across(facts_over, over, keep_flipped=False)
        outgoing, before = lax.optimization_barrier((outgoing, before))
        arrived = [scatter(outgoing)]
        panel, far, where = near(
            FIRST_ROWS, rows - FIRST_ROWS, *shared, pt, a_blocks, *sizes, before, came
        )
        slot_of = before[3]
    else:
        arrived = came + [scatter(across(facts_over, over, keep_flipped=False)[0])]
        panel, far, where, slot_of = near(0, rows, *shared, pt, a_blocks, *sizes)
    sums = add_far(place, where, pcols_t, slot_of, arrived, far, panel, chips)
    own_rows = group_rows // (2 * chips)
    line = ("zh", "zl")
    if chips == 4:
        give, keep, give_late, keep_late = sums
        got, = swap("core", give)
        out = pair(keep, got, (jnp.bfloat16,) * 2)
        give_late, keep_late, *out = lax.optimization_barrier((give_late, keep_late, *out))
        got_late, = swap("core", give_late)
        out_late, mine = pair(keep_late, got_late, (jnp.bfloat16, jnp.float32))
        terms = [
            lax.ppermute(piece, line, [(q, q ^ off) for q in range(chips)])
            for off, piece in zip((3, 2, 1), [*out, out_late])
        ]
        return last(mine, terms, own_rows)
    give, keep = sums
    got, = swap("core", give)
    both = keep + got.astype(jnp.float32)
    mine = lax.dynamic_index_in_dim(both, chip, 0, keepdims=False)
    came = lax.all_to_all(
        both.astype(jnp.bfloat16), line, split_axis=0, concat_axis=0, tiled=True
    ).astype(jnp.float32)
    other = jnp.arange(chips)[:, None, None] != chip
    return last(mine + jnp.sum(jnp.where(other, came, 0.0), 0), [], own_rows)


def solution(mesh):
    groups, ranks = mesh.shape["group"], mesh.shape["rank"]
    chips = ranks // 2
    every = ("group", "zh", "zl", "core")
    fine = Mesh(mesh.devices.reshape(groups, 2, chips // 2, 2), every)
    in_specs = (P(every), P(every), P(every), P(every), P(every), P("group"))
    return jax.shard_map(
        functools.partial(local, chips, groups),
        mesh=fine,
        in_specs=in_specs,
        out_specs=P(every),
        check_vma=False,
    )
```

time: 101 us -> 91 us (0.901)
  waiting for transfers between devices: 32.6 us -> 22.6 us
  Pallas kernels: 38.3 us -> 47.5 us
  local copies, waits for them, and re-layouts: 6.46 us -> 1.24 us
  starting transfers between devices: 22 us -> 18.1 us
    ppermute x10 -> x3, starting transfers between devices: 13.4 us -> 4.45 us  [local(): lax.ppermute(piece, line, [(q, q ^ off) for q in range(chips)])]
    ppermute x10 -> x3, waiting for transfers between devices: 25.6 us -> 18.5 us  [local(): lax.ppermute(piece, line, [(q, q ^ off) for q in range(chips)])]
    ppermute x5 -> x4, waiting for transfers between devices: 6.98 us -> 1.52 us  [swap(): return [lax.ppermute(one, axis, [(0, 1), (1, 0)]) for one in arrays]]
    pallas_call x4 -> x5, Pallas kernels: 34.9 us -> 40.3 us  [the longest x2 32.5 us: near(): pl.pallas_call(functools.partial(near_kernel, first_row, len(came)), out_...]
    all_to_all x1 -> x2, starting transfers between devices: 3.7 us -> 8.79 us  [the longest x1 5.1 us: local(): came = [scatter(outgoing)]]
    unnamed x28 -> x14, local copies, waits for them, and re-layouts: 4.85 us -> 0.64 us
    pallas_call x1 -> x2, Pallas kernels: 2.42 us -> 6.24 us  [pack(): pl.pallas_call(functools.partial(pack_kernel, slots, parts), out_shape=(j...]
    all_to_all x1 -> x2, waiting for transfers between devices: 0.01 us -> 2.56 us  [the longest x1 2.56 us: local(): came = [scatter(outgoing)]]
  transfers between devices with their start and end apart: 16 -> 9, of which waited for: 10 -> 4; matrix products, arithmetic and copies ran while one was open for 2% -> 1% of each run, Pallas kernels for 20% -> 43%
where the time goes in v3:
time: 91 us; the launch traced here: 90.3 us
  Pallas kernels  47.5 us (52%)
  waiting for transfers between devices  22.6 us (25%)
  starting transfers between devices  18.1 us (20%)
  local copies, waits for them, and re-layouts  1.24 us (1%)
    pallas_call x2, Pallas kernels, near(): pl.pallas_call(functools.partial(near_kernel, first_row, len(came)), out_...  32.5 us
    ppermute x3, waiting for transfers between devices, local(): lax.ppermute(piece, line, [(q, q ^ off) for q in range(chips)])  18.5 us
    pallas_call x1, Pallas kernels, add_far(): pl.pallas_call(functools.partial(far_kernel, counts, steps, chips), out_s...  7.72 us
    pallas_call x2, Pallas kernels, pack(): pl.pallas_call(functools.partial(pack_kernel, slots, parts), out_shape=(j...  6.24 us
    all_to_all x1, starting transfers between devices, local(): came = [scatter(outgoing)]  5.1 us
    ppermute x4, starting transfers between devices, swap(): return [lax.ppermute(one, axis, [(0, 1), (1, 0)]) for one in arrays]  4.88 us
    ppermute x3, starting transfers between devices, local(): lax.ppermute(piece, line, [(q, q ^ off) for q in range(chips)])  4.45 us
    all_to_all x1, starting transfers between devices, local(): arrived = [scatter(outgoing)]  3.7 us
  transfers between devices with their start and end apart: 9, of which 4 were waited for; matrix products, arithmetic and copies ran while one was open for 1% of the time, Pallas kernels for 43%

profile of v3, /device:TPU:0, one launch (start us, length us, event | category | flops | bytes accessed | tf_op | source)
XLA Modules:
  0.0 90.3 jit_solution(14395459259912308872)
XLA Ops:
  0.0 0.7 pad_add_fusion.facts_ref
  0.7 0.0 copy-start.6
  0.7 4.1 %collective-permute-start.1 = (s32[6,32]{1,0:T(8,128)S(1)}, s32[6,32]{1,0:T(8,128)S(1)}, u32[]{:S(2)}, u32[]{:S(2)}) collective-permute-start(s32[6,32]{1,0:T(8,128)S(1)} %pad_add_fusion.facts_ref), channel_id=1, source_target_pairs={{0,4},{4,0},{1,5},{5,1},{2,6},{6,2},{3,7},{7,3},{8,12},{12,8},{9,1... | collective-permute-start | bytes 2312 | tf_op jit(solution)/shard_map/ppermute | solution.py:543
  4.8 0.1 collective-permute-start
  4.9 0.6 stack.27.place_ref
  5.5 0.0 copy-done.6
  5.5 3.7 %pack.2 = (bf16[16,272,128]{2,1,0:T(8,128)(2,1)}, bf16[8,128,128]{2,1,0:T(8,128)(2,1)}) custom-call(s32[7]{0:T(128)} %stack.27.place_ref, s32[6,32]{1,0:T(8,128)} %copy-done.6, bf16[8,128,128]{2,1,0:T(8,128)(2,1)} %p_in.1), custom_call_target="tpu_custom_call" | custom-call | tf_op jit(solution)/shard_map/pack/pallas_call | solution.py:83
  9.2 5.1 %all-to-all-start = ((bf16[16,272,128]{2,1,0:T(8,128)(2,1)}), bf16[16,272,128]{2,1,0:T(8,128)(2,1)S(1)}, u32[]{:S(2)}, u32[]{:S(2)}) async-start(bf16[16,272,128]{2,1,0:T(8,128)(2,1)} %get-tuple-element.52), calls=%async_computation | async-start | bytes 2228224 | tf_op jit(solution)/shard_map/all_to_all | solution.py:569
  14.3 0.0 copy-start.1
  14.3 14.1 %near.2 = (f32[8,896,128]{2,1,0:T(8,128)}, bf16[64,128,128]{2,1,0:T(8,128)(2,1)}, s32[65]{0:T(128)}, s32[32,256]{1,0:T(8,128)}) custom-call(s32[7]{0:T(128)} %stack.27.place_ref, s32[8,22]{1,0:T(8,128)} %acols_ref.3, s32[4,8]{1,0:T(4,128)} %bitcast.11, s32[32,27]{1,0:T(8,128)} %ccols_ref.3, s32[32,27]{1,0:T(8,128)} %ccols_ref.3, ...), custom_call_target="tpu_custom_call" | custom-call | flops 99999997952 | bytes 100000000 | tf_op jit(solution)/shard_map/near/pallas_call | solution.py:375
  28.4 0.0 collective-permute-done.1.facts_ref
  28.4 0.0 collective-permute-done.p_in
  28.5 0.0 copy-done.1
  28.5 2.5 %pack.3 = bf16[16,272,128]{2,1,0:T(8,128)(2,1)} custom-call(s32[7]{0:T(128)S(1)} %copy-done.1, s32[6,32]{1,0:T(8,128)S(1)} %collective-permute-done.1.facts_ref, bf16[8,128,128]{2,1,0:T(8,128)(2,1)S(1)} %collective-permute-done.p_in), custom_call_target="tpu_custom_call" | custom-call | tf_op jit(solution)/shard_map/pack/pallas_call | solution.py:83
  31.0 2.6 %all-to-all-done.refs_6_ = bf16[16,272,128]{2,1,0:T(8,128)(2,1)S(1)} async-done(((bf16[16,272,128]{2,1,0:T(8,128)(2,1)}), bf16[16,272,128]{2,1,0:T(8,128)(2,1)S(1)}, u32[]{:S(2)}, u32[]{:S(2)}) %all-to-all-start) | async-done | bytes 1114144 | tf_op jit(solution)/shard_map/all_to_all | solution.py:569
  33.6 0.0 copy-start.5
  33.6 3.7 %all-to-all-start.1 = ((bf16[16,272,128]{2,1,0:T(8,128)(2,1)}), bf16[16,272,128]{2,1,0:T(8,128)(2,1)S(1)}, u32[]{:S(2)}, u32[]{:S(2)}) async-start(bf16[16,272,128]{2,1,0:T(8,128)(2,1)} %pack.3), calls=%async_computation.1 | async-start | bytes 2228224 | tf_op jit(solution)/shard_map/all_to_all | solution.py:575
  37.3 0.0 copy-done.5
  37.3 0.0 copy-start
  37.3 0.0 copy-start.2
  37.3 0.0 copy-start.3
  37.3 18.4 %near.3 = (f32[8,896,128]{2,1,0:T(8,128)}, bf16[64,128,128]{2,1,0:T(8,128)(2,1)}, s32[65]{0:T(128)}) custom-call(s32[7]{0:T(128)} %stack.27.place_ref, s32[8,22]{1,0:T(8,128)} %acols_ref.3, s32[4,8]{1,0:T(4,128)} %bitcast.12, s32[32,27]{1,0:T(8,128)} %ccols_ref.3, s32[65]{0:T(128)} %get-tuple-element.48.refs_0_, ...), custom_call_target="tpu_custom_call" | custom-call | flops 99999997952 | bytes 100000000 | tf_op jit(solution)/shard_map/near/pallas_call | solution.py:375
  55.7 0.0 all-to-all-done.1.refs_0_
  55.7 0.0 copy-done
  55.7 0.0 copy-done.2
  55.7 0.0 copy-done.3
  55.7 0.0 copy-start.4
  55.7 0.6 copy-done.4
  56.3 7.7 %add_far.1 = (bf16[2,864,128]{2,1,0:T(8,128)(2,1)S(1)}, f32[2,864,128]{2,1,0:T(8,128)S(1)}, bf16[2,864,128]{2,1,0:T(8,128)(2,1)S(1)}, f32[2,864,128]{2,1,0:T(8,128)S(1)}) custom-call(s32[7]{0:T(128)S(1)} %copy-done.2, s32[65]{0:T(128)S(1)} %copy-done.4, s32[4,8]{1,0:T(4,128)S(1)} %bitcast.13, s32[32,256]{1,0:T(8,128)S(1)} %copy-done, ...), custom_call_target="tpu_custom_call" | custom-call | tf_op jit(solution)/shard_map/add_far/pallas_call | solution.py:490
  64.1 0.3 collective-permute-start.2
  64.4 1.5 %collective-permute-done.2.got_ref = bf16[2,864,128]{2,1,0:T(8,128)(2,1)S(1)} collective-permute-done((bf16[2,864,128]{2,1,0:T(8,128)(2,1)S(1)}, bf16[2,864,128]{2,1,0:T(8,128)(2,1)S(1)}, u32[]{:S(2)}, u32[]{:S(2)}) %collective-permute-start.2) | collective-permute-done | bytes 442400 | tf_op jit(solution)/shard_map/ppermute | solution.py:543
  65.9 0.1 pair.2
  66.0 0.3 collective-permute-start.3
  66.3 2.7 %collective-permute-start.4 = (bf16[864,128]{1,0:T(8,128)(2,1)S(1)}, bf16[864,128]{1,0:T(8,128)(2,1)S(1)}, u32[]{:S(2)}, u32[]{:S(2)}) collective-permute-start(bf16[864,128]{1,0:T(8,128)(2,1)S(1)} %get-tuple-element.66), channel_id=1, source_target_pairs={{0,6},{2,4},{4,2},{6,0},{1,7},{3,5},{5,3},{7,1},{8,14},{10,12},{12... | collective-permute-start | bytes 663560 | tf_op jit(solution)/shard_map/ppermute | solution.py:594
  69.1 0.4 collective-permute-start.5
  69.5 0.0 collective-permute-done.3.got_ref
  69.5 0.1 pair.3
  69.6 1.3 %collective-permute-start.6 = (bf16[864,128]{1,0:T(8,128)(2,1)S(1)}, bf16[864,128]{1,0:T(8,128)(2,1)S(1)}, u32[]{:S(2)}, u32[]{:S(2)}) collective-permute-start(bf16[864,128]{1,0:T(8,128)(2,1)S(1)} %get-tuple-element.68), channel_id=1, source_target_pairs={{0,2},{2,0},{4,6},{6,4},{1,3},{3,1},{5,7},{7,5},{8,10},{10,8},{12,... | collective-permute-start | bytes 663560 | tf_op jit(solution)/shard_map/ppermute | solution.py:594
  70.9 5.7 %collective-permute-done.4.refs_0_ = bf16[864,128]{1,0:T(8,128)(2,1)S(1)} collective-permute-done((bf16[864,128]{1,0:T(8,128)(2,1)S(1)}, bf16[864,128]{1,0:T(8,128)(2,1)S(1)}, u32[]{:S(2)}, u32[]{:S(2)}) %collective-permute-start.4) | collective-permute-done | bytes 221216 | tf_op jit(solution)/shard_map/ppermute | solution.py:594
  76.5 12.8 %collective-permute-done.5.refs_1_ = bf16[864,128]{1,0:T(8,128)(2,1)S(1)} collective-permute-done((bf16[864,128]{1,0:T(8,128)(2,1)S(1)}, bf16[864,128]{1,0:T(8,128)(2,1)S(1)}, u32[]{:S(2)}, u32[]{:S(2)}) %collective-permute-start.5) | collective-permute-done | bytes 221216 | tf_op jit(solution)/shard_map/ppermute | solution.py:594
  89.4 0.0 collective-permute-done.6.refs_2_
  89.4 1.0 %last.1 = f32[4,32,864]{2,1,0:T(8,128)} custom-call(f32[864,128]{1,0:T(8,128)S(1)} %get-tuple-element.65.mine_ref, bf16[864,128]{1,0:T(8,128)(2,1)S(1)} %collective-permute-done.4.refs_0_, bf16[864,128]{1,0:T(8,128)(2,1)S(1)} %collective-permute-done.5.refs_1_, bf16[864,128]{1,0:T(8,128)(2,1)S(1)} %collective-permute-done.6.refs_2_), custom_call_target="tpu_custom_call" | custom-call | tf_op jit(solution)/shard_map/last/pallas_call | solution.py:532
Async XLA Ops:
  0.7 4.8 %copy-start.6 = (s32[6,32]{1,0:T(8,128)}, s32[6,32]{1,0:T(8,128)S(1)}, u32[]{:S(2)}) copy-start(s32[6,32]{1,0:T(8,128)S(1)} %pad_add_fusion.facts_ref) | copy-start | bytes 2308
  0.7 27.7 %collective-permute-start.1 = (s32[6,32]{1,0:T(8,128)S(1)}, s32[6,32]{1,0:T(8,128)S(1)}, u32[]{:S(2)}, u32[]{:S(2)}) collective-permute-start(s32[6,32]{1,0:T(8,128)S(1)} %pad_add_fusion.facts_ref), channel_id=1, source_target_pairs={{0,4},{4,0},{1,5},{5,1},{2,6},{6,2},{3,7},{7,3},{8,12},{12,8},{9,1... | collective-permute-start | bytes 2312 | tf_op jit(solution)/shard_map/ppermute | solution.py:543
  4.8 23.6 %collective-permute-start = (bf16[8,128,128]{2,1,0:T(8,128)(2,1)}, bf16[8,128,128]{2,1,0:T(8,128)(2,1)S(1)}, u32[]{:S(2)}, u32[]{:S(2)}) collective-permute-start(bf16[8,128,128]{2,1,0:T(8,128)(2,1)} %p_in.1), channel_id=1, source_target_pairs={{0,4},{4,0},{1,5},{5,1},{2,6},{6,2},{3,7},{7,3},{8,12},{12,8},{9,1... | collective-permute-start | bytes 786440 | tf_op jit(solution)/shard_map/ppermute | solution.py:543
  9.2 24.3 %all-to-all-start = ((bf16[16,272,128]{2,1,0:T(8,128)(2,1)}), bf16[16,272,128]{2,1,0:T(8,128)(2,1)S(1)}, u32[]{:S(2)}, u32[]{:S(2)}) async-start(bf16[16,272,128]{2,1,0:T(8,128)(2,1)} %get-tuple-element.52), calls=%async_computation | async-start | bytes 2228224 | tf_op jit(solution)/shard_map/all_to_all | solution.py:569
  14.3 14.1 %copy-start.1 = (s32[7]{0:T(128)S(1)}, s32[7]{0:T(128)}, u32[]{:S(2)}) copy-start(s32[7]{0:T(128)} %stack.27.place_ref) | copy-start | bytes 88
  33.6 3.7 %copy-start.5 = (bf16[16,272,128]{2,1,0:T(8,128)(2,1)}, bf16[16,272,128]{2,1,0:T(8,128)(2,1)S(1)}, u32[]{:S(2)}) copy-start(bf16[16,272,128]{2,1,0:T(8,128)(2,1)S(1)} %all-to-all-done.refs_6_) | copy-start | bytes 3342340
  33.6 22.1 %all-to-all-start.1 = ((bf16[16,272,128]{2,1,0:T(8,128)(2,1)}), bf16[16,272,128]{2,1,0:T(8,128)(2,1)S(1)}, u32[]{:S(2)}, u32[]{:S(2)}) async-start(bf16[16,272,128]{2,1,0:T(8,128)(2,1)} %pack.3), calls=%async_computation.1 | async-start | bytes 2228224 | tf_op jit(solution)/shard_map/all_to_all | solution.py:575
  37.3 18.4 %copy-start = (s32[32,256]{1,0:T(8,128)S(1)}, s32[32,256]{1,0:T(8,128)}, u32[]{:S(2)}) copy-start(s32[32,256]{1,0:T(8,128)} %get-tuple-element.49.refs_1_.slot_of_ref) | copy-start | bytes 98308
  37.3 18.4 %copy-start.2 = (s32[7]{0:T(128)S(1)}, s32[7]{0:T(128)}, u32[]{:S(2)}) copy-start(s32[7]{0:T(128)} %stack.27.place_ref) | copy-start | bytes 88
  37.3 18.4 %copy-start.3 = (s32[8,4]{0,1:T(4,128)S(1)}, s32[8,4]{0,1:T(4,128)}, u32[]{:S(2)}) copy-start(s32[8,4]{0,1:T(4,128)} %param.9) | copy-start | bytes 388
  55.7 0.6 copy-start.4
  64.1 1.9 %collective-permute-start.2 = (bf16[2,864,128]{2,1,0:T(8,128)(2,1)S(1)}, bf16[2,864,128]{2,1,0:T(8,128)(2,1)S(1)}, u32[]{:S(2)}, u32[]{:S(2)}) collective-permute-start(bf16[2,864,128]{2,1,0:T(8,128)(2,1)S(1)} %get-tuple-element.60), channel_id=1, source_target_pairs={{0,1},{1,0},{2,3},{3,2},{4,5},{5,4},{6,7},{7,6},{8,9},{9,8},{10,11... | collective-permute-start | bytes 1327112 | tf_op jit(solution)/shard_map/ppermute | solution.py:543
  66.0 3.5 %collective-permute-start.3 = (bf16[2,864,128]{2,1,0:T(8,128)(2,1)S(1)}, bf16[2,864,128]{2,1,0:T(8,128)(2,1)S(1)}, u32[]{:S(2)}, u32[]{:S(2)}) collective-permute-start(bf16[2,864,128]{2,1,0:T(8,128)(2,1)S(1)} %get-tuple-element.64), channel_id=1, source_target_pairs={{0,1},{1,0},{2,3},{3,2},{4,5},{5,4},{6,7},{7,6},{8,9},{9,8},{10,11... | collective-permute-start | bytes 1327112 | tf_op jit(solution)/shard_map/ppermute | solution.py:543
  66.3 10.2 %collective-permute-start.4 = (bf16[864,128]{1,0:T(8,128)(2,1)S(1)}, bf16[864,128]{1,0:T(8,128)(2,1)S(1)}, u32[]{:S(2)}, u32[]{:S(2)}) collective-permute-start(bf16[864,128]{1,0:T(8,128)(2,1)S(1)} %get-tuple-element.66), channel_id=1, source_target_pairs={{0,6},{2,4},{4,2},{6,0},{1,7},{3,5},{5,3},{7,1},{8,14},{10,12},{12... | collective-permute-start | bytes 663560 | tf_op jit(solution)/shard_map/ppermute | solution.py:594
  69.1 20.3 %collective-permute-start.5 = (bf16[864,128]{1,0:T(8,128)(2,1)S(1)}, bf16[864,128]{1,0:T(8,128)(2,1)S(1)}, u32[]{:S(2)}, u32[]{:S(2)}) collective-permute-start(bf16[864,128]{1,0:T(8,128)(2,1)S(1)} %get-tuple-element.67), channel_id=1, source_target_pairs={{0,4},{2,6},{4,0},{6,2},{1,5},{3,7},{5,1},{7,3},{8,12},{10,14},{12... | collective-permute-start | bytes 663560 | tf_op jit(solution)/shard_map/ppermute | solution.py:594
  69.6 19.8 %collective-permute-start.6 = (bf16[864,128]{1,0:T(8,128)(2,1)S(1)}, bf16[864,128]{1,0:T(8,128)(2,1)S(1)}, u32[]{:S(2)}, u32[]{:S(2)}) collective-permute-start(bf16[864,128]{1,0:T(8,128)(2,1)S(1)} %get-tuple-element.68), channel_id=1, source_target_pairs={{0,2},{2,0},{4,6},{6,4},{1,3},{3,1},{5,7},{7,5},{8,10},{10,8},{12,... | collective-permute-start | bytes 663560 | tf_op jit(solution)/shard_map/ppermute | solution.py:594

commit v4 on v3

--- a/solution.py
+++ b/solution.py
@@ -16,7 +16,7 @@
 VMEM_MOST = 56 << 20
 PACK_MOST = 60 << 20
 FAR_MOST = 50 << 20
-FIRST_ROWS = 5
+FIRST_ROWS = 6
 
 
 def whole(*shape):
@@ -194,7 +194,7 @@
             place_one(index, slot)
         return carry
 
-    lax.fori_loop(0, total, place_source, 0, unroll=4)
+    lax.fori_loop(0, total, place_source, 0, unroll=16)
 
 
 def near_kernel(
@@ -394,25 +394,46 @@
 
 
 def far_kernel(
-    counts, steps, chips, place_ref, where_ref, pcols_ref, slot_of_ref, far_in, panel_in, *refs
+    counts, steps, chips, place_ref, where_in, pcols_ref, slot_of_ref, far_in, panel_in, *refs
 ):
     arrived, refs = refs[: len(counts)], refs[len(counts) :]
     waves = 2 if steps == 1 else 1
     outs, refs = refs[: 2 * waves], refs[2 * waves :]
     panel, far_ref, products, columns, columns_s, sems, *extra = refs
+    if steps == 1:
+        where_ref, *extra = extra
     hidden = bool(extra)
     gathered = extra[0] if hidden else panel
     step = 0 if steps == 1 else pl.program_id(0)
     tall = outs[0].shape[1]
     core, own_chip = place_ref[0], place_ref[2]
     load = pltpu.make_async_copy(panel_in, panel, sems.at[0])
-    load_far = pltpu.make_async_copy(far_in, far_ref, sems.at[1])
+    if steps == 1:
+        slots = products.shape[0] // counts[0]
+        group_count = counts[0] // chips
+        spans = [
+            pl.ds(pl.multiple_of((2 * group + 1 - place_ref[3]) * slots * chips, 8), slots * chips)
+            for group in range(group_count)
+        ]
+        loads = [
+            pltpu.make_async_copy(far_in.at[one], far_ref.at[one], sems.at[4 + at])
+            for at, one in enumerate(spans)
+        ]
+        loads.append(pltpu.make_async_copy(where_in, where_ref, sems.at[3]))
+    else:
+        where_ref = where_in
+        loads = [pltpu.make_async_copy(far_in, far_ref, sems.at[1])]
+
+    def far_ready():
+        for one in loads:
+            one.wait()
 
     def at_start(action):
         action() if steps == 1 else pl.when(step == 0)(action)
 
     def begin():
-        load_far.start()
+        for one in loads:
+            one.start()
         load.start()
 
     at_start(begin)
@@ -421,7 +442,7 @@
     add_slots(
         sources("across" if steps == 1 else "both", place_ref, counts[0], step),
         [(arrived[a], e) for a, count in enumerate(counts) for e in range(count)],
-        lambda: at_start(load_far.wait),
+        lambda: at_start(far_ready),
         (lambda: None) if hidden else (lambda: at_start(load.wait)),
         place_ref, where_ref, pcols_ref, slot_of_ref, far_ref, gathered,
         products, columns, columns_s, sems.at[2],
@@ -466,13 +487,13 @@
     ]
     scratch_shapes = [pltpu.VMEM(*one) for one in scratch] + [
         pltpu.SMEM((sum(counts), span), jnp.int32),
-        pltpu.SemaphoreType.DMA((3,)),
+        pltpu.SemaphoreType.DMA((8,)),
     ]
     if steps == 1:
-        scratch_shapes.append(pltpu.VMEM(*held))
+        scratch_shapes.append(pltpu.SMEM(where.shape, where.dtype))
         vmem = pl.BlockSpec(memory_space=pltpu.VMEM)
         how = dict(
-            in_specs=[smem] * 4 + [hbm, hbm] + [vmem] * len(arrived),
+            in_specs=[smem, hbm, smem, smem, hbm, hbm] + [vmem] * len(arrived),
             out_specs=(vmem,) * len(outs),
             scratch_shapes=scratch_shapes,
         )

time: 91 us -> 88.7 us (0.975)
  Pallas kernels: 47.5 us -> 46 us
    all_to_all x1, waiting for transfers between devices: 2.56 us -> 0.99 us  [local(): came = [scatter(outgoing)]]
  transfers between devices with their start and end apart: 9 -> 9, of which waited for: 4 -> 5; matrix products, arithmetic and copies ran while one was open for 1% -> 1% of each run, Pallas kernels for 43% -> 43%
where the time goes in v4:
time: 88.7 us; the launch traced here: 88.1 us
  Pallas kernels  46 us (52%)
  waiting for transfers between devices  21.8 us (25%)
  starting transfers between devices  18.2 us (21%)
  local copies, waits for them, and re-layouts  1.24 us (1%)
    pallas_call x2, Pallas kernels, near(): pl.pallas_call(functools.partial(near_kernel, first_row, len(came)), out_...  31.8 us
    ppermute x3, waiting for transfers between devices, local(): lax.ppermute(piece, line, [(q, q ^ off) for q in range(chips)])  18.2 us
    pallas_call x1, Pallas kernels, add_far(): pl.pallas_call(functools.partial(far_kernel, counts, steps, chips), out_s...  6.87 us
    pallas_call x2, Pallas kernels, pack(): pl.pallas_call(functools.partial(pack_kernel, slots, parts), out_shape=(j...  6.23 us
    all_to_all x1, starting transfers between devices, local(): came = [scatter(outgoing)]  5.12 us
    ppermute x3, starting transfers between devices, local(): lax.ppermute(piece, line, [(q, q ^ off) for q in range(chips)])  4.47 us
    ppermute x4, starting transfers between devices, swap(): return [lax.ppermute(one, axis, [(0, 1), (1, 0)]) for one in arrays]  4.45 us
    all_to_all x1, starting transfers between devices, local(): arrived = [scatter(outgoing)]  4.16 us
  transfers between devices with their start and end apart: 9, of which 5 were waited for; matrix products, arithmetic and copies ran while one was open for 1% of the time, Pallas kernels for 43%

profile of v4, /device:TPU:0, one launch (start us, length us, event | category | flops | bytes accessed | tf_op | source)
XLA Modules:
  0.0 88.1 jit_solution(17396459709112551546)
XLA Ops:
  0.0 0.7 pad_add_fusion.facts_ref
  0.7 0.0 copy-start.6
  0.7 4.1 %collective-permute-start.1 = (s32[6,32]{1,0:T(8,128)S(1)}, s32[6,32]{1,0:T(8,128)S(1)}, u32[]{:S(2)}, u32[]{:S(2)}) collective-permute-start(s32[6,32]{1,0:T(8,128)S(1)} %pad_add_fusion.facts_ref), channel_id=1, source_target_pairs={{0,4},{4,0},{1,5},{5,1},{2,6},{6,2},{3,7},{7,3},{8,12},{12,8},{9,1... | collective-permute-start | bytes 2312 | tf_op jit(solution)/shard_map/ppermute | solution.py:564
  4.8 0.1 collective-permute-start
  4.9 0.6 stack.27.place_ref
  5.5 0.0 copy-done.6
  5.5 3.7 %pack.2 = (bf16[16,272,128]{2,1,0:T(8,128)(2,1)}, bf16[8,128,128]{2,1,0:T(8,128)(2,1)}) custom-call(s32[7]{0:T(128)} %stack.27.place_ref, s32[6,32]{1,0:T(8,128)} %copy-done.6, bf16[8,128,128]{2,1,0:T(8,128)(2,1)} %p_in.1), custom_call_target="tpu_custom_call" | custom-call | tf_op jit(solution)/shard_map/pack/pallas_call | solution.py:83
  9.2 5.1 %all-to-all-start = ((bf16[16,272,128]{2,1,0:T(8,128)(2,1)}), bf16[16,272,128]{2,1,0:T(8,128)(2,1)S(1)}, u32[]{:S(2)}, u32[]{:S(2)}) async-start(bf16[16,272,128]{2,1,0:T(8,128)(2,1)} %get-tuple-element.52), calls=%async_computation | async-start | bytes 2228224 | tf_op jit(solution)/shard_map/all_to_all | solution.py:590
  14.3 0.0 copy-start.1
  14.3 15.7 %near.2 = (f32[8,896,128]{2,1,0:T(8,128)}, bf16[64,128,128]{2,1,0:T(8,128)(2,1)}, s32[65]{0:T(128)}, s32[32,256]{1,0:T(8,128)}) custom-call(s32[7]{0:T(128)} %stack.27.place_ref, s32[8,22]{1,0:T(8,128)} %acols_ref.3, s32[4,8]{1,0:T(4,128)} %bitcast.11, s32[32,27]{1,0:T(8,128)} %ccols_ref.3, s32[32,27]{1,0:T(8,128)} %ccols_ref.3, ...), custom_call_target="tpu_custom_call" | custom-call | flops 99999997952 | bytes 100000000 | tf_op jit(solution)/shard_map/near/pallas_call | solution.py:375
  30.0 0.0 collective-permute-done.1.facts_ref
  30.0 0.0 collective-permute-done.p_in
  30.0 0.0 copy-done.1
  30.1 2.5 %pack.3 = bf16[16,272,128]{2,1,0:T(8,128)(2,1)} custom-call(s32[7]{0:T(128)S(1)} %copy-done.1, s32[6,32]{1,0:T(8,128)S(1)} %collective-permute-done.1.facts_ref, bf16[8,128,128]{2,1,0:T(8,128)(2,1)S(1)} %collective-permute-done.p_in), custom_call_target="tpu_custom_call" | custom-call | tf_op jit(solution)/shard_map/pack/pallas_call | solution.py:83
  32.6 1.0 %all-to-all-done.refs_6_ = bf16[16,272,128]{2,1,0:T(8,128)(2,1)S(1)} async-done(((bf16[16,272,128]{2,1,0:T(8,128)(2,1)}), bf16[16,272,128]{2,1,0:T(8,128)(2,1)S(1)}, u32[]{:S(2)}, u32[]{:S(2)}) %all-to-all-start) | async-done | bytes 1114144 | tf_op jit(solution)/shard_map/all_to_all | solution.py:590
  33.6 0.0 copy-start.5
  33.6 4.2 %all-to-all-start.1 = ((bf16[16,272,128]{2,1,0:T(8,128)(2,1)}), bf16[16,272,128]{2,1,0:T(8,128)(2,1)S(1)}, u32[]{:S(2)}, u32[]{:S(2)}) async-start(bf16[16,272,128]{2,1,0:T(8,128)(2,1)} %pack.3), calls=%async_computation.1 | async-start | bytes 2228224 | tf_op jit(solution)/shard_map/all_to_all | solution.py:596
  37.7 0.0 copy-done.5
  37.7 0.0 copy-start
  37.8 0.0 copy-start.2
  37.8 0.0 copy-start.3
  37.8 16.1 %near.3 = (f32[8,896,128]{2,1,0:T(8,128)}, bf16[64,128,128]{2,1,0:T(8,128)(2,1)}, s32[65]{0:T(128)}) custom-call(s32[7]{0:T(128)} %stack.27.place_ref, s32[8,22]{1,0:T(8,128)} %acols_ref.3, s32[4,8]{1,0:T(4,128)} %bitcast.12, s32[32,27]{1,0:T(8,128)} %ccols_ref.3, s32[65]{0:T(128)} %get-tuple-element.48.refs_0_, ...), custom_call_target="tpu_custom_call" | custom-call | flops 99999997952 | bytes 100000000 | tf_op jit(solution)/shard_map/near/pallas_call | solution.py:375
  53.9 0.8 all-to-all-done.1.refs_0_
  54.6 0.0 copy-done
  54.6 0.0 copy-done.2
  54.6 0.0 copy-done.3
  54.7 0.0 copy-start.4
  54.7 0.6 copy-done.4
  55.3 6.9 %add_far.1 = (bf16[2,864,128]{2,1,0:T(8,128)(2,1)S(1)}, f32[2,864,128]{2,1,0:T(8,128)S(1)}, bf16[2,864,128]{2,1,0:T(8,128)(2,1)S(1)}, f32[2,864,128]{2,1,0:T(8,128)S(1)}) custom-call(s32[7]{0:T(128)S(1)} %copy-done.2, s32[65]{0:T(128)S(1)} %copy-done.4, s32[4,8]{1,0:T(4,128)S(1)} %bitcast.13, s32[32,256]{1,0:T(8,128)S(1)} %copy-done, ...), custom_call_target="tpu_custom_call" | custom-call | tf_op jit(solution)/shard_map/add_far/pallas_call | solution.py:511
  62.2 0.1 collective-permute-start.2
  62.2 1.8 %collective-permute-done.2.got_ref = bf16[2,864,128]{2,1,0:T(8,128)(2,1)S(1)} collective-permute-done((bf16[2,864,128]{2,1,0:T(8,128)(2,1)S(1)}, bf16[2,864,128]{2,1,0:T(8,128)(2,1)S(1)}, u32[]{:S(2)}, u32[]{:S(2)}) %collective-permute-start.2) | collective-permute-done | bytes 442400 | tf_op jit(solution)/shard_map/ppermute | solution.py:564
  64.0 0.1 pair.2
  64.1 0.2 collective-permute-start.3
  64.3 3.2 %collective-permute-start.4 = (bf16[864,128]{1,0:T(8,128)(2,1)S(1)}, bf16[864,128]{1,0:T(8,128)(2,1)S(1)}, u32[]{:S(2)}, u32[]{:S(2)}) collective-permute-start(bf16[864,128]{1,0:T(8,128)(2,1)S(1)} %get-tuple-element.66), channel_id=1, source_target_pairs={{0,6},{2,4},{4,2},{6,0},{1,7},{3,5},{5,3},{7,1},{8,14},{10,12},{12... | collective-permute-start | bytes 663560 | tf_op jit(solution)/shard_map/ppermute | solution.py:615
  67.5 0.0 collective-permute-start.5
  67.5 0.0 collective-permute-done.3.got_ref
  67.5 0.1 pair.3
  67.6 1.2 %collective-permute-start.6 = (bf16[864,128]{1,0:T(8,128)(2,1)S(1)}, bf16[864,128]{1,0:T(8,128)(2,1)S(1)}, u32[]{:S(2)}, u32[]{:S(2)}) collective-permute-start(bf16[864,128]{1,0:T(8,128)(2,1)S(1)} %get-tuple-element.68), channel_id=1, source_target_pairs={{0,2},{2,0},{4,6},{6,4},{1,3},{3,1},{5,7},{7,5},{8,10},{10,8},{12,... | collective-permute-start | bytes 663560 | tf_op jit(solution)/shard_map/ppermute | solution.py:615
  68.8 5.7 %collective-permute-done.4.refs_0_ = bf16[864,128]{1,0:T(8,128)(2,1)S(1)} collective-permute-done((bf16[864,128]{1,0:T(8,128)(2,1)S(1)}, bf16[864,128]{1,0:T(8,128)(2,1)S(1)}, u32[]{:S(2)}, u32[]{:S(2)}) %collective-permute-start.4) | collective-permute-done | bytes 221216 | tf_op jit(solution)/shard_map/ppermute | solution.py:615
  74.5 12.6 %collective-permute-done.5.refs_1_ = bf16[864,128]{1,0:T(8,128)(2,1)S(1)} collective-permute-done((bf16[864,128]{1,0:T(8,128)(2,1)S(1)}, bf16[864,128]{1,0:T(8,128)(2,1)S(1)}, u32[]{:S(2)}, u32[]{:S(2)}) %collective-permute-start.5) | collective-permute-done | bytes 221216 | tf_op jit(solution)/shard_map/ppermute | solution.py:615
  87.1 0.0 collective-permute-done.6.refs_2_
  87.1 1.0 %last.1 = f32[4,32,864]{2,1,0:T(8,128)} custom-call(f32[864,128]{1,0:T(8,128)S(1)} %get-tuple-element.65.mine_ref, bf16[864,128]{1,0:T(8,128)(2,1)S(1)} %collective-permute-done.4.refs_0_, bf16[864,128]{1,0:T(8,128)(2,1)S(1)} %collective-permute-done.5.refs_1_, bf16[864,128]{1,0:T(8,128)(2,1)S(1)} %collective-permute-done.6.refs_2_), custom_call_target="tpu_custom_call" | custom-call | tf_op jit(solution)/shard_map/last/pallas_call | solution.py:553
Async XLA Ops:
  0.7 4.8 %copy-start.6 = (s32[6,32]{1,0:T(8,128)}, s32[6,32]{1,0:T(8,128)S(1)}, u32[]{:S(2)}) copy-start(s32[6,32]{1,0:T(8,128)S(1)} %pad_add_fusion.facts_ref) | copy-start | bytes 2308
  0.7 29.3 %collective-permute-start.1 = (s32[6,32]{1,0:T(8,128)S(1)}, s32[6,32]{1,0:T(8,128)S(1)}, u32[]{:S(2)}, u32[]{:S(2)}) collective-permute-start(s32[6,32]{1,0:T(8,128)S(1)} %pad_add_fusion.facts_ref), channel_id=1, source_target_pairs={{0,4},{4,0},{1,5},{5,1},{2,6},{6,2},{3,7},{7,3},{8,12},{12,8},{9,1... | collective-permute-start | bytes 2312 | tf_op jit(solution)/shard_map/ppermute | solution.py:564
  4.8 25.2 %collective-permute-start = (bf16[8,128,128]{2,1,0:T(8,128)(2,1)}, bf16[8,128,128]{2,1,0:T(8,128)(2,1)S(1)}, u32[]{:S(2)}, u32[]{:S(2)}) collective-permute-start(bf16[8,128,128]{2,1,0:T(8,128)(2,1)} %p_in.1), channel_id=1, source_target_pairs={{0,4},{4,0},{1,5},{5,1},{2,6},{6,2},{3,7},{7,3},{8,12},{12,8},{9,1... | collective-permute-start | bytes 786440 | tf_op jit(solution)/shard_map/ppermute | solution.py:564
  9.2 24.4 %all-to-all-start = ((bf16[16,272,128]{2,1,0:T(8,128)(2,1)}), bf16[16,272,128]{2,1,0:T(8,128)(2,1)S(1)}, u32[]{:S(2)}, u32[]{:S(2)}) async-start(bf16[16,272,128]{2,1,0:T(8,128)(2,1)} %get-tuple-element.52), calls=%async_computation | async-start | bytes 2228224 | tf_op jit(solution)/shard_map/all_to_all | solution.py:590
  14.3 15.7 %copy-start.1 = (s32[7]{0:T(128)S(1)}, s32[7]{0:T(128)}, u32[]{:S(2)}) copy-start(s32[7]{0:T(128)} %stack.27.place_ref) | copy-start | bytes 88
  33.6 4.2 %copy-start.5 = (bf16[16,272,128]{2,1,0:T(8,128)(2,1)}, bf16[16,272,128]{2,1,0:T(8,128)(2,1)S(1)}, u32[]{:S(2)}) copy-start(bf16[16,272,128]{2,1,0:T(8,128)(2,1)S(1)} %all-to-all-done.refs_6_) | copy-start | bytes 3342340
  33.6 21.1 %all-to-all-start.1 = ((bf16[16,272,128]{2,1,0:T(8,128)(2,1)}), bf16[16,272,128]{2,1,0:T(8,128)(2,1)S(1)}, u32[]{:S(2)}, u32[]{:S(2)}) async-start(bf16[16,272,128]{2,1,0:T(8,128)(2,1)} %pack.3), calls=%async_computation.1 | async-start | bytes 2228224 | tf_op jit(solution)/shard_map/all_to_all | solution.py:596
  37.7 16.9 %copy-start = (s32[32,256]{1,0:T(8,128)S(1)}, s32[32,256]{1,0:T(8,128)}, u32[]{:S(2)}) copy-start(s32[32,256]{1,0:T(8,128)} %get-tuple-element.49.refs_1_.slot_of_ref) | copy-start | bytes 98308
  37.8 16.9 %copy-start.2 = (s32[7]{0:T(128)S(1)}, s32[7]{0:T(128)}, u32[]{:S(2)}) copy-start(s32[7]{0:T(128)} %stack.27.place_ref) | copy-start | bytes 88
  37.8 16.9 %copy-start.3 = (s32[8,4]{0,1:T(4,128)S(1)}, s32[8,4]{0,1:T(4,128)}, u32[]{:S(2)}) copy-start(s32[8,4]{0,1:T(4,128)} %param.9) | copy-start | bytes 388
  54.7 0.6 copy-start.4
  62.2 1.9 %collective-permute-start.2 = (bf16[2,864,128]{2,1,0:T(8,128)(2,1)S(1)}, bf16[2,864,128]{2,1,0:T(8,128)(2,1)S(1)}, u32[]{:S(2)}, u32[]{:S(2)}) collective-permute-start(bf16[2,864,128]{2,1,0:T(8,128)(2,1)S(1)} %get-tuple-element.60), channel_id=1, source_target_pairs={{0,1},{1,0},{2,3},{3,2},{4,5},{5,4},{6,7},{7,6},{8,9},{9,8},{10,11... | collective-permute-start | bytes 1327112 | tf_op jit(solution)/shard_map/ppermute | solution.py:564
  64.1 3.4 %collective-permute-start.3 = (bf16[2,864,128]{2,1,0:T(8,128)(2,1)S(1)}, bf16[2,864,128]{2,1,0:T(8,128)(2,1)S(1)}, u32[]{:S(2)}, u32[]{:S(2)}) collective-permute-start(bf16[2,864,128]{2,1,0:T(8,128)(2,1)S(1)} %get-tuple-element.64), channel_id=1, source_target_pairs={{0,1},{1,0},{2,3},{3,2},{4,5},{5,4},{6,7},{7,6},{8,9},{9,8},{10,11... | collective-permute-start | bytes 1327112 | tf_op jit(solution)/shard_map/ppermute | solution.py:564
  64.3 10.2 %collective-permute-start.4 = (bf16[864,128]{1,0:T(8,128)(2,1)S(1)}, bf16[864,128]{1,0:T(8,128)(2,1)S(1)}, u32[]{:S(2)}, u32[]{:S(2)}) collective-permute-start(bf16[864,128]{1,0:T(8,128)(2,1)S(1)} %get-tuple-element.66), channel_id=1, source_target_pairs={{0,6},{2,4},{4,2},{6,0},{1,7},{3,5},{5,3},{7,1},{8,14},{10,12},{12... | collective-permute-start | bytes 663560 | tf_op jit(solution)/shard_map/ppermute | solution.py:615
  67.5 19.6 %collective-permute-start.5 = (bf16[864,128]{1,0:T(8,128)(2,1)S(1)}, bf16[864,128]{1,0:T(8,128)(2,1)S(1)}, u32[]{:S(2)}, u32[]{:S(2)}) collective-permute-start(bf16[864,128]{1,0:T(8,128)(2,1)S(1)} %get-tuple-element.67), channel_id=1, source_target_pairs={{0,4},{2,6},{4,0},{6,2},{1,5},{3,7},{5,1},{7,3},{8,12},{10,14},{12... | collective-permute-start | bytes 663560 | tf_op jit(solution)/shard_map/ppermute | solution.py:615
  67.6 19.5 %collective-permute-start.6 = (bf16[864,128]{1,0:T(8,128)(2,1)S(1)}, bf16[864,128]{1,0:T(8,128)(2,1)S(1)}, u32[]{:S(2)}, u32[]{:S(2)}) collective-permute-start(bf16[864,128]{1,0:T(8,128)(2,1)S(1)} %get-tuple-element.68), channel_id=1, source_target_pairs={{0,2},{2,0},{4,6},{6,4},{1,3},{3,1},{5,7},{7,5},{8,10},{10,8},{12,... | collective-permute-start | bytes 663560 | tf_op jit(solution)/shard_map/ppermute | solution.py:615

commit v5 on v4

--- a/solution.py
+++ b/solution.py
@@ -394,14 +394,14 @@
 
 
 def far_kernel(
-    counts, steps, chips, place_ref, where_in, pcols_ref, slot_of_ref, far_in, panel_in, *refs
+    counts, steps, chips, place_ref, where_in, pcols_ref, slot_of_in, far_in, panel_in, *refs
 ):
     arrived, refs = refs[: len(counts)], refs[len(counts) :]
     waves = 2 if steps == 1 else 1
     outs, refs = refs[: 2 * waves], refs[2 * waves :]
     panel, far_ref, products, columns, columns_s, sems, *extra = refs
     if steps == 1:
-        where_ref, *extra = extra
+        where_ref, slot_of_ref, *extra = extra
     hidden = bool(extra)
     gathered = extra[0] if hidden else panel
     step = 0 if steps == 1 else pl.program_id(0)
@@ -420,8 +420,9 @@
             for at, one in enumerate(spans)
         ]
         loads.append(pltpu.make_async_copy(where_in, where_ref, sems.at[3]))
+        loads.append(pltpu.make_async_copy(slot_of_in, slot_of_ref, sems.at[1]))
     else:
-        where_ref = where_in
+        where_ref, slot_of_ref = where_in, slot_of_in
         loads = [pltpu.make_async_copy(far_in, far_ref, sems.at[1])]
 
     def far_ready():
@@ -491,9 +492,10 @@
     ]
     if steps == 1:
         scratch_shapes.append(pltpu.SMEM(where.shape, where.dtype))
+        scratch_shapes.append(pltpu.SMEM(slot_of.shape, slot_of.dtype))
         vmem = pl.BlockSpec(memory_space=pltpu.VMEM)
         how = dict(
-            in_specs=[smem, hbm, smem, smem, hbm, hbm] + [vmem] * len(arrived),
+            in_specs=[smem, hbm, smem, hbm, hbm, hbm] + [vmem] * len(arrived),
             out_specs=(vmem,) * len(outs),
             scratch_shapes=scratch_shapes,
         )

time: 88.7 us -> 88.2 us (level)
  no operation moved by 1% of the time
where the time goes in v5:
time: 88.2 us; the launch traced here: 87.6 us
  Pallas kernels  45.5 us (52%)
  waiting for transfers between devices  21.8 us (25%)
  starting transfers between devices  18.2 us (21%)
  local copies, waits for them, and re-layouts  1.24 us (1%)
    pallas_call x2, Pallas kernels, near(): pl.pallas_call(functools.partial(near_kernel, first_row, len(came)), out_...  31.8 us
    ppermute x3, waiting for transfers between devices, local(): lax.ppermute(piece, line, [(q, q ^ off) for q in range(chips)])  18.2 us
    pallas_call x1, Pallas kernels, add_far(): pl.pallas_call(functools.partial(far_kernel, counts, steps, chips), out_s...  6.37 us
    pallas_call x2, Pallas kernels, pack(): pl.pallas_call(functools.partial(pack_kernel, slots, parts), out_shape=(j...  6.23 us
    all_to_all x1, starting transfers between devices, local(): came = [scatter(outgoing)]  5.12 us
    ppermute x3, starting transfers between devices, local(): lax.ppermute(piece, line, [(q, q ^ off) for q in range(chips)])  4.47 us
    ppermute x4, starting transfers between devices, swap(): return [lax.ppermute(one, axis, [(0, 1), (1, 0)]) for one in arrays]  4.45 us
    all_to_all x1, starting transfers between devices, local(): arrived = [scatter(outgoing)]  4.16 us
  transfers between devices with their start and end apart: 9, of which 5 were waited for; matrix products, arithmetic and copies ran while one was open for 1% of the time, Pallas kernels for 43%

profile of v5, /device:TPU:0, one launch (start us, length us, event | category | flops | bytes accessed | tf_op | source)
XLA Modules:
  0.0 87.6 jit_solution(18294245498238542663)
XLA Ops:
  0.0 0.7 pad_add_fusion.facts_ref
  0.7 0.0 copy-start.6
  0.7 4.1 %collective-permute-start.1 = (s32[6,32]{1,0:T(8,128)S(1)}, s32[6,32]{1,0:T(8,128)S(1)}, u32[]{:S(2)}, u32[]{:S(2)}) collective-permute-start(s32[6,32]{1,0:T(8,128)S(1)} %pad_add_fusion.facts_ref), channel_id=1, source_target_pairs={{0,4},{4,0},{1,5},{5,1},{2,6},{6,2},{3,7},{7,3},{8,12},{12,8},{9,1... | collective-permute-start | bytes 2312 | tf_op jit(solution)/shard_map/ppermute | solution.py:566
  4.8 0.1 collective-permute-start
  4.9 0.6 stack.27.place_ref
  5.5 0.0 copy-done.6
  5.5 3.7 %pack.2 = (bf16[16,272,128]{2,1,0:T(8,128)(2,1)}, bf16[8,128,128]{2,1,0:T(8,128)(2,1)}) custom-call(s32[7]{0:T(128)} %stack.27.place_ref, s32[6,32]{1,0:T(8,128)} %copy-done.6, bf16[8,128,128]{2,1,0:T(8,128)(2,1)} %p_in.1), custom_call_target="tpu_custom_call" | custom-call | tf_op jit(solution)/shard_map/pack/pallas_call | solution.py:83
  9.2 5.1 %all-to-all-start = ((bf16[16,272,128]{2,1,0:T(8,128)(2,1)}), bf16[16,272,128]{2,1,0:T(8,128)(2,1)S(1)}, u32[]{:S(2)}, u32[]{:S(2)}) async-start(bf16[16,272,128]{2,1,0:T(8,128)(2,1)} %get-tuple-element.52), calls=%async_computation | async-start | bytes 2228224 | tf_op jit(solution)/shard_map/all_to_all | solution.py:592
  14.3 0.0 copy-start.1
  14.3 15.7 %near.2 = (f32[8,896,128]{2,1,0:T(8,128)}, bf16[64,128,128]{2,1,0:T(8,128)(2,1)}, s32[65]{0:T(128)}, s32[32,256]{1,0:T(8,128)}) custom-call(s32[7]{0:T(128)} %stack.27.place_ref, s32[8,22]{1,0:T(8,128)} %acols_ref.3, s32[4,8]{1,0:T(4,128)} %bitcast.11, s32[32,27]{1,0:T(8,128)} %ccols_ref.3, s32[32,27]{1,0:T(8,128)} %ccols_ref.3, ...), custom_call_target="tpu_custom_call" | custom-call | flops 99999997952 | bytes 100000000 | tf_op jit(solution)/shard_map/near/pallas_call | solution.py:375
  30.0 0.0 collective-permute-done.1.facts_ref
  30.0 0.0 collective-permute-done.p_in
  30.1 0.0 copy-done.1
  30.1 2.5 %pack.3 = bf16[16,272,128]{2,1,0:T(8,128)(2,1)} custom-call(s32[7]{0:T(128)S(1)} %copy-done.1, s32[6,32]{1,0:T(8,128)S(1)} %collective-permute-done.1.facts_ref, bf16[8,128,128]{2,1,0:T(8,128)(2,1)S(1)} %collective-permute-done.p_in), custom_call_target="tpu_custom_call" | custom-call | tf_op jit(solution)/shard_map/pack/pallas_call | solution.py:83
  32.6 1.0 %all-to-all-done.refs_6_ = bf16[16,272,128]{2,1,0:T(8,128)(2,1)S(1)} async-done(((bf16[16,272,128]{2,1,0:T(8,128)(2,1)}), bf16[16,272,128]{2,1,0:T(8,128)(2,1)S(1)}, u32[]{:S(2)}, u32[]{:S(2)}) %all-to-all-start) | async-done | bytes 1114144 | tf_op jit(solution)/shard_map/all_to_all | solution.py:592
  33.6 0.0 copy-start.5
  33.6 4.2 %all-to-all-start.1 = ((bf16[16,272,128]{2,1,0:T(8,128)(2,1)}), bf16[16,272,128]{2,1,0:T(8,128)(2,1)S(1)}, u32[]{:S(2)}, u32[]{:S(2)}) async-start(bf16[16,272,128]{2,1,0:T(8,128)(2,1)} %pack.3), calls=%async_computation.1 | async-start | bytes 2228224 | tf_op jit(solution)/shard_map/all_to_all | solution.py:598
  37.7 0.0 copy-done.5
  37.8 0.0 copy-start
  37.8 0.0 copy-start.2
  37.8 0.0 copy-start.3
  37.8 16.1 %near.3 = (f32[8,896,128]{2,1,0:T(8,128)}, bf16[64,128,128]{2,1,0:T(8,128)(2,1)}, s32[65]{0:T(128)}) custom-call(s32[7]{0:T(128)} %stack.27.place_ref, s32[8,22]{1,0:T(8,128)} %acols_ref.3, s32[4,8]{1,0:T(4,128)} %bitcast.12, s32[32,27]{1,0:T(8,128)} %ccols_ref.3, s32[65]{0:T(128)} %get-tuple-element.48.refs_0_, ...), custom_call_target="tpu_custom_call" | custom-call | flops 99999997952 | bytes 100000000 | tf_op jit(solution)/shard_map/near/pallas_call | solution.py:375
  53.9 0.8 all-to-all-done.1.refs_0_
  54.6 0.0 copy-done
  54.6 0.0 copy-done.2
  54.7 0.0 copy-done.3
  54.7 0.0 copy-start.4
  54.7 0.6 copy-done.4
  55.3 6.4 %add_far.1 = (bf16[2,864,128]{2,1,0:T(8,128)(2,1)S(1)}, f32[2,864,128]{2,1,0:T(8,128)S(1)}, bf16[2,864,128]{2,1,0:T(8,128)(2,1)S(1)}, f32[2,864,128]{2,1,0:T(8,128)S(1)}) custom-call(s32[7]{0:T(128)S(1)} %copy-done.2, s32[65]{0:T(128)S(1)} %copy-done.4, s32[4,8]{1,0:T(4,128)S(1)} %bitcast.13, s32[32,256]{1,0:T(8,128)S(1)} %copy-done, ...), custom_call_target="tpu_custom_call" | custom-call | tf_op jit(solution)/shard_map/add_far/pallas_call | solution.py:513
  61.7 0.1 collective-permute-start.2
  61.7 1.8 %collective-permute-done.2.got_ref = bf16[2,864,128]{2,1,0:T(8,128)(2,1)S(1)} collective-permute-done((bf16[2,864,128]{2,1,0:T(8,128)(2,1)S(1)}, bf16[2,864,128]{2,1,0:T(8,128)(2,1)S(1)}, u32[]{:S(2)}, u32[]{:S(2)}) %collective-permute-start.2) | collective-permute-done | bytes 442400 | tf_op jit(solution)/shard_map/ppermute | solution.py:566
  63.5 0.1 pair.2
  63.6 0.2 collective-permute-start.3
  63.8 3.2 %collective-permute-start.4 = (bf16[864,128]{1,0:T(8,128)(2,1)S(1)}, bf16[864,128]{1,0:T(8,128)(2,1)S(1)}, u32[]{:S(2)}, u32[]{:S(2)}) collective-permute-start(bf16[864,128]{1,0:T(8,128)(2,1)S(1)} %get-tuple-element.66), channel_id=1, source_target_pairs={{0,6},{2,4},{4,2},{6,0},{1,7},{3,5},{5,3},{7,1},{8,14},{10,12},{12... | collective-permute-start | bytes 663560 | tf_op jit(solution)/shard_map/ppermute | solution.py:617
  67.0 0.0 collective-permute-start.5
  67.0 0.0 collective-permute-done.3.got_ref
  67.0 0.1 pair.3
  67.1 1.2 %collective-permute-start.6 = (bf16[864,128]{1,0:T(8,128)(2,1)S(1)}, bf16[864,128]{1,0:T(8,128)(2,1)S(1)}, u32[]{:S(2)}, u32[]{:S(2)}) collective-permute-start(bf16[864,128]{1,0:T(8,128)(2,1)S(1)} %get-tuple-element.68), channel_id=1, source_target_pairs={{0,2},{2,0},{4,6},{6,4},{1,3},{3,1},{5,7},{7,5},{8,10},{10,8},{12,... | collective-permute-start | bytes 663560 | tf_op jit(solution)/shard_map/ppermute | solution.py:617
  68.4 5.7 %collective-permute-done.4.refs_0_ = bf16[864,128]{1,0:T(8,128)(2,1)S(1)} collective-permute-done((bf16[864,128]{1,0:T(8,128)(2,1)S(1)}, bf16[864,128]{1,0:T(8,128)(2,1)S(1)}, u32[]{:S(2)}, u32[]{:S(2)}) %collective-permute-start.4) | collective-permute-done | bytes 221216 | tf_op jit(solution)/shard_map/ppermute | solution.py:617
  74.0 12.6 %collective-permute-done.5.refs_1_ = bf16[864,128]{1,0:T(8,128)(2,1)S(1)} collective-permute-done((bf16[864,128]{1,0:T(8,128)(2,1)S(1)}, bf16[864,128]{1,0:T(8,128)(2,1)S(1)}, u32[]{:S(2)}, u32[]{:S(2)}) %collective-permute-start.5) | collective-permute-done | bytes 221216 | tf_op jit(solution)/shard_map/ppermute | solution.py:617
  86.6 0.0 collective-permute-done.6.refs_2_
  86.6 1.0 %last.1 = f32[4,32,864]{2,1,0:T(8,128)} custom-call(f32[864,128]{1,0:T(8,128)S(1)} %get-tuple-element.65.mine_ref, bf16[864,128]{1,0:T(8,128)(2,1)S(1)} %collective-permute-done.4.refs_0_, bf16[864,128]{1,0:T(8,128)(2,1)S(1)} %collective-permute-done.5.refs_1_, bf16[864,128]{1,0:T(8,128)(2,1)S(1)} %collective-permute-done.6.refs_2_), custom_call_target="tpu_custom_call" | custom-call | tf_op jit(solution)/shard_map/last/pallas_call | solution.py:555
Async XLA Ops:
  0.7 4.8 %copy-start.6 = (s32[6,32]{1,0:T(8,128)}, s32[6,32]{1,0:T(8,128)S(1)}, u32[]{:S(2)}) copy-start(s32[6,32]{1,0:T(8,128)S(1)} %pad_add_fusion.facts_ref) | copy-start | bytes 2308
  0.7 29.3 %collective-permute-start.1 = (s32[6,32]{1,0:T(8,128)S(1)}, s32[6,32]{1,0:T(8,128)S(1)}, u32[]{:S(2)}, u32[]{:S(2)}) collective-permute-start(s32[6,32]{1,0:T(8,128)S(1)} %pad_add_fusion.facts_ref), channel_id=1, source_target_pairs={{0,4},{4,0},{1,5},{5,1},{2,6},{6,2},{3,7},{7,3},{8,12},{12,8},{9,1... | collective-permute-start | bytes 2312 | tf_op jit(solution)/shard_map/ppermute | solution.py:566
  4.8 25.2 %collective-permute-start = (bf16[8,128,128]{2,1,0:T(8,128)(2,1)}, bf16[8,128,128]{2,1,0:T(8,128)(2,1)S(1)}, u32[]{:S(2)}, u32[]{:S(2)}) collective-permute-start(bf16[8,128,128]{2,1,0:T(8,128)(2,1)} %p_in.1), channel_id=1, source_target_pairs={{0,4},{4,0},{1,5},{5,1},{2,6},{6,2},{3,7},{7,3},{8,12},{12,8},{9,1... | collective-permute-start | bytes 786440 | tf_op jit(solution)/shard_map/ppermute | solution.py:566
  9.2 24.4 %all-to-all-start = ((bf16[16,272,128]{2,1,0:T(8,128)(2,1)}), bf16[16,272,128]{2,1,0:T(8,128)(2,1)S(1)}, u32[]{:S(2)}, u32[]{:S(2)}) async-start(bf16[16,272,128]{2,1,0:T(8,128)(2,1)} %get-tuple-element.52), calls=%async_computation | async-start | bytes 2228224 | tf_op jit(solution)/shard_map/all_to_all | solution.py:592
  14.3 15.7 %copy-start.1 = (s32[7]{0:T(128)S(1)}, s32[7]{0:T(128)}, u32[]{:S(2)}) copy-start(s32[7]{0:T(128)} %stack.27.place_ref) | copy-start | bytes 88
  33.6 4.2 %copy-start.5 = (bf16[16,272,128]{2,1,0:T(8,128)(2,1)}, bf16[16,272,128]{2,1,0:T(8,128)(2,1)S(1)}, u32[]{:S(2)}) copy-start(bf16[16,272,128]{2,1,0:T(8,128)(2,1)S(1)} %all-to-all-done.refs_6_) | copy-start | bytes 3342340
  33.6 21.1 %all-to-all-start.1 = ((bf16[16,272,128]{2,1,0:T(8,128)(2,1)}), bf16[16,272,128]{2,1,0:T(8,128)(2,1)S(1)}, u32[]{:S(2)}, u32[]{:S(2)}) async-start(bf16[16,272,128]{2,1,0:T(8,128)(2,1)} %pack.3), calls=%async_computation.1 | async-start | bytes 2228224 | tf_op jit(solution)/shard_map/all_to_all | solution.py:598
  37.8 16.9 %copy-start = (s32[32,256]{1,0:T(8,128)S(1)}, s32[32,256]{1,0:T(8,128)}, u32[]{:S(2)}) copy-start(s32[32,256]{1,0:T(8,128)} %get-tuple-element.49.refs_1_.slot_of_in) | copy-start | bytes 98308
  37.8 16.9 %copy-start.2 = (s32[7]{0:T(128)S(1)}, s32[7]{0:T(128)}, u32[]{:S(2)}) copy-start(s32[7]{0:T(128)} %stack.27.place_ref) | copy-start | bytes 88
  37.8 16.9 %copy-start.3 = (s32[8,4]{0,1:T(4,128)S(1)}, s32[8,4]{0,1:T(4,128)}, u32[]{:S(2)}) copy-start(s32[8,4]{0,1:T(4,128)} %param.9) | copy-start | bytes 388
  54.7 0.6 copy-start.4
  61.7 1.9 %collective-permute-start.2 = (bf16[2,864,128]{2,1,0:T(8,128)(2,1)S(1)}, bf16[2,864,128]{2,1,0:T(8,128)(2,1)S(1)}, u32[]{:S(2)}, u32[]{:S(2)}) collective-permute-start(bf16[2,864,128]{2,1,0:T(8,128)(2,1)S(1)} %get-tuple-element.60), channel_id=1, source_target_pairs={{0,1},{1,0},{2,3},{3,2},{4,5},{5,4},{6,7},{7,6},{8,9},{9,8},{10,11... | collective-permute-start | bytes 1327112 | tf_op jit(solution)/shard_map/ppermute | solution.py:566
  63.6 3.4 %collective-permute-start.3 = (bf16[2,864,128]{2,1,0:T(8,128)(2,1)S(1)}, bf16[2,864,128]{2,1,0:T(8,128)(2,1)S(1)}, u32[]{:S(2)}, u32[]{:S(2)}) collective-permute-start(bf16[2,864,128]{2,1,0:T(8,128)(2,1)S(1)} %get-tuple-element.64), channel_id=1, source_target_pairs={{0,1},{1,0},{2,3},{3,2},{4,5},{5,4},{6,7},{7,6},{8,9},{9,8},{10,11... | collective-permute-start | bytes 1327112 | tf_op jit(solution)/shard_map/ppermute | solution.py:566
  63.8 10.2 %collective-permute-start.4 = (bf16[864,128]{1,0:T(8,128)(2,1)S(1)}, bf16[864,128]{1,0:T(8,128)(2,1)S(1)}, u32[]{:S(2)}, u32[]{:S(2)}) collective-permute-start(bf16[864,128]{1,0:T(8,128)(2,1)S(1)} %get-tuple-element.66), channel_id=1, source_target_pairs={{0,6},{2,4},{4,2},{6,0},{1,7},{3,5},{5,3},{7,1},{8,14},{10,12},{12... | collective-permute-start | bytes 663560 | tf_op jit(solution)/shard_map/ppermute | solution.py:617
  67.0 19.6 %collective-permute-start.5 = (bf16[864,128]{1,0:T(8,128)(2,1)S(1)}, bf16[864,128]{1,0:T(8,128)(2,1)S(1)}, u32[]{:S(2)}, u32[]{:S(2)}) collective-permute-start(bf16[864,128]{1,0:T(8,128)(2,1)S(1)} %get-tuple-element.67), channel_id=1, source_target_pairs={{0,4},{2,6},{4,0},{6,2},{1,5},{3,7},{5,1},{7,3},{8,12},{10,14},{12... | collective-permute-start | bytes 663560 | tf_op jit(solution)/shard_map/ppermute | solution.py:617
  67.1 19.5 %collective-permute-start.6 = (bf16[864,128]{1,0:T(8,128)(2,1)S(1)}, bf16[864,128]{1,0:T(8,128)(2,1)S(1)}, u32[]{:S(2)}, u32[]{:S(2)}) collective-permute-start(bf16[864,128]{1,0:T(8,128)(2,1)S(1)} %get-tuple-element.68), channel_id=1, source_target_pairs={{0,2},{2,0},{4,6},{6,4},{1,3},{3,1},{5,7},{7,5},{8,10},{10,8},{12,... | collective-permute-start | bytes 663560 | tf_op jit(solution)/shard_map/ppermute | solution.py:617

commit v6 on v5

--- a/solution.py
+++ b/solution.py
@@ -510,6 +510,8 @@
                 scratch_shapes=scratch_shapes,
             )
         )
+    if steps == 1:
+        where = pltpu.with_memory_space_constraint(where, pltpu.HBM)
     return pl.pallas_call(
         functools.partial(far_kernel, counts, steps, chips),
         out_shape=tuple(jax.ShapeDtypeStruct(*one) for one in outs),

time: 88.2 us -> 87.7 us (level)
  transfers between devices with their start and end apart: 9 -> 9, of which waited for: 5 -> 5; matrix products, arithmetic and copies ran while one was open for 1% -> 1% of each run, Pallas kernels for 43% -> 44%
where the time goes in v6:
time: 87.7 us; the launch traced here: 87 us
  Pallas kernels  45.5 us (52%)
  waiting for transfers between devices  21.7 us (25%)
  starting transfers between devices  18.2 us (21%)
    pallas_call x2, Pallas kernels, near(): pl.pallas_call(functools.partial(near_kernel, first_row, len(came)), out_...  31.8 us
    ppermute x3, waiting for transfers between devices, local(): lax.ppermute(piece, line, [(q, q ^ off) for q in range(chips)])  18.2 us
    pallas_call x1, Pallas kernels, add_far(): pl.pallas_call(functools.partial(far_kernel, counts, steps, chips), out_s...  6.38 us
    pallas_call x2, Pallas kernels, pack(): pl.pallas_call(functools.partial(pack_kernel, slots, parts), out_shape=(j...  6.27 us
    all_to_all x1, starting transfers between devices, local(): came = [scatter(outgoing)]  5.11 us
    ppermute x3, starting transfers between devices, local(): lax.ppermute(piece, line, [(q, q ^ off) for q in range(chips)])  4.47 us
    ppermute x4, starting transfers between devices, swap(): return [lax.ppermute(one, axis, [(0, 1), (1, 0)]) for one in arrays]  4.45 us
    all_to_all x1, starting transfers between devices, local(): arrived = [scatter(outgoing)]  4.19 us
  transfers between devices with their start and end apart: 9, of which 5 were waited for; matrix products, arithmetic and copies ran while one was open for 1% of the time, Pallas kernels for 44%

profile of v6, /device:TPU:0, one launch (start us, length us, event | category | flops | bytes accessed | tf_op | source)
XLA Modules:
  0.0 87.0 jit_solution(18321684123381098309)
XLA Ops:
  0.0 0.7 pad_add_fusion.facts_ref
  0.7 0.0 copy-start.5
  0.7 4.1 %collective-permute-start.1 = (s32[6,32]{1,0:T(8,128)S(1)}, s32[6,32]{1,0:T(8,128)S(1)}, u32[]{:S(2)}, u32[]{:S(2)}) collective-permute-start(s32[6,32]{1,0:T(8,128)S(1)} %pad_add_fusion.facts_ref), channel_id=1, source_target_pairs={{0,4},{4,0},{1,5},{5,1},{2,6},{6,2},{3,7},{7,3},{8,12},{12,8},{9,1... | collective-permute-start | bytes 2312 | tf_op jit(solution)/shard_map/ppermute | solution.py:568
  4.8 0.1 collective-permute-start
  4.9 0.7 stack.27.place_ref
  5.6 0.0 copy-done.5
  5.6 3.7 %pack.2 = (bf16[16,272,128]{2,1,0:T(8,128)(2,1)}, bf16[8,128,128]{2,1,0:T(8,128)(2,1)}) custom-call(s32[7]{0:T(128)} %stack.27.place_ref, s32[6,32]{1,0:T(8,128)} %copy-done.5, bf16[8,128,128]{2,1,0:T(8,128)(2,1)} %p_in.1), custom_call_target="tpu_custom_call" | custom-call | tf_op jit(solution)/shard_map/pack/pallas_call | solution.py:83
  9.3 5.1 %all-to-all-start = ((bf16[16,272,128]{2,1,0:T(8,128)(2,1)}), bf16[16,272,128]{2,1,0:T(8,128)(2,1)S(1)}, u32[]{:S(2)}, u32[]{:S(2)}) async-start(bf16[16,272,128]{2,1,0:T(8,128)(2,1)} %get-tuple-element.52), calls=%async_computation | async-start | bytes 2228224 | tf_op jit(solution)/shard_map/all_to_all | solution.py:594
  14.4 0.0 copy-start.1
  14.4 15.7 %near.2 = (f32[8,896,128]{2,1,0:T(8,128)}, bf16[64,128,128]{2,1,0:T(8,128)(2,1)}, s32[65]{0:T(128)}, s32[32,256]{1,0:T(8,128)}) custom-call(s32[7]{0:T(128)} %stack.27.place_ref, s32[8,22]{1,0:T(8,128)} %acols_ref.3, s32[4,8]{1,0:T(4,128)} %bitcast.11, s32[32,27]{1,0:T(8,128)} %ccols_ref.3, s32[32,27]{1,0:T(8,128)} %ccols_ref.3, ...), custom_call_target="tpu_custom_call" | custom-call | flops 99999997952 | bytes 100000000 | tf_op jit(solution)/shard_map/near/pallas_call | solution.py:375
  30.1 0.0 collective-permute-done.1.facts_ref
  30.1 0.0 collective-permute-done.p_in
  30.1 0.0 copy-done.1
  30.1 2.5 %pack.3 = bf16[16,272,128]{2,1,0:T(8,128)(2,1)} custom-call(s32[7]{0:T(128)S(1)} %copy-done.1, s32[6,32]{1,0:T(8,128)S(1)} %collective-permute-done.1.facts_ref, bf16[8,128,128]{2,1,0:T(8,128)(2,1)S(1)} %collective-permute-done.p_in), custom_call_target="tpu_custom_call" | custom-call | tf_op jit(solution)/shard_map/pack/pallas_call | solution.py:83
  32.7 1.0 %all-to-all-done.refs_6_ = bf16[16,272,128]{2,1,0:T(8,128)(2,1)S(1)} async-done(((bf16[16,272,128]{2,1,0:T(8,128)(2,1)}), bf16[16,272,128]{2,1,0:T(8,128)(2,1)S(1)}, u32[]{:S(2)}, u32[]{:S(2)}) %all-to-all-start) | async-done | bytes 1114144 | tf_op jit(solution)/shard_map/all_to_all | solution.py:594
  33.6 0.0 copy-start.4
  33.6 4.2 %all-to-all-start.1 = ((bf16[16,272,128]{2,1,0:T(8,128)(2,1)}), bf16[16,272,128]{2,1,0:T(8,128)(2,1)S(1)}, u32[]{:S(2)}, u32[]{:S(2)}) async-start(bf16[16,272,128]{2,1,0:T(8,128)(2,1)} %pack.3), calls=%async_computation.1 | async-start | bytes 2228224 | tf_op jit(solution)/shard_map/all_to_all | solution.py:600
  37.8 0.0 copy-done.4
  37.8 0.0 copy-start
  37.9 0.0 copy-start.2
  37.9 0.0 copy-start.3
  37.9 16.1 %near.3 = (f32[8,896,128]{2,1,0:T(8,128)}, bf16[64,128,128]{2,1,0:T(8,128)(2,1)}, s32[65]{0:T(128)}) custom-call(s32[7]{0:T(128)} %stack.27.place_ref, s32[8,22]{1,0:T(8,128)} %acols_ref.3, s32[4,8]{1,0:T(4,128)} %bitcast.12, s32[32,27]{1,0:T(8,128)} %ccols_ref.3, s32[65]{0:T(128)} %get-tuple-element.48.refs_0_, ...), custom_call_target="tpu_custom_call" | custom-call | flops 99999997952 | bytes 100000000 | tf_op jit(solution)/shard_map/near/pallas_call | solution.py:375
  54.0 0.8 all-to-all-done.1.refs_0_
  54.7 0.0 copy-done
  54.7 0.0 copy-done.2
  54.7 0.0 copy-done.3
  54.8 6.4 %add_far.1 = (bf16[2,864,128]{2,1,0:T(8,128)(2,1)S(1)}, f32[2,864,128]{2,1,0:T(8,128)S(1)}, bf16[2,864,128]{2,1,0:T(8,128)(2,1)S(1)}, f32[2,864,128]{2,1,0:T(8,128)S(1)}) custom-call(s32[7]{0:T(128)S(1)} %copy-done.2, s32[65]{0:T(128)} %get-tuple-element.53.where_in, s32[4,8]{1,0:T(4,128)S(1)} %bitcast.13, s32[32,256]{1,0:T(8,128)S(1)} %copy-done, ...), custom_call_target="tpu_custom_call" | custom-call | tf_op jit(solution)/shard_map/add_far/pallas_call | solution.py:515
  61.1 0.1 collective-permute-start.2
  61.2 1.8 %collective-permute-done.2.got_ref = bf16[2,864,128]{2,1,0:T(8,128)(2,1)S(1)} collective-permute-done((bf16[2,864,128]{2,1,0:T(8,128)(2,1)S(1)}, bf16[2,864,128]{2,1,0:T(8,128)(2,1)S(1)}, u32[]{:S(2)}, u32[]{:S(2)}) %collective-permute-start.2) | collective-permute-done | bytes 442400 | tf_op jit(solution)/shard_map/ppermute | solution.py:568
  63.0 0.1 pair.2
  63.1 0.2 collective-permute-start.3
  63.3 3.2 %collective-permute-start.4 = (bf16[864,128]{1,0:T(8,128)(2,1)S(1)}, bf16[864,128]{1,0:T(8,128)(2,1)S(1)}, u32[]{:S(2)}, u32[]{:S(2)}) collective-permute-start(bf16[864,128]{1,0:T(8,128)(2,1)S(1)} %get-tuple-element.66), channel_id=1, source_target_pairs={{0,6},{2,4},{4,2},{6,0},{1,7},{3,5},{5,3},{7,1},{8,14},{10,12},{12... | collective-permute-start | bytes 663560 | tf_op jit(solution)/shard_map/ppermute | solution.py:619
  66.5 0.0 collective-permute-start.5
  66.5 0.0 collective-permute-done.3.got_ref
  66.5 0.1 pair.3
  66.6 1.3 %collective-permute-start.6 = (bf16[864,128]{1,0:T(8,128)(2,1)S(1)}, bf16[864,128]{1,0:T(8,128)(2,1)S(1)}, u32[]{:S(2)}, u32[]{:S(2)}) collective-permute-start(bf16[864,128]{1,0:T(8,128)(2,1)S(1)} %get-tuple-element.68), channel_id=1, source_target_pairs={{0,2},{2,0},{4,6},{6,4},{1,3},{3,1},{5,7},{7,5},{8,10},{10,8},{12,... | collective-permute-start | bytes 663560 | tf_op jit(solution)/shard_map/ppermute | solution.py:619
  67.8 5.7 %collective-permute-done.4.refs_0_ = bf16[864,128]{1,0:T(8,128)(2,1)S(1)} collective-permute-done((bf16[864,128]{1,0:T(8,128)(2,1)S(1)}, bf16[864,128]{1,0:T(8,128)(2,1)S(1)}, u32[]{:S(2)}, u32[]{:S(2)}) %collective-permute-start.4) | collective-permute-done | bytes 221216 | tf_op jit(solution)/shard_map/ppermute | solution.py:619
  73.5 12.6 %collective-permute-done.5.refs_1_ = bf16[864,128]{1,0:T(8,128)(2,1)S(1)} collective-permute-done((bf16[864,128]{1,0:T(8,128)(2,1)S(1)}, bf16[864,128]{1,0:T(8,128)(2,1)S(1)}, u32[]{:S(2)}, u32[]{:S(2)}) %collective-permute-start.5) | collective-permute-done | bytes 221216 | tf_op jit(solution)/shard_map/ppermute | solution.py:619
  86.0 0.0 collective-permute-done.6.refs_2_
  86.0 1.0 %last.1 = f32[4,32,864]{2,1,0:T(8,128)} custom-call(f32[864,128]{1,0:T(8,128)S(1)} %get-tuple-element.65.mine_ref, bf16[864,128]{1,0:T(8,128)(2,1)S(1)} %collective-permute-done.4.refs_0_, bf16[864,128]{1,0:T(8,128)(2,1)S(1)} %collective-permute-done.5.refs_1_, bf16[864,128]{1,0:T(8,128)(2,1)S(1)} %collective-permute-done.6.refs_2_), custom_call_target="tpu_custom_call" | custom-call | tf_op jit(solution)/shard_map/last/pallas_call | solution.py:557
Async XLA Ops:
  0.7 4.8 %copy-start.5 = (s32[6,32]{1,0:T(8,128)}, s32[6,32]{1,0:T(8,128)S(1)}, u32[]{:S(2)}) copy-start(s32[6,32]{1,0:T(8,128)S(1)} %pad_add_fusion.facts_ref) | copy-start | bytes 2308
  0.7 29.4 %collective-permute-start.1 = (s32[6,32]{1,0:T(8,128)S(1)}, s32[6,32]{1,0:T(8,128)S(1)}, u32[]{:S(2)}, u32[]{:S(2)}) collective-permute-start(s32[6,32]{1,0:T(8,128)S(1)} %pad_add_fusion.facts_ref), channel_id=1, source_target_pairs={{0,4},{4,0},{1,5},{5,1},{2,6},{6,2},{3,7},{7,3},{8,12},{12,8},{9,1... | collective-permute-start | bytes 2312 | tf_op jit(solution)/shard_map/ppermute | solution.py:568
  4.8 25.3 %collective-permute-start = (bf16[8,128,128]{2,1,0:T(8,128)(2,1)}, bf16[8,128,128]{2,1,0:T(8,128)(2,1)S(1)}, u32[]{:S(2)}, u32[]{:S(2)}) collective-permute-start(bf16[8,128,128]{2,1,0:T(8,128)(2,1)} %p_in.1), channel_id=1, source_target_pairs={{0,4},{4,0},{1,5},{5,1},{2,6},{6,2},{3,7},{7,3},{8,12},{12,8},{9,1... | collective-permute-start | bytes 786440 | tf_op jit(solution)/shard_map/ppermute | solution.py:568
  9.3 24.3 %all-to-all-start = ((bf16[16,272,128]{2,1,0:T(8,128)(2,1)}), bf16[16,272,128]{2,1,0:T(8,128)(2,1)S(1)}, u32[]{:S(2)}, u32[]{:S(2)}) async-start(bf16[16,272,128]{2,1,0:T(8,128)(2,1)} %get-tuple-element.52), calls=%async_computation | async-start | bytes 2228224 | tf_op jit(solution)/shard_map/all_to_all | solution.py:594
  14.4 15.7 %copy-start.1 = (s32[7]{0:T(128)S(1)}, s32[7]{0:T(128)}, u32[]{:S(2)}) copy-start(s32[7]{0:T(128)} %stack.27.place_ref) | copy-start | bytes 88
  33.6 4.2 %copy-start.4 = (bf16[16,272,128]{2,1,0:T(8,128)(2,1)}, bf16[16,272,128]{2,1,0:T(8,128)(2,1)S(1)}, u32[]{:S(2)}) copy-start(bf16[16,272,128]{2,1,0:T(8,128)(2,1)S(1)} %all-to-all-done.refs_6_) | copy-start | bytes 3342340
  33.6 21.1 %all-to-all-start.1 = ((bf16[16,272,128]{2,1,0:T(8,128)(2,1)}), bf16[16,272,128]{2,1,0:T(8,128)(2,1)S(1)}, u32[]{:S(2)}, u32[]{:S(2)}) async-start(bf16[16,272,128]{2,1,0:T(8,128)(2,1)} %pack.3), calls=%async_computation.1 | async-start | bytes 2228224 | tf_op jit(solution)/shard_map/all_to_all | solution.py:600
  37.8 16.9 %copy-start = (s32[32,256]{1,0:T(8,128)S(1)}, s32[32,256]{1,0:T(8,128)}, u32[]{:S(2)}) copy-start(s32[32,256]{1,0:T(8,128)} %get-tuple-element.49.refs_1_.slot_of_in) | copy-start | bytes 98308
  37.9 16.9 %copy-start.2 = (s32[7]{0:T(128)S(1)}, s32[7]{0:T(128)}, u32[]{:S(2)}) copy-start(s32[7]{0:T(128)} %stack.27.place_ref) | copy-start | bytes 88
  37.9 16.9 %copy-start.3 = (s32[8,4]{0,1:T(4,128)S(1)}, s32[8,4]{0,1:T(4,128)}, u32[]{:S(2)}) copy-start(s32[8,4]{0,1:T(4,128)} %param.9) | copy-start | bytes 388
  61.1 1.9 %collective-permute-start.2 = (bf16[2,864,128]{2,1,0:T(8,128)(2,1)S(1)}, bf16[2,864,128]{2,1,0:T(8,128)(2,1)S(1)}, u32[]{:S(2)}, u32[]{:S(2)}) collective-permute-start(bf16[2,864,128]{2,1,0:T(8,128)(2,1)S(1)} %get-tuple-element.60), channel_id=1, source_target_pairs={{0,1},{1,0},{2,3},{3,2},{4,5},{5,4},{6,7},{7,6},{8,9},{9,8},{10,11... | collective-permute-start | bytes 1327112 | tf_op jit(solution)/shard_map/ppermute | solution.py:568
  63.1 3.4 %collective-permute-start.3 = (bf16[2,864,128]{2,1,0:T(8,128)(2,1)S(1)}, bf16[2,864,128]{2,1,0:T(8,128)(2,1)S(1)}, u32[]{:S(2)}, u32[]{:S(2)}) collective-permute-start(bf16[2,864,128]{2,1,0:T(8,128)(2,1)S(1)} %get-tuple-element.64), channel_id=1, source_target_pairs={{0,1},{1,0},{2,3},{3,2},{4,5},{5,4},{6,7},{7,6},{8,9},{9,8},{10,11... | collective-permute-start | bytes 1327112 | tf_op jit(solution)/shard_map/ppermute | solution.py:568
  63.3 10.2 %collective-permute-start.4 = (bf16[864,128]{1,0:T(8,128)(2,1)S(1)}, bf16[864,128]{1,0:T(8,128)(2,1)S(1)}, u32[]{:S(2)}, u32[]{:S(2)}) collective-permute-start(bf16[864,128]{1,0:T(8,128)(2,1)S(1)} %get-tuple-element.66), channel_id=1, source_target_pairs={{0,6},{2,4},{4,2},{6,0},{1,7},{3,5},{5,3},{7,1},{8,14},{10,12},{12... | collective-permute-start | bytes 663560 | tf_op jit(solution)/shard_map/ppermute | solution.py:619
  66.5 19.5 %collective-permute-start.5 = (bf16[864,128]{1,0:T(8,128)(2,1)S(1)}, bf16[864,128]{1,0:T(8,128)(2,1)S(1)}, u32[]{:S(2)}, u32[]{:S(2)}) collective-permute-start(bf16[864,128]{1,0:T(8,128)(2,1)S(1)} %get-tuple-element.67), channel_id=1, source_target_pairs={{0,4},{2,6},{4,0},{6,2},{1,5},{3,7},{5,1},{7,3},{8,12},{10,14},{12... | collective-permute-start | bytes 663560 | tf_op jit(solution)/shard_map/ppermute | solution.py:619
  66.6 19.5 %collective-permute-start.6 = (bf16[864,128]{1,0:T(8,128)(2,1)S(1)}, bf16[864,128]{1,0:T(8,128)(2,1)S(1)}, u32[]{:S(2)}, u32[]{:S(2)}) collective-permute-start(bf16[864,128]{1,0:T(8,128)(2,1)S(1)} %get-tuple-element.68), channel_id=1, source_target_pairs={{0,2},{2,0},{4,6},{6,4},{1,3},{3,1},{5,7},{7,5},{8,10},{10,8},{12,... | collective-permute-start | bytes 663560 | tf_op jit(solution)/shard_map/ppermute | solution.py:619
